TPU v7x, 32 devices: a whole 2x2x4 slice. The times are simulated.
32 devices in a mesh: batch: 4 (over y, core), seq: 8 (over z, x).
Axes of the slice: x: 2, y: 2, z: 4, core: 2. Of those that a mesh axis runs over, the one named last changes fastest.
Arguments:
- hidden_in: bfloat16 [8, 1024, 2560], P('batch', 'seq'), may hold values from -40 to 40
- attn_gain: bfloat16 [2560], P(('batch', 'seq')), may hold values from 0.25 to 1.75
- query_weight: bfloat16 [2560, 2560], P(('batch', 'seq')), may hold values from -0.125 to 0.125
- key_weight: bfloat16 [2560, 640], P(('batch', 'seq')), may hold values from -0.125 to 0.125
- value_weight: bfloat16 [2560, 640], P(('batch', 'seq')), may hold values from -0.125 to 0.125
- out_weight: bfloat16 [2560, 2560], P(('batch', 'seq')), may hold values from -0.625 to 0.625
- mlp_gain: bfloat16 [2560], P(('batch', 'seq')), may hold values from 0.25 to 1.75
- gate_weight: bfloat16 [2560, 6912], P(('batch', 'seq')), may hold values from -0.125 to 0.125
- up_weight: bfloat16 [2560, 6912], P(('batch', 'seq')), may hold values from -0.125 to 0.125
- down_weight: bfloat16 [2560, 6912], P(('batch', 'seq')), may hold values from -0.078125 to 0.078125
- segment_ids: int32 [8, 1024], P('batch'), may hold values from 0 to 127, as said below
- grad_output: bfloat16 [8, 1024, 2560], P('batch', 'seq'), may hold values from -6 to 6
Outputs:
- output: bfloat16 [8, 1024, 2560], P('batch', 'seq')
- grad_input: float32 [8, 1024, 2560], P('batch', 'seq')
- grad_attn_gain: float32 [2560], P(('batch', 'seq'))
- grad_query: float32 [2560, 2560], P(('batch', 'seq'))
- grad_key: float32 [2560, 640], P(('batch', 'seq'))
- grad_value: float32 [2560, 640], P(('batch', 'seq'))
- grad_out: float32 [2560, 2560], P(('batch', 'seq'))
- grad_mlp_gain: float32 [2560], P(('batch', 'seq'))
- grad_gate: float32 [2560, 6912], P(('batch', 'seq'))
- grad_up: float32 [2560, 6912], P(('batch', 'seq'))
- grad_down: float32 [2560, 6912], P(('batch', 'seq'))
Inputs may be any that keep to these rules, and one draw needn't show every extreme that they name: `segment_ids`: in each sequence the ids start at 0, never fall, rise by at most one from a token to the next and rise only at positions that are multiples of 8; among the 2 sequences of each index of batch one is a single document; some sequence starts a new document at every multiple of 8.
All inputs are finite; a program needn't handle non-finite values.
Results may differ from a plain program's by a relative error of at most 0.013.
Values may be sent and summed in bfloat16 or wider, within the bound.
A program may use at most 896 MiB of HBM per device.

v0:
```python
import math

import jax
import jax.numpy as jnp
from jax import lax
from jax.sharding import PartitionSpec as P

HEADS = 32
KV_HEADS = 8
HEAD_DIM = 80


EPSILON = 1e-05
ROPE_BASE = 10000.0


def rotate(values, cosine, sine_table):
    half_dim = values.shape[-1] // 2
    first_half = values[..., :half_dim]
    second_half = values[..., half_dim:]
    return jnp.concatenate(
        [
            first_half * cosine - second_half * sine_table,
            second_half * cosine + first_half * sine_table,
        ],
        -1,
    )


def unrotate(values, cosine, sine_table):
    half_dim = values.shape[-1] // 2
    first_half = values[..., :half_dim]
    second_half = values[..., half_dim:]
    return jnp.concatenate(
        [
            first_half * cosine + second_half * sine_table,
            second_half * cosine - first_half * sine_table,
        ],
        -1,
    )


def fetch_attention(query_weight, key_weight, value_weight, out_weight, attn_gain):
    return (
        lax.all_gather(query_weight, ("batch", "seq"), axis=0, tiled=True),
        lax.all_gather(key_weight, ("batch", "seq"), axis=0, tiled=True),
        lax.all_gather(value_weight, ("batch", "seq"), axis=0, tiled=True),
        lax.all_gather(out_weight, ("batch", "seq"), axis=0, tiled=True),
        lax.all_gather(attn_gain, ("batch", "seq"), axis=0, tiled=True),
    )


def fetch_mlp(gate_weight, up_weight, down_weight, mlp_gain):
    return (
        lax.all_gather(gate_weight, ("batch", "seq"), axis=0, tiled=True),
        lax.all_gather(up_weight, ("batch", "seq"), axis=0, tiled=True),
        lax.all_gather(down_weight, ("batch", "seq"), axis=0, tiled=True),
        lax.all_gather(mlp_gain, ("batch", "seq"), axis=0, tiled=True),
    )


def by_columns(left, right):
    return lax.dot_general(
        left, right, (((1,), (1,)), ((), ())), preferred_element_type=jnp.float32
    )


def by_rows(left, right):
    return lax.dot_general(
        left, right, (((0,), (0,)), ((), ())), preferred_element_type=jnp.float32
    )


def shards(
    hidden_in,
    attn_gain,
    query_weight,
    key_weight,
    value_weight,
    out_weight,
    mlp_gain,
    gate_weight,
    up_weight,
    down_weight,
    segment_ids,
    grad_output,
):
    seq_b, local_len, width = hidden_in.shape
    seq_len = segment_ids.shape[1]
    token_rows = seq_b * local_len
    repeat = HEADS // KV_HEADS
    query_width = HEADS * HEAD_DIM
    key_width = KV_HEADS * HEAD_DIM
    scaling = 1.0 / math.sqrt(HEAD_DIM)
    offset = lax.axis_index("seq") * local_len
    positions = offset + jnp.arange(local_len, dtype=jnp.int32)
    key_place = jnp.arange(seq_len, dtype=jnp.int32)
    half_dim = HEAD_DIM // 2
    frequency = ROPE_BASE ** (-(jnp.arange(half_dim, dtype=jnp.float32) * 2.0 / HEAD_DIM))
    angles = positions.astype(jnp.float32)[:, None] * frequency[None, :]
    cosine = jnp.cos(angles)[:, None, :]
    sine_table = jnp.sin(angles)[:, None, :]
    query_segments = lax.dynamic_slice_in_dim(segment_ids, offset, local_len, 1)
    query_full, key_full, value_full, out_full, attn_gain_full = fetch_attention(
        query_weight, key_weight, value_weight, out_weight, attn_gain
    )
    gain_one = attn_gain_full.astype(jnp.float32)
    source = hidden_in.astype(jnp.float32).reshape(token_rows, width)
    inv_one = lax.rsqrt(jnp.mean(source * source, -1, keepdims=True) + EPSILON)
    normed_one = source * inv_one
    normed_low = (normed_one * gain_one).astype(jnp.bfloat16)
    queries = jnp.dot(normed_low, query_full, preferred_element_type=jnp.float32)
    key_rows = jnp.dot(normed_low, key_full, preferred_element_type=jnp.float32)
    value_rows = jnp.dot(normed_low, value_full, preferred_element_type=jnp.float32).astype(
        jnp.bfloat16
    )
    queries = rotate(queries.reshape(seq_b, local_len, HEADS, HEAD_DIM), cosine, sine_table).astype(
        jnp.bfloat16
    )
    key_rows = rotate(
        key_rows.reshape(seq_b, local_len, KV_HEADS, HEAD_DIM), cosine, sine_table
    ).astype(jnp.bfloat16)
    key_all, value_all = (
        lax.all_gather(key_rows.reshape(seq_b, local_len, key_width), "seq", axis=1, tiled=True),
        lax.all_gather(value_rows.reshape(seq_b, local_len, key_width), "seq", axis=1, tiled=True),
    )

    def scores_of(query_seq, key_heads, query_seg, key_seg):
        grouped = query_seq.reshape(local_len, KV_HEADS, repeat, HEAD_DIM)
        raw_scores = (
            jnp.einsum("igrd,jgd->grij", grouped, key_heads, preferred_element_type=jnp.float32)
            * scaling
        )
        allowed = (query_seg[:, None] == key_seg[None, :]) & (
            key_place[None, :] <= positions[:, None]
        )
        return jnp.where(allowed, raw_scores, -1e30)

    def attend(entries):
        query_seq, key_seq, value_seq, query_seg, key_seg = entries
        value_heads = value_seq.reshape(seq_len, KV_HEADS, HEAD_DIM)
        scores = scores_of(
            query_seq, key_seq.reshape(seq_len, KV_HEADS, HEAD_DIM), query_seg, key_seg
        )
        highest = jnp.max(scores, -1, keepdims=True)
        weight = jnp.exp(scores - highest)
        total = jnp.sum(weight, -1, keepdims=True)
        probabilities = (weight / total).astype(jnp.bfloat16)
        mixed_heads = jnp.einsum(
            "grij,jgd->igrd", probabilities, value_heads, preferred_element_type=jnp.float32
        )
        return (
            mixed_heads.reshape(local_len, query_width).astype(jnp.bfloat16),
            highest + jnp.log(total),
        )

    attended, log_total = lax.map(
        attend, (queries, key_all, value_all, query_segments, segment_ids)
    )
    mixed_rows = attended.reshape(token_rows, query_width)
    middle = source + by_columns(mixed_rows, out_full)
    gate_full, up_full, down_full, mlp_gain_full = fetch_mlp(
        gate_weight, up_weight, down_weight, mlp_gain
    )
    gain_two = mlp_gain_full.astype(jnp.float32)
    inv_two = lax.rsqrt(jnp.mean(middle * middle, -1, keepdims=True) + EPSILON)
    normed_two = middle * inv_two
    normed_mid = (normed_two * gain_two).astype(jnp.bfloat16)
    gate_value = jnp.dot(normed_mid, gate_full, preferred_element_type=jnp.float32)
    up_value = jnp.dot(normed_mid, up_full, preferred_element_type=jnp.float32)
    active = (jax.nn.silu(gate_value) * up_value).astype(jnp.bfloat16)
    result = (
        (middle + by_columns(active, down_full))
        .astype(jnp.bfloat16)
        .reshape(seq_b, local_len, width)
    )
    gate_back, up_back, down_back, unused_gain = fetch_mlp(
        gate_weight, up_weight, down_weight, mlp_gain
    )
    cotangent = grad_output.reshape(token_rows, width)
    grad_active = jnp.dot(cotangent, down_back, preferred_element_type=jnp.float32)
    sigmoid_gate = jax.nn.sigmoid(gate_value)
    grad_gate = (
        grad_active * up_value * sigmoid_gate * (1.0 + gate_value * (1.0 - sigmoid_gate))
    ).astype(jnp.bfloat16)
    grad_up = (grad_active * jax.nn.silu(gate_value)).astype(jnp.bfloat16)
    grad_norm_mid = by_columns(grad_gate, gate_back) + by_columns(grad_up, up_back)
    gain_two_term = jnp.sum(grad_norm_mid * normed_two, 0)
    scaled_two = grad_norm_mid * gain_two
    grad_middle = cotangent.astype(jnp.float32) + inv_two * (
        scaled_two - normed_two * jnp.mean(scaled_two * normed_two, -1, keepdims=True)
    )
    mlp_grads = lax.psum_scatter(
        jnp.concatenate(
            [
                by_rows(normed_mid, grad_gate),
                by_rows(normed_mid, grad_up),
                by_rows(cotangent, active),
            ],
            1,
        ),
        ("batch", "seq"),
        scatter_dimension=0,
        tiled=True,
    )
    query_back, key_back, value_back, out_back, unused_attn = fetch_attention(
        query_weight, key_weight, value_weight, out_weight, attn_gain
    )
    grad_branch = grad_middle.astype(jnp.bfloat16)
    grad_mixed = jnp.dot(grad_branch, out_back, preferred_element_type=jnp.float32).astype(
        jnp.bfloat16
    )
    out_term = by_rows(grad_branch, mixed_rows)

    def attend_back(entries):
        query_seq, key_seq, value_seq, query_seg, key_seg, log_seq, grad_seq = entries
        key_heads = key_seq.reshape(seq_len, KV_HEADS, HEAD_DIM)
        value_heads = value_seq.reshape(seq_len, KV_HEADS, HEAD_DIM)
        scores = scores_of(query_seq, key_heads, query_seg, key_seg)
        probabilities = jnp.exp(scores - log_seq)
        grad_grouped = grad_seq.reshape(local_len, KV_HEADS, repeat, HEAD_DIM)
        grad_probs = jnp.einsum(
            "igrd,jgd->grij", grad_grouped, value_heads, preferred_element_type=jnp.float32
        )
        centre = jnp.sum(probabilities * grad_probs, -1, keepdims=True)
        grad_scores = (probabilities * (grad_probs - centre)).astype(jnp.bfloat16)
        grad_values = jnp.einsum(
            "grij,igrd->jgd",
            probabilities.astype(jnp.bfloat16),
            grad_grouped,
            preferred_element_type=jnp.float32,
        )
        grad_keys = (
            jnp.einsum(
                "grij,igrd->jgd",
                grad_scores,
                query_seq.reshape(local_len, KV_HEADS, repeat, HEAD_DIM),
                preferred_element_type=jnp.float32,
            )
            * scaling
        )
        grad_queries = (
            jnp.einsum("grij,jgd->igrd", grad_scores, key_heads, preferred_element_type=jnp.float32)
            * scaling
        )
        return (
            grad_queries.reshape(local_len, HEADS, HEAD_DIM),
            grad_keys.reshape(seq_len, key_width),
            grad_values.reshape(seq_len, key_width),
        )

    grad_queries, grad_keys_all, grad_values_all = lax.map(
        attend_back,
        (
            queries,
            key_all,
            value_all,
            query_segments,
            segment_ids,
            log_total,
            grad_mixed.reshape(seq_b, local_len, query_width),
        ),
    )
    grad_keys, grad_values = (
        lax.psum_scatter(grad_keys_all, "seq", scatter_dimension=1, tiled=True),
        lax.psum_scatter(grad_values_all, "seq", scatter_dimension=1, tiled=True),
    )
    grad_q_raw = (
        unrotate(grad_queries, cosine, sine_table)
        .astype(jnp.bfloat16)
        .reshape(token_rows, query_width)
    )
    grad_k_raw = (
        unrotate(grad_keys.reshape(seq_b, local_len, KV_HEADS, HEAD_DIM), cosine, sine_table)
        .astype(jnp.bfloat16)
        .reshape(token_rows, key_width)
    )
    grad_v_raw = grad_values.astype(jnp.bfloat16).reshape(token_rows, key_width)
    grad_norm_one = (
        by_columns(grad_q_raw, query_back)
        + by_columns(grad_k_raw, key_back)
        + by_columns(grad_v_raw, value_back)
    )
    gain_one_term = jnp.sum(grad_norm_one * normed_one, 0)
    scaled_one = grad_norm_one * gain_one
    grad_input = grad_middle + inv_one * (
        scaled_one - normed_one * jnp.mean(scaled_one * normed_one, -1, keepdims=True)
    )
    attn_term = jnp.concatenate(
        [
            by_rows(normed_low, grad_q_raw),
            by_rows(normed_low, grad_k_raw),
            by_rows(normed_low, grad_v_raw),
            out_term,
        ],
        1,
    )
    gains_term = jnp.stack([gain_one_term, gain_two_term], 1)
    attn_grads, gain_grads = (
        lax.psum_scatter(attn_term, ("batch", "seq"), scatter_dimension=0, tiled=True),
        lax.psum_scatter(gains_term, ("batch", "seq"), scatter_dimension=0, tiled=True),
    )
    ff_width = gate_weight.shape[1]
    return (
        result,
        grad_input.reshape(seq_b, local_len, width),
        gain_grads[:, 0],
        attn_grads[:, :query_width],
        attn_grads[:, query_width : query_width + key_width],
        attn_grads[:, query_width + key_width : query_width + 2 * key_width],
        attn_grads[:, query_width + 2 * key_width :],
        gain_grads[:, 1],
        mlp_grads[:, :ff_width],
        mlp_grads[:, ff_width : 2 * ff_width],
        mlp_grads[:, 2 * ff_width :],
    )


def solution(mesh):
    in_specs = (
        P("batch", "seq", None),
        P(("batch", "seq")),
        P(("batch", "seq"), None),
        P(("batch", "seq"), None),
        P(("batch", "seq"), None),
        P(("batch", "seq"), None),
        P(("batch", "seq")),
        P(("batch", "seq"), None),
        P(("batch", "seq"), None),
        P(("batch", "seq"), None),
        P("batch", None),
        P("batch", "seq", None),
    )
    out_specs = (
        P("batch", "seq", None),
        P("batch", "seq", None),
        P(("batch", "seq")),
        P(("batch", "seq"), None),
        P(("batch", "seq"), None),
        P(("batch", "seq"), None),
        P(("batch", "seq"), None),
        P(("batch", "seq")),
        P(("batch", "seq"), None),
        P(("batch", "seq"), None),
        P(("batch", "seq"), None),
    )
    return jax.shard_map(shards, mesh=mesh, in_specs=in_specs, out_specs=out_specs, check_vma=False)
```

profile of v0, /device:TPU:0, one launch (start us, length us, event | category | flops | bytes accessed | tf_op | source)
XLA Modules:
  0.0 4677.8 jit_solution(3533639103870512994)
XLA Ops:
  11.2 42.2 all-reduce.2
  55.7 17.3 all-gather.10.cloned.1.call-done
  73.0 3.1 convolution_convert_fusion.1
  77.7 56.4 %all-gather.14.cloned.1.call-done = bf16[2560,640]{1,0:T(8,128)(2,1)} async-done(((bf16[80,640]{1,0:T(8,128)(2,1)}), bf16[2560,640]{1,0:T(8,128)(2,1)}) %all-gather.14.cloned.1.call-update) | async-done | bytes 3276816 | tf_op jit(solution)/shard_map/all_gather | solution.py:46
  134.1 5.6 copy.59
  139.7 3.0 fusion.33
  147.1 87.3 %all-gather.18.cloned.1.call-done = bf16[2560,2560]{1,0:T(8,128)(2,1)} async-done(((bf16[80,2560]{1,0:T(8,128)(2,1)}), bf16[2560,2560]{1,0:T(8,128)(2,1)}) %all-gather.18.cloned.1.call-update) | async-done | bytes 13107216 | tf_op jit(solution)/shard_map/all_gather | solution.py:45
  234.4 17.9 copy.60
  252.3 6.9 fusion.31
  259.7 32.3 all-gather.12.cloned.1.call-done
  292.0 57.6 %all-gather.16.cloned.1.call-done = bf16[2,1024,640]{1,2,0:T(8,128)(2,1)} async-done(((bf16[2,128,640]{1,2,0:T(8,128)(2,1)}), bf16[2,1024,640]{1,2,0:T(8,128)(2,1)}) %all-gather.16.cloned.1.call-update) | async-done | bytes 2621456 | tf_op jit(solution)/shard_map/all_gather | solution.py:124
  349.5 60.6 %while.28 = (s32[]{:T(128)}, bf16[2,128,2560]{2,1,0:T(8,128)(2,1)}, f32[2,8,4,128,1]{3,2,1,4,0:T(4,128)S(1)}, bf16[2,1024,640]{1,2,0:T(8,128)(2,1)}, s32[2,128]{...) while((s32[]{:T(128)}, bf16[2,128,2560]{2,1,0:T(8,128)(2,1)}, ...), condition=%wide.region_4.5_spmd.clone, body=%wide.region_1.4_spmd.clone.sunk | while | flops 1393225856 | bytes 64109192 | solution.py:157
  351.9 7.4 fusion.131
  359.3 9.4 fusion.132
  368.8 8.9 fusion.133
  382.3 7.2 fusion.131
  389.6 9.4 fusion.132
  399.0 8.9 fusion.133
  410.1 38.9 all-gather.20.cloned.1.call-done
  449.0 7.2 multiply_reduce_fusion.4
  458.0 195.9 %all-gather.24.cloned.1.call-done = bf16[2560,6912]{1,0:T(8,128)(2,1)} async-done(((bf16[80,6912]{1,0:T(8,128)(2,1)}), bf16[2560,6912]{1,0:T(8,128)(2,1)}) %all-gather.24.cloned.1.call-update) | async-done | bytes 35389456 | tf_op jit(solution)/shard_map/all_gather | solution.py:56
  653.9 19.9 fusion.52
  673.8 185.0 %all-gather.22.cloned.1.call-done = bf16[2560,6912]{1,0:T(8,128)(2,1)} async-done(((bf16[80,6912]{1,0:T(8,128)(2,1)}), bf16[2560,6912]{1,0:T(8,128)(2,1)}) %all-gather.22.cloned.1.call-update) | async-done | bytes 35389456 | tf_op jit(solution)/shard_map/all_gather | solution.py:55
  858.8 19.6 fusion.51
  878.3 185.3 %all-gather.26.cloned.1.call-done = bf16[2560,6912]{1,0:T(8,128)(2,1)} async-done(((bf16[80,6912]{1,0:T(8,128)(2,1)}), bf16[2560,6912]{1,0:T(8,128)(2,1)}) %all-gather.26.cloned.1.call-update) | async-done | bytes 35389456 | tf_op jit(solution)/shard_map/all_gather | solution.py:57
  1063.6 24.5 multiply_convert_fusion
  1088.1 17.9 fusion.53
  1106.0 20.4 multiply_reduce_fusion
  1126.4 3.3 multiply_add_fusion.1
  1129.7 9.2 convolution_convert_fusion
  1138.9 116.9 %while.29 = (s32[]{:T(128)}, f32[2,128,32,80]{1,3,2,0:T(8,128)}, f32[2,1024,640]{1,2,0:T(8,128)}, f32[2,1024,640]{2,1,0:T(8,128)}, bf16[2,1024,640]{1,2,0:T(8,12...) while((s32[]{:T(128)}, f32[2,128,32,80]{1,3,2,0:T(8,128)}, ...), condition=%wide.region_9.10_spmd.clone, body=%wide.region_7.9_spmd.clone.sunk | while | flops 3394564096 | bytes 292920480 | solution.py:252
  1145.5 9.9 fusion.147
  1155.5 9.7 fusion.148
  1165.2 9.9 fusion.149
  1175.1 3.2 copy.129
  1178.3 5.1 convolution_multiply_fusion.2
  1183.4 6.2 bitcast_multiply_fusion.4
  1192.7 2.4 copy-done.18
  1203.9 9.9 fusion.147
  1213.9 9.7 fusion.148
  1223.5 9.9 fusion.149
  1233.5 3.2 copy.129
  1236.6 5.1 convolution_multiply_fusion.2
  1241.8 6.2 bitcast_multiply_fusion.4
  1259.5 9.3 fusion.29
  1268.8 10.7 fusion.37
  1279.6 10.8 fusion.27
  1290.4 66.7 %reduce-scatter.10.cloned.1.call-done = f32[2,128,640]{1,2,0:T(8,128)} async-done(((f32[2,1024,640]{1,2,0:T(8,128)}), f32[2,128,640]{1,2,0:T(8,128)}) %reduce-scatter.10.cloned.1.call-update) | async-done | bytes 655376 | tf_op jit(solution)/shard_map/reduce_scatter | solution.py:265
  1358.7 3.7 fusion.40
  1362.4 100.6 %reduce-scatter.12.cloned.1.call-done = f32[2,128,640]{2,1,0:T(8,128)} async-done(((f32[2,1024,640]{2,1,0:T(8,128)}), f32[2,128,640]{2,1,0:T(8,128)}) %reduce-scatter.12.cloned.1.call-update) | async-done | bytes 655376 | tf_op jit(solution)/shard_map/reduce_scatter | solution.py:266
  1464.2 4.0 convolution_bitcast_fusion.1
  1470.9 3.4 multiply_reduce_fusion.1
  1475.9 44.8 pad_maximum_fusion.1
  1520.7 62.2 %copy.87 = f32[2560,6400]{1,0:T(8,128)} copy(f32[2560,6400]{0,1:T(8,128)} %pad_maximum_fusion.1) | data formatting | bytes 131072000
  1584.2 26.7 convolution_bitcast_fusion
  1610.9 27.2 fusion.55
  1638.1 26.8 fusion.54
  1664.9 138.5 %pad_maximum_fusion = f32[2560,20736]{1,0:T(8,128)} fusion(f32[2560,6912]{1,0:T(8,128)} %convolution_bitcast_fusion, f32[2560,6912]{1,0:T(8,128)} %fusion.55, f32[2560,6912]{1,0:T(8,128)} %fusion.54), kind=kLoop, calls=%fused_computation.50 | loop fusion | flops 106168320 | bytes 424673280 | tf_op jit(solution)/shard_map/concatenate | solution.py:194
  1803.5 18.3 fusion.26
  1821.8 4.7 multiply_add_fusion
  1828.6 1151.5 %reduce-scatter.18.cloned.1.call-done = f32[80,6400]{1,0:T(8,128)} async-done(((f32[2560,6400]{1,0:T(8,128)}), f32[80,6400]{1,0:T(8,128)}) %reduce-scatter.18.cloned.1.call-update) | async-done | bytes 2048016
  2981.9 2.7 fusion.47
  2984.6 1680.5 %reduce-scatter.14.cloned.1.call-done = f32[80,20736]{1,0:T(8,128)} async-done(((f32[2560,20736]{1,0:T(8,128)}), f32[80,20736]{1,0:T(8,128)}) %reduce-scatter.14.cloned.1.call-update) | async-done | bytes 6635536 | tf_op jit(solution)/shard_map/reduce_scatter | solution.py:193
  4665.1 5.9 fusion.46
  (252 shorter events, 64.9 us)
Async XLA Ops:
  7.2 47.9 %copy-start.3 = (bf16[2,128,2560]{2,1,0:T(8,128)(2,1)S(1)}, bf16[2,128,2560]{2,1,0:T(8,128)(2,1)}, u32[]{:S(2)}) copy-start(bf16[2,128,2560]{2,1,0:T(8,128)(2,1)} %param.16) | copy-start | bytes 3932164
  7.2 65.8 %all-gather.10.cloned.1.call-start = ((), (), s32[]{:S(2)}) async-start(), calls=%async_computation.5 | async-start | bytes 3379200 | tf_op jit(solution)/shard_map/all_gather | solution.py:47
  7.9 126.2 %all-gather.14.cloned.1.call-start = ((), (), s32[]{:S(2)}) async-start(), calls=%async_computation.7 | async-start | bytes 3379200 | tf_op jit(solution)/shard_map/all_gather | solution.py:46
  8.7 225.7 %all-gather.18.cloned.1.call-start = ((), (), s32[]{:S(2)}) async-start(), calls=%async_computation.9 | async-start | bytes 13516800 | tf_op jit(solution)/shard_map/all_gather | solution.py:45
  9.4 282.6 %all-gather.12.cloned.1.call-start = ((), (), s32[]{:S(2)}) async-start(), calls=%async_computation.6 | async-start | bytes 2949120 | tf_op jit(solution)/shard_map/all_gather | solution.py:125
  53.4 23.9 copy-start.31
  77.1 272.5 %all-gather.16.cloned.1.call-start = ((), (), s32[]{:S(2)}) async-start(), calls=%async_computation.8 | async-start | bytes 2949120 | tf_op jit(solution)/shard_map/all_gather | solution.py:124
  77.3 181.9 %copy-start.27 = (f32[128,40]{0,1:T(8,128)}, f32[128,40]{0,1:T(8,128)S(1)}, u32[]{:S(2)}) copy-start(f32[128,40]{0,1:T(8,128)S(1)} %get-tuple-element.333) | copy-start | bytes 61444
  77.3 181.9 %copy-start.29 = (f32[128,40]{0,1:T(8,128)}, f32[128,40]{0,1:T(8,128)S(1)}, u32[]{:S(2)}) copy-start(f32[128,40]{0,1:T(8,128)S(1)} %get-tuple-element.334) | copy-start | bytes 61444
  77.7 174.6 %copy-start.9 = (bf16[2,128,2560]{2,1,0:T(8,128)(2,1)}, bf16[2,128,2560]{2,1,0:T(8,128)(2,1)S(1)}, u32[]{:S(2)}) copy-start(bf16[2,128,2560]{2,1,0:T(8,128)(2,1)S(1)} %multiply_convert_fusion.4) | copy-start | bytes 3932164
  142.8 4.3 copy-start.34
  143.6 305.4 %all-gather.20.cloned.1.call-start = ((), (), s32[]{:S(2)}) async-start(), calls=%async_computation.10 | async-start | bytes 13516800 | tf_op jit(solution)/shard_map/all_gather | solution.py:48
  144.2 509.7 %all-gather.24.cloned.1.call-start = ((), (), s32[]{:S(2)}) async-start(), calls=%async_computation.12 | async-start | bytes 36495360 | tf_op jit(solution)/shard_map/all_gather | solution.py:56
  144.9 713.8 %all-gather.22.cloned.1.call-start = ((), (), s32[]{:S(2)}) async-start(), calls=%async_computation.11 | async-start | bytes 36495360 | tf_op jit(solution)/shard_map/all_gather | solution.py:55
  145.7 918.0 %all-gather.26.cloned.1.call-start = ((), (), s32[]{:S(2)}) async-start(), calls=%async_computation.13 | async-start | bytes 36495360 | tf_op jit(solution)/shard_map/all_gather | solution.py:57
  146.4 1210.7 %reduce-scatter.10.cloned.1.call-start = ((), (), s32[]{:S(2)}) async-start(), calls=%async_computation.14 | async-start | bytes 5898240 | tf_op jit(solution)/shard_map/reduce_scatter | solution.py:265
  349.5 99.5 %copy-start.4 = (bf16[2,128,2560]{2,1,0:T(8,128)(2,1)S(1)}, bf16[2,128,2560]{2,1,0:T(8,128)(2,1)}, u32[]{:S(2)}) copy-start(bf16[2,128,2560]{2,1,0:T(8,128)(2,1)} %param.16) | copy-start | bytes 3932164
  449.0 8.7 copy-start.37
  458.0 400.8 %copy-start.12 = (bf16[256,2560]{1,0:T(8,128)(2,1)}, bf16[256,2560]{1,0:T(8,128)(2,1)S(1)}, u32[]{:S(2)}) copy-start(bf16[256,2560]{1,0:T(8,128)(2,1)S(1)} %multiply_convert_fusion.3) | copy-start | bytes 3932164
  1106.0 20.4 copy-start.19
  1129.6 9.2 copy-start.7
  1139.1 2.1 copy-start.1
  1178.3 11.5 slice-start.2
  1178.3 13.0 slice-start
  1183.4 6.2 copy-start.22
  1183.4 6.3 slice-start.3
  1183.4 7.8 slice-start.1
  1189.8 2.7 copy-start
  1192.5 2.7 copy-start.18
  1192.5 5.0 copy-start.2
  1192.5 5.0 copy-start.16
  1192.5 5.0 copy-start.36
  1192.5 5.0 copy-start.44
  1195.1 2.3 copy-start.17
  1197.5 2.1 copy-start.1
  1236.6 11.5 slice-start.2
  1236.6 13.0 slice-start
  1241.8 6.2 copy-start.22
  1241.8 6.3 slice-start.3
  1241.8 7.8 slice-start.1
  1248.1 2.7 copy-start
  1250.8 2.7 copy-start.18
  1250.8 5.0 copy-start.2
  1250.8 5.0 copy-start.16
  1250.8 5.0 copy-start.36
  1250.8 5.0 copy-start.44
  1253.5 2.3 copy-start.17
  1255.8 207.2 %reduce-scatter.12.cloned.1.call-start = ((), (), s32[]{:S(2)}) async-start(), calls=%async_computation.15 | async-start | bytes 5898240 | tf_op jit(solution)/shard_map/reduce_scatter | solution.py:266
  1256.6 569.9 %reduce-scatter.16.cloned.1.call-start = ((), (), s32[]{:S(2)}) async-start(), calls=%async_computation.17 | async-start | bytes 1351680
  1259.5 9.4 copy-start.8
  1259.5 9.4 copy-start.26
  1268.8 10.8 copy-start.10
  1464.2 4.1 copy-start.11
  1464.2 4.4 copy-start.25
  1468.6 2.3 copy-start.21
  1468.6 2.3 copy-start.32
  1468.6 2.3 copy-start.39
  1475.9 1504.3 %reduce-scatter.18.cloned.1.call-start = ((), (), s32[]{:S(2)}) async-start(), calls=%async_computation.18 | async-start | bytes 67584000
  1582.9 3082.2 %reduce-scatter.14.cloned.1.call-start = ((), (), s32[]{:S(2)}) async-start(), calls=%async_computation.16 | async-start | bytes 218972160 | tf_op jit(solution)/shard_map/reduce_scatter | solution.py:193
  1584.2 26.7 copy-start.13
  1803.4 18.3 copy-start.42
  1803.4 18.3 copy-start.6
  1803.4 18.3 copy-start.33
  1803.5 18.3 copy-start.40
  (16 other events, 25.1 us)
Sparse Core Ops, SparseCore 0:
  10.9 62.1 all-gather.9
  75.8 58.2 all-gather.13
  137.0 97.3 all-gather.17
  236.9 55.0 all-gather.11
  294.5 55.0 all-gather.15
  352.2 96.7 all-gather.19
  452.0 201.8 all-gather.23
  656.9 201.8 all-gather.21
  861.8 201.8 all-gather.25
  1256.0 101.1 reduce-scatter.9
  1360.7 102.2 reduce-scatter.11
  1476.0 135.3 reduce-scatter.15
  1613.8 1366.2 reduce-scatter.17
  2986.4 1678.6 reduce-scatter.13
where the time goes:
time: 4680 us
  waiting for transfers between devices  3860 us (82%)
  matrix products  373 us (8%)
  other arithmetic  239 us (5%)
  local copies, waits for them, and re-layouts  146 us (3%)
    reduce_scatter x1, waiting for transfers between devices, shards(): lax.psum_scatter(jnp.concatenate([by_rows(normed_mid, grad_gate), by_rows...  1680 us
    unnamed x16, waiting for transfers between devices  1160 us
    all_gather x1, waiting for transfers between devices, fetch_mlp(): lax.all_gather(up_weight, ('batch', 'seq'), axis=0, tiled=True)  196 us
    all_gather x1, waiting for transfers between devices, fetch_mlp(): lax.all_gather(down_weight, ('batch', 'seq'), axis=0, tiled=True)  185 us
    all_gather x1, waiting for transfers between devices, fetch_mlp(): lax.all_gather(gate_weight, ('batch', 'seq'), axis=0, tiled=True)  185 us
    concatenate x1, other arithmetic, shards(): jnp.concatenate([by_rows(normed_mid, grad_gate), by_rows(normed_mid, grad...  139 us
    dot_general x7, matrix products, by_rows(): lax.dot_general(left, right, (((0,), (0,)), ((), ())), preferred_element_...  110 us
    reduce_scatter x1, waiting for transfers between devices, shards(): lax.psum_scatter(grad_values_all, 'seq', scatter_dimension=1, tiled=True)  101 us
  transfers between devices with their start and end apart: 14, of which 13 were waited for; matrix products, arithmetic and copies ran while one was open for 12% of the time, Pallas kernels for 0%

commit v1 on v0

v1 whole, which is shorter than its diff:
```python
import math

import jax
import jax.numpy as jnp
from jax import lax
from jax.sharding import Mesh
from jax.sharding import PartitionSpec as P

HEADS = 32
KV_HEADS = 8
HEAD_DIM = 80
HALF = HEAD_DIM // 2
REPEAT = HEADS // KV_HEADS

EPSILON = 1e-05
ROPE_BASE = 10000.0

CHIPS = 4
SPLIT = 2 * CHIPS
PLANE = ("y", "core", "lo")
EVERY = ("y", "core", "hi", "lo")


def dot(left, right):
    return lax.dot_general(
        left, right, (((1,), (0,)), ((), ())), preferred_element_type=jnp.float32
    )


def by_columns(left, right):
    return lax.dot_general(
        left, right, (((1,), (1,)), ((), ())), preferred_element_type=jnp.float32
    )


def by_rows(left, right):
    return lax.dot_general(
        left, right, (((0,), (0,)), ((), ())), preferred_element_type=jnp.float32
    )


def swap_core(value):
    return lax.ppermute(value, "core", [(0, 1), (1, 0)])


def swap_chip(value, step):
    return lax.ppermute(value, ("y", "lo"), [(chip, chip ^ step) for chip in range(CHIPS)])


def gather_plane(value):
    slots = []
    for step in range(CHIPS):
        here = value if step == 0 else swap_chip(value, step)
        slots += [here, swap_core(here)]
    return jnp.concatenate(slots, 0)


def scatter_plane(partial):
    rows, cols = partial.shape[0] // SPLIT, partial.shape[1]
    slots = partial.astype(jnp.bfloat16).reshape(CHIPS, 2, rows, cols)
    total = None
    for step in range(CHIPS - 1, -1, -1):
        pair = slots[step, 0].astype(jnp.float32) + swap_core(slots[step, 1]).astype(jnp.float32)
        if step:
            pair = swap_chip(pair.astype(jnp.bfloat16), step).astype(jnp.float32)
        total = pair if total is None else total + pair
    return total


def to_plane(weight):
    rows, cols = weight.shape[0], weight.shape[1] // SPLIT
    split = jnp.swapaxes(weight.reshape(rows, SPLIT, cols), 0, 1)
    return lax.all_to_all(split, PLANE, 0, 0, tiled=True).reshape(SPLIT * rows, cols)


def from_plane(grads):
    rows, cols = grads.shape[0] // SPLIT, grads.shape[1]
    back = lax.all_to_all(grads.reshape(SPLIT, rows, cols), PLANE, 0, 0, tiled=True)
    return jnp.swapaxes(back, 0, 1)


def along(weight):
    return lax.all_gather(weight, "hi", axis=0, tiled=True)


def sum_along(grads):
    return lax.psum_scatter(grads, "hi", scatter_dimension=0, tiled=True)


def by_step(value, at, axis):
    steps = [
        lax.dynamic_index_in_dim(value, at ^ step, axis) for step in range(value.shape[axis])
    ]
    return jnp.concatenate(steps, axis)


def rotate(values, cosine, sine_table):
    first_half, second_half = values[..., :HALF], values[..., HALF:]
    return jnp.concatenate(
        [
            first_half * cosine - second_half * sine_table,
            second_half * cosine + first_half * sine_table,
        ],
        -1,
    )


def shards(
    sizes,
    hidden_in,
    attn_gain,
    query_weight,
    key_weight,
    value_weight,
    out_weight,
    mlp_gain,
    gate_weight,
    up_weight,
    down_weight,
    segment_ids,
    grad_output,
):
    y_n, hi_n, lo_n = sizes
    batch_n = 2 * y_n
    seq_b, local_len, width = hidden_in.shape
    seq_len = segment_ids.shape[1]
    rows = seq_b * local_len
    tokens = SPLIT * rows
    own_rows = query_weight.shape[0]
    ff_width = gate_weight.shape[1]
    ff_pad = -(-ff_width // (SPLIT * 128)) * SPLIT * 128
    query_cols = HEADS * HEAD_DIM // SPLIT
    qkv_cols = query_cols + 2 * HEAD_DIM
    scaling = 1.0 / math.sqrt(HEAD_DIM)
    y_at, core_at = lax.axis_index("y"), lax.axis_index("core")
    hi_at, lo_at = lax.axis_index("hi"), lax.axis_index("lo")

    def reorder(value):
        lead = value.shape[:-1]
        value = value.reshape(lead + (batch_n, hi_n, lo_n * own_rows))
        return jnp.swapaxes(value, -3, -2).reshape(lead + (width,))

    def restore(value):
        lead = value.shape[:-1]
        value = value.reshape(lead + (hi_n, batch_n, lo_n * own_rows))
        return jnp.swapaxes(value, -3, -2).reshape(lead + (width,))

    offset = (hi_at * lo_n + lo_at) * local_len
    own_segments = lax.dynamic_slice_in_dim(segment_ids, offset, local_len, 1)
    small = jnp.concatenate(
        [attn_gain, mlp_gain, own_segments.astype(jnp.bfloat16).reshape(rows)]
    )
    small_pad = -(-small.shape[0] // 128) * 128
    small = jnp.pad(small, (0, small_pad - small.shape[0])).reshape(1, small_pad)
    small = lax.all_gather(small, EVERY, axis=0, tiled=True).astype(jnp.float32)
    small = small.reshape(batch_n, hi_n, lo_n, small_pad)
    gain_one = reorder(small[..., :own_rows].reshape(width))
    gain_two = reorder(small[..., own_rows : 2 * own_rows].reshape(width))
    segments = small[..., 2 * own_rows : 2 * own_rows + rows].reshape(
        y_n, 2, hi_n, lo_n, seq_b, local_len
    )
    segments = by_step(segments, y_at, 0)
    segments = by_step(segments, core_at, 1)
    segments = by_step(segments, lo_at, 3)
    segments = segments.transpose(0, 1, 4, 2, 3, 5)
    seqs = y_n * 2 * seq_b
    key_segments = segments.reshape(seqs, seq_len)
    queries_len = lo_n * local_len
    query_segments = lax.dynamic_index_in_dim(segments, hi_at, 3, keepdims=False).reshape(
        seqs, queries_len
    )
    lo_place = lo_at ^ jnp.arange(lo_n)
    inner = (lo_place[:, None] * local_len + jnp.arange(local_len)[None, :]).reshape(queries_len)
    query_place = hi_at * queries_len + inner
    key_place = (jnp.arange(hi_n)[:, None] * queries_len + inner[None, :]).reshape(seq_len)
    frequency = ROPE_BASE ** (-(jnp.arange(HALF, dtype=jnp.float32) * 2.0 / HEAD_DIM))
    angles = query_place.astype(jnp.float32)[:, None] * frequency[None, :]

    def table(values):
        values = values.reshape(1, lo_n, 1, 1, local_len, 1, HALF)
        values = jnp.broadcast_to(values, (y_n, lo_n, 2, seq_b, local_len, 1, HALF))
        return values.reshape(tokens, 1, HALF)

    cosine, sine_table = table(jnp.cos(angles)), table(jnp.sin(angles))

    heads_weight = jnp.concatenate(
        [
            query_weight.reshape(own_rows, SPLIT, query_cols),
            key_weight.reshape(own_rows, SPLIT, HEAD_DIM),
            value_weight.reshape(own_rows, SPLIT, HEAD_DIM),
            jnp.zeros((own_rows, SPLIT, 512 - qkv_cols), jnp.bfloat16),
            out_weight.reshape(own_rows, SPLIT, query_cols),
            jnp.zeros((own_rows, SPLIT, 384 - query_cols), jnp.bfloat16),
        ],
        -1,
    ).reshape(own_rows, SPLIT * 896)
    heads_plane = to_plane(heads_weight)
    qkv_full = along(heads_plane[:, :512])
    out_full = along(heads_plane[:, 512:])

    def widen(weight):
        return jnp.pad(weight, ((0, 0), (0, ff_pad - ff_width)))

    gate_full = along(to_plane(widen(gate_weight)))
    up_full = along(to_plane(widen(up_weight)))
    down_full = along(to_plane(widen(down_weight)))

    source = reorder(hidden_in.reshape(rows, width)).astype(jnp.float32)
    inv_one = lax.rsqrt(jnp.mean(source * source, -1, keepdims=True) + EPSILON)
    normed_one = source * inv_one
    normed_low = gather_plane((normed_one * gain_one).astype(jnp.bfloat16))
    cotangent = reorder(grad_output.reshape(rows, width))
    cotangent_all = gather_plane(cotangent)

    qkv = dot(normed_low, qkv_full)
    queries = rotate(qkv[:, :query_cols].reshape(tokens, REPEAT, HEAD_DIM), cosine, sine_table)
    key_rows = rotate(
        qkv[:, query_cols : query_cols + HEAD_DIM].reshape(tokens, 1, HEAD_DIM), cosine, sine_table
    )
    queries = queries.astype(jnp.bfloat16)
    key_value = jnp.concatenate(
        [key_rows.reshape(tokens, HEAD_DIM), qkv[:, query_cols + HEAD_DIM : qkv_cols]], 1
    ).astype(jnp.bfloat16)
    key_value = along(key_value)

    def by_seq(values):
        last = values.shape[1:]
        lead = values.shape[0] // tokens
        values = values.reshape((lead, y_n, lo_n, 2, seq_b, local_len) + last)
        values = values.transpose((1, 3, 4, 0, 2, 5) + tuple(range(6, 6 + len(last))))
        return values.reshape((seqs, lead * queries_len) + last)

    def by_token(values):
        last = values.shape[2:]
        lead = values.shape[1] // queries_len
        values = values.reshape((y_n, 2, seq_b, lead, lo_n, local_len) + last)
        values = values.transpose((3, 0, 4, 1, 2, 5) + tuple(range(6, 6 + len(last))))
        return values.reshape((lead * tokens,) + last)

    queries = by_seq(queries)
    key_value = by_seq(key_value)
    key_all, value_all = key_value[..., :HEAD_DIM], key_value[..., HEAD_DIM:]

    def scores_of(query_seq, key_seq, query_seg, key_seg):
        raw_scores = (
            jnp.einsum("ird,jd->rij", query_seq, key_seq, preferred_element_type=jnp.float32)
            * scaling
        )
        allowed = (query_seg[:, None] == key_seg[None, :]) & (
            key_place[None, :] <= query_place[:, None]
        )
        return jnp.where(allowed, raw_scores, -1e30)

    def attend(entries):
        query_seq, key_seq, value_seq, query_seg, key_seg = entries
        scores = scores_of(query_seq, key_seq, query_seg, key_seg)
        highest = jnp.max(scores, -1, keepdims=True)
        weight = jnp.exp(scores - highest)
        total = jnp.sum(weight, -1, keepdims=True)
        probabilities = (weight / total).astype(jnp.bfloat16)
        mixed_heads = jnp.einsum(
            "rij,jd->ird", probabilities, value_seq, preferred_element_type=jnp.float32
        )
        return mixed_heads.astype(jnp.bfloat16), highest + jnp.log(total)

    attended, log_total = lax.map(
        attend, (queries, key_all, value_all, query_segments, key_segments)
    )
    mixed_rows = by_token(attended).reshape(tokens, query_cols)
    mixed_rows = jnp.pad(mixed_rows, ((0, 0), (0, 384 - query_cols)))
    middle = source + scatter_plane(by_columns(mixed_rows, out_full))

    inv_two = lax.rsqrt(jnp.mean(middle * middle, -1, keepdims=True) + EPSILON)
    normed_two = middle * inv_two
    normed_mid = gather_plane((normed_two * gain_two).astype(jnp.bfloat16))
    gate_value = dot(normed_mid, gate_full)
    up_value = dot(normed_mid, up_full)
    active = (jax.nn.silu(gate_value) * up_value).astype(jnp.bfloat16)
    result = restore((middle + scatter_plane(by_columns(active, down_full))).astype(jnp.bfloat16))
    grad_active = dot(cotangent_all, down_full)
    sigmoid_gate = jax.nn.sigmoid(gate_value)
    grad_gate = (
        grad_active * up_value * sigmoid_gate * (1.0 + gate_value * (1.0 - sigmoid_gate))
    ).astype(jnp.bfloat16)
    grad_up = (grad_active * jax.nn.silu(gate_value)).astype(jnp.bfloat16)
    grad_norm_mid = scatter_plane(by_columns(grad_gate, gate_full) + by_columns(grad_up, up_full))
    gain_two_term = jnp.sum(grad_norm_mid * normed_two, 0)
    scaled_two = grad_norm_mid * gain_two
    grad_middle = cotangent.astype(jnp.float32) + inv_two * (
        scaled_two - normed_two * jnp.mean(scaled_two * normed_two, -1, keepdims=True)
    )

    def finish(left, right):
        return from_plane(sum_along(by_rows(left, right).astype(jnp.bfloat16)))

    def finish_mlp(left, right):
        grads = finish(left, right).reshape(own_rows, ff_pad)
        return grads[:, :ff_width].astype(jnp.float32)

    gate_grads = finish_mlp(normed_mid, grad_gate)
    up_grads = finish_mlp(normed_mid, grad_up)
    down_grads = finish_mlp(cotangent_all, active)

    grad_branch = gather_plane(grad_middle.astype(jnp.bfloat16))
    grad_mixed = dot(grad_branch, out_full)[:, :query_cols].astype(jnp.bfloat16)
    grad_mixed = by_seq(grad_mixed.reshape(tokens, REPEAT, HEAD_DIM))
    out_grads = finish(grad_branch, mixed_rows)[..., :query_cols].reshape(own_rows, -1)

    def attend_back(entries):
        query_seq, key_seq, value_seq, query_seg, key_seg, log_seq, grad_seq = entries
        scores = scores_of(query_seq, key_seq, query_seg, key_seg)
        probabilities = jnp.exp(scores - log_seq)
        grad_probs = jnp.einsum(
            "ird,jd->rij", grad_seq, value_seq, preferred_element_type=jnp.float32
        )
        centre = jnp.sum(probabilities * grad_probs, -1, keepdims=True)
        grad_scores = (probabilities * (grad_probs - centre)).astype(jnp.bfloat16)
        grad_values = jnp.einsum(
            "rij,ird->jd",
            probabilities.astype(jnp.bfloat16),
            grad_seq,
            preferred_element_type=jnp.float32,
        )
        grad_keys = (
            jnp.einsum("rij,ird->jd", grad_scores, query_seq, preferred_element_type=jnp.float32)
            * scaling
        )
        grad_queries = (
            jnp.einsum("rij,jd->ird", grad_scores, key_seq, preferred_element_type=jnp.float32)
            * scaling
        )
        return grad_queries, jnp.concatenate([grad_keys, grad_values], 1).astype(jnp.bfloat16)

    grad_queries, grad_key_value = lax.map(
        attend_back,
        (queries, key_all, value_all, query_segments, key_segments, log_total, grad_mixed),
    )
    grad_key_value = sum_along(by_token(grad_key_value)).astype(jnp.float32)
    grad_queries = rotate(by_token(grad_queries), cosine, -sine_table)
    grad_keys = rotate(
        grad_key_value[:, :HEAD_DIM].reshape(tokens, 1, HEAD_DIM), cosine, -sine_table
    )
    grad_qkv = jnp.concatenate(
        [
            grad_queries.reshape(tokens, query_cols),
            grad_keys.reshape(tokens, HEAD_DIM),
            grad_key_value[:, HEAD_DIM:],
            jnp.zeros((tokens, 512 - qkv_cols), jnp.float32),
        ],
        1,
    ).astype(jnp.bfloat16)
    grad_norm_one = scatter_plane(by_columns(grad_qkv, qkv_full))
    gain_one_term = jnp.sum(grad_norm_one * normed_one, 0)
    scaled_one = grad_norm_one * gain_one
    grad_input = grad_middle + inv_one * (
        scaled_one - normed_one * jnp.mean(scaled_one * normed_one, -1, keepdims=True)
    )
    head_terms = jnp.concatenate(
        [
            by_rows(normed_low, grad_qkv)[:, :qkv_cols],
            gain_one_term[:, None],
            gain_two_term[:, None],
            jnp.zeros((width, 512 - qkv_cols - 2), jnp.float32),
        ],
        1,
    ).astype(jnp.bfloat16)
    head_grads = from_plane(sum_along(head_terms)).astype(jnp.float32)
    return (
        result.reshape(seq_b, local_len, width),
        restore(grad_input).reshape(seq_b, local_len, width),
        jnp.sum(head_grads[..., qkv_cols], 1),
        head_grads[..., :query_cols].reshape(own_rows, -1),
        head_grads[..., query_cols : query_cols + HEAD_DIM].reshape(own_rows, -1),
        head_grads[..., query_cols + HEAD_DIM : qkv_cols].reshape(own_rows, -1),
        out_grads.astype(jnp.float32),
        jnp.sum(head_grads[..., qkv_cols + 1], 1),
        gate_grads,
        up_grads,
        down_grads,
    )


def solution(mesh):
    batch_n, seq_n = mesh.shape["batch"], mesh.shape["seq"]
    y_n = batch_n // 2
    lo_n = CHIPS // y_n
    hi_n = seq_n // lo_n
    fine = Mesh(mesh.devices.reshape(y_n, 2, hi_n, lo_n), EVERY)
    token = P(("y", "core"), ("hi", "lo"), None)
    vector = P(EVERY)
    matrix = P(EVERY, None)
    in_specs = (
        token, vector, matrix, matrix, matrix, matrix, vector, matrix, matrix, matrix,
        P(("y", "core"), None), token,
    )
    out_specs = (
        token, token, vector, matrix, matrix, matrix, matrix, vector, matrix, matrix, matrix,
    )

    def run(*arrays):
        return shards((y_n, hi_n, lo_n), *arrays)

    return jax.shard_map(run, mesh=fine, in_specs=in_specs, out_specs=out_specs, check_vma=False)
```

time: 4680 us -> 1440 us (0.31)
  waiting for transfers between devices: 3860 us -> 500 us
  local copies, waits for them, and re-layouts: 146 us -> 316 us
  other arithmetic: 239 us -> 115 us
  starting transfers between devices: 0.55 us -> 70.1 us
  matrix products: 373 us -> 313 us
  blocking collectives: 42.2 us -> 90.9 us
    reduce_scatter x3 -> x6, waiting for transfers between devices: 1850 us -> 190 us  [sum_along(): return lax.psum_scatter(grads, 'hi', scatter_dimension=0, tiled=True)]
    unnamed x16 -> x12, waiting for transfers between devices: 1160 us -> 0.2 us
    all_gather x9 -> x6, waiting for transfers between devices: 856 us -> 0.01 us  [along(): return lax.all_gather(weight, 'hi', axis=0, tiled=True)]
    ppermute x0 -> x56, waiting for transfers between devices: none -> 284 us  [the longest x24 284 us: swap_chip(): lax.ppermute(value, ('y', 'lo'), [(chip, chip ^ step) for chip in range(C...]
    concatenate x2 -> x5, other arithmetic: 183 us -> 4.67 us  [the longest x1 3.65 us: shards(): jnp.concatenate([by_rows(normed_low, grad_qkv)[:, :qkv_cols], gain_one_te...]
    unnamed x72 -> x208, local copies, waits for them, and re-layouts: 72 us -> 147 us
    all_gather x0 -> x1, blocking collectives: none -> 71.6 us  [shards(): small = lax.all_gather(small, EVERY, axis=0, tiled=True).astype(jnp.float32)]
    reshape x1 -> x25, local copies, waits for them, and re-layouts: 0.9 us -> 61 us  [the longest x5 21.4 us: by_token(): values = values.reshape((y_n, 2, seq_b, lead, lo_n, local_len) + last)]
  transfers between devices with their start and end apart: 14 -> 76, of which waited for: 13 -> 23; matrix products, arithmetic and copies ran while one was open for 12% -> 35% of each run, Pallas kernels for 0% -> 0%
where the time goes in v1:
time: 1440 us; the launch traced here: 1420 us
  waiting for transfers between devices  500 us (35%)
  local copies, waits for them, and re-layouts  316 us (22%)
  matrix products  313 us (22%)
  other arithmetic  115 us (8%)
  blocking collectives  90.9 us (6%)
  starting transfers between devices  70.1 us (5%)
  between operations  15.9 us (1%)
    ppermute x24, waiting for transfers between devices, swap_chip(): lax.ppermute(value, ('y', 'lo'), [(chip, chip ^ step) for chip in range(C...  284 us
    reduce_scatter x6, waiting for transfers between devices, sum_along(): return lax.psum_scatter(grads, 'hi', scatter_dimension=0, tiled=True)  190 us
    unnamed x208, local copies, waits for them, and re-layouts  147 us
    dot_general x5, matrix products, dot(): lax.dot_general(left, right, (((1,), (0,)), ((), ())), preferred_element_...  75 us
    all_gather x1, blocking collectives, shards(): small = lax.all_gather(small, EVERY, axis=0, tiled=True).astype(jnp.float32)  71.6 us
    dot_general x5, matrix products, by_rows(): lax.dot_general(left, right, (((0,), (0,)), ((), ())), preferred_element_...  66.4 us
    dot_general x5, matrix products, by_columns(): lax.dot_general(left, right, (((1,), (1,)), ((), ())), preferred_element_...  62 us
    convert_element_type x12, other arithmetic, scatter_plane(): pair = swap_chip(pair.astype(jnp.bfloat16), step).astype(jnp.float32)  30.7 us
  transfers between devices with their start and end apart: 76, of which 23 were waited for; matrix products, arithmetic and copies ran while one was open for 35% of the time, Pallas kernels for 0%

profile of v1, /device:TPU:0, one launch (start us, length us, event | category | flops | bytes accessed | tf_op | source)
XLA Modules:
  0.0 1422.4 jit_solution(13511132703825426225)
XLA Ops:
  16.0 5.2 all-to-all-start
  25.8 71.6 %all-gather.1 = bf16[32,1,512]{2,1,0:T(2,128)(2,1)S(1)} all-gather(bf16[1,1,512]{2,1,0:T(2,128)(2,1)S(1)} %reshape.534), channel_id=2, replica_groups=mesh['y'=2,'core'=2,'hi'=4,'lo'=2] {'y','core','hi','lo'}, dimensions={0}, use_global_device_ids=true | all-gather | bytes 33792 | tf_op jit(solution)/shard_map/all_gather | solution.py:155
  110.9 26.5 %collective-permute-done.1 = bf16[256,2560]{0,1:T(8,128)(2,1)} collective-permute-done((bf16[256,2560]{0,1:T(8,128)(2,1)}, bf16[256,2560]{0,1:T(8,128)(2,1)}, u32[]{:S(2)}, u32[]{:S(2)}) %collective-permute-start.1) | collective-permute-done | bytes 1310752 | tf_op jit(solution)/shard_map/ppermute | solution.py:47
  140.3 19.0 %collective-permute-done.5 = bf16[256,2560]{0,1:T(8,128)(2,1)} collective-permute-done((bf16[256,2560]{0,1:T(8,128)(2,1)}, bf16[256,2560]{0,1:T(8,128)(2,1)}, u32[]{:S(2)}, u32[]{:S(2)}) %collective-permute-start.5) | collective-permute-done | bytes 1310752 | tf_op jit(solution)/shard_map/ppermute | solution.py:47
  175.8 9.2 fusion.123
  191.8 19.3 %all_to_all.45 = bf16[8,80,896]{2,1,0:T(8,128)(2,1)} all-to-all(bf16[8,80,896]{2,1,0:T(8,128)(2,1)S(1)} %copy.193), channel_id=1, replica_groups=mesh['y'=2,'core'=2,'hi'=4,'lo'=2] {'y','core','lo'}, dimensions={0} | all-to-all | bytes 2293760 | tf_op jit(solution)/shard_map/all_to_all | solution.py:73
  213.8 4.2 all-to-all-start.1
  220.4 13.6 all-to-all-done.1
  249.4 4.3 reshape.467
  253.7 5.5 reshape.461
  259.2 5.3 copy.177
  264.4 5.5 reshape.462
  273.4 54.5 %while.26 = (s32[]{:T(128)}, bf16[8,256,4,80]{1,3,2,0:T(8,128)(2,1)}, f32[8,4,256,1]{2,1,3,0:T(4,128)}, bf16[8,1024,80]{1,2,0:T(8,128)(2,1)}, f32[8,256]{1,0:T(8...) while((s32[]{:T(128)}, ...), condition=%wide.region_4.5_spmd.clone, body=%wide.region_1.4_spmd.clone.sunk | while | flops 348996096 | bytes 14356653 | solution.py:266
  331.8 4.4 copy.295
  336.3 4.3 reshape_reshape.23
  340.6 7.5 convolution_convert_fusion.2
  348.1 4.0 fusion.119
  357.6 4.3 copy.204
  361.8 4.4 reshape_reshape.26
  373.7 4.2 all-to-all-start.3
  402.8 26.1 %collective-permute-done.31 = bf16[256,2560]{0,1:T(8,128)(2,1)} collective-permute-done((bf16[256,2560]{0,1:T(8,128)(2,1)}, bf16[256,2560]{0,1:T(8,128)(2,1)}, u32[]{:S(2)}, u32[]{:S(2)}) %collective-permute-start.31) | collective-permute-done | bytes 1310752 | tf_op jit(solution)/shard_map/ppermute | solution.py:47
  433.2 9.0 all-to-all-done.3
  447.7 22.5 %collective-permute-done.8 = bf16[256,2560]{0,1:T(8,128)(2,1)} collective-permute-done((bf16[256,2560]{0,1:T(8,128)(2,1)}, bf16[256,2560]{0,1:T(8,128)(2,1)}, u32[]{:S(2)}, u32[]{:S(2)}) %collective-permute-start.8) | collective-permute-done | bytes 1310752 | tf_op jit(solution)/shard_map/ppermute | solution.py:47
  470.2 26.9 %collective-permute-done.10 = bf16[256,2560]{0,1:T(8,128)(2,1)} collective-permute-done((bf16[256,2560]{0,1:T(8,128)(2,1)}, bf16[256,2560]{0,1:T(8,128)(2,1)}, u32[]{:S(2)}, u32[]{:S(2)}) %collective-permute-start.10) | collective-permute-done | bytes 1310752 | tf_op jit(solution)/shard_map/ppermute | solution.py:47
  497.2 3.9 multiply_reduce_fusion.4
  514.0 20.7 %collective-permute-done.15 = bf16[256,2560]{0,1:T(8,128)(2,1)S(1)} collective-permute-done((bf16[256,2560]{0,1:T(8,128)(2,1)S(1)}, bf16[256,2560]{0,1:T(8,128)(2,1)S(1)}, u32[]{:S(2)}, u32[]{:S(2)}) %collective-permute-start.15) | collective-permute-done | bytes 1310752 | tf_op jit(solution)/shard_map/ppermute | solution.py:47
  538.5 24.2 %collective-permute-done.19 = bf16[256,2560]{0,1:T(8,128)(2,1)S(1)} collective-permute-done((bf16[256,2560]{0,1:T(8,128)(2,1)S(1)}, bf16[256,2560]{0,1:T(8,128)(2,1)S(1)}, u32[]{:S(2)}, u32[]{:S(2)}) %collective-permute-start.19) | collective-permute-done | bytes 1310752 | tf_op jit(solution)/shard_map/ppermute | solution.py:47
  562.7 5.1 collective-permute-done.17
  576.4 17.0 %fusion.125 = f32[2048,896]{1,0:T(8,128)} fusion(bf16[2048,2560]{0,1:T(8,128)(2,1)} %constant_dynamic-update-slice_fusion.8, bf16[2560,896]{1,0:T(8,128)(2,1)} %all-gather.17.cloned.1.call-done), kind=kOutput, calls=%fused_computation.262 | convolution fusion | flops 9395240960 | bytes 22413312 | tf_op jit(solution)/shard_map/dot_general | solution.py:25
  593.4 17.5 %fusion.124 = f32[2048,896]{1,0:T(8,128)} fusion(bf16[2048,2560]{0,1:T(8,128)(2,1)} %constant_dynamic-update-slice_fusion.8, bf16[2560,896]{1,0:T(8,128)(2,1)} %all-gather.15.cloned.1.call-done), kind=kOutput, calls=%fused_computation.261 | convolution fusion | flops 9395240960 | bytes 22413312 | tf_op jit(solution)/shard_map/dot_general | solution.py:25
  610.8 23.6 %multiply_convert_fusion = (bf16[2048,896]{1,0:T(8,128)(2,1)}, bf16[2048,896]{1,0:T(8,128)(2,1)S(1)}, bf16[2048,896]{1,0:T(8,128)(2,1)}) fusion(f32[2048,896]{1,0:T(8,128)} %fusion.124, f32[2048,896]{1,0:T(8,128)} %fusion.125, bf16[2048,2560]{0,1:T(8,128)(2,1)} %constant_dynamic-update-slice_fusion.16, bf16[2560,896]{1,0:T(8,128)(2,1)} %all-gather.19.cloned.1.call-done), kind=kOutput, calls=%fused_computation.85 | convolution fusion | flops 9422766080 | bytes 40763392 | tf_op jit(solution)/shard_map/dot_general | solution.py:25
  634.5 14.1 fusion.126
  648.6 19.5 %add_convert_fusion = bf16[2048,2560]{1,0:T(8,128)(2,1)} fusion(f32[2048,2560]{1,0:T(8,128)} %fusion.126, bf16[2048,896]{1,0:T(8,128)(2,1)} %get-tuple-element.298, bf16[2560,896]{1,0:T(8,128)(2,1)} %all-gather.17.cloned.1.call-done), kind=kOutput, calls=%fused_computation.81 | convolution fusion | flops 9405726720 | bytes 39714816 | tf_op jit(solution)/shard_map/dot_general | solution.py:31
  668.1 7.3 fusion.117
  704.4 22.6 %collective-permute-done.36 = bf16[256,2560]{0,1:T(8,128)(2,1)} collective-permute-done((bf16[256,2560]{0,1:T(8,128)(2,1)}, bf16[256,2560]{0,1:T(8,128)(2,1)}, u32[]{:S(2)}, u32[]{:S(2)}) %collective-permute-start.36) | collective-permute-done | bytes 1310752 | tf_op jit(solution)/shard_map/ppermute | solution.py:47
  727.0 27.7 %collective-permute-done.38 = bf16[256,2560]{0,1:T(8,128)(2,1)} collective-permute-done((bf16[256,2560]{0,1:T(8,128)(2,1)}, bf16[256,2560]{0,1:T(8,128)(2,1)}, u32[]{:S(2)}, u32[]{:S(2)}) %collective-permute-start.38) | collective-permute-done | bytes 1310752 | tf_op jit(solution)/shard_map/ppermute | solution.py:47
  754.7 4.6 multiply_reduce_fusion
  766.7 28.5 %collective-permute-done.43 = bf16[256,2560]{0,1:T(8,128)(2,1)} collective-permute-done((bf16[256,2560]{0,1:T(8,128)(2,1)}, bf16[256,2560]{0,1:T(8,128)(2,1)}, u32[]{:S(2)}, u32[]{:S(2)}) %collective-permute-start.43) | collective-permute-done | bytes 1310752 | tf_op jit(solution)/shard_map/ppermute | solution.py:47
  795.2 27.2 %collective-permute-done.47 = bf16[256,2560]{0,1:T(8,128)(2,1)S(1)} collective-permute-done((bf16[256,2560]{0,1:T(8,128)(2,1)}, bf16[256,2560]{0,1:T(8,128)(2,1)S(1)}, u32[]{:S(2)}, u32[]{:S(2)}) %collective-permute-start.47) | collective-permute-done | bytes 1310752 | tf_op jit(solution)/shard_map/ppermute | solution.py:47
  836.4 7.7 fusion.127
  847.3 109.2 %while.27 = (s32[]{:T(128)}, f32[8,256,4,80]{1,3,2,0:T(8,128)}, bf16[8,1024,160]{1,2,0:T(8,128)(2,1)}, bf16[8,1024,80]{1,2,0:T(8,128)(2,1)}, f32[8,256]{1,0:T(8,...) while((s32[]{:T(128)}, f32[8,256,4,80]{1,3,2,0:T(8,128)}, ...), condition=%wide.region_9.10_spmd.clone, body=%wide.region_7.9_spmd.clone.sunk | while | flops 856359424 | bytes 35030216 | solution.py:334
  956.5 4.4 reshape.484
  960.9 5.6 copy.294
  966.5 5.5 reshape.485
  973.4 9.3 convolution_convert_fusion.6
  982.7 16.3 %convolution_convert_fusion.3 = bf16[2560,896]{1,0:T(8,128)(2,1)} fusion(bf16[2048,2560]{0,1:T(8,128)(2,1)} %constant_dynamic-update-slice_fusion.16, bf16[2048,896]{1,0:T(8,128)(2,1)} %get-tuple-element.300), kind=kOutput, calls=%fused_computation.90 | convolution fusion | flops 9397534720 | bytes 18743296 | tf_op jit(solution)/shard_map/dot_general | solution.py:37
  999.1 16.2 %convolution_convert_fusion.4 = bf16[2560,896]{1,0:T(8,128)(2,1)} fusion(bf16[2048,2560]{0,1:T(8,128)(2,1)} %constant_dynamic-update-slice_fusion.8, bf16[2048,896]{1,0:T(8,128)(2,1)} %get-tuple-element.298), kind=kOutput, calls=%fused_computation.91 | convolution fusion | flops 9397534720 | bytes 18743296 | tf_op jit(solution)/shard_map/dot_general | solution.py:37
  1016.4 14.4 %convolution_convert_fusion.1 = bf16[2048,2560]{1,0:T(8,128)(2,1)S(1)} fusion(bf16[2048,896]{1,0:T(8,128)(2,1)} %get-tuple-element.300, bf16[2560,896]{1,0:T(8,128)(2,1)} %all-gather.19.cloned.1.call-done), kind=kOutput, calls=%fused_computation.83 | convolution fusion | flops 9400483840 | bytes 18743296 | tf_op jit(solution)/shard_map/dot_general | solution.py:31
  1036.5 16.2 %convolution_convert_fusion.5 = bf16[2560,896]{1,0:T(8,128)(2,1)} fusion(bf16[2048,2560]{0,1:T(8,128)(2,1)} %constant_dynamic-update-slice_fusion.8, bf16[2048,896]{1,0:T(8,128)(2,1)} %copy-done.69), kind=kOutput, calls=%fused_computation.92 | convolution fusion | flops 9397534720 | bytes 18743296 | tf_op jit(solution)/shard_map/dot_general | solution.py:37
  1066.1 6.4 convolution_convert_fusion
  1118.3 33.6 %reduce-scatter.17.cloned.1.call-done = bf16[640,896]{1,0:T(8,128)(2,1)} async-done(((bf16[2560,896]{1,0:T(8,128)(2,1)}), bf16[640,896]{1,0:T(8,128)(2,1)}) %reduce-scatter.17.cloned.1.call-update) | async-done | bytes 1146896 | tf_op jit(solution)/shard_map/reduce_scatter | solution.py:87
  1151.9 4.5 all-to-all-start.8
  1156.4 8.4 fusion.111
  1173.4 4.9 multiply_reduce_fusion.1
  1178.3 59.5 %reduce-scatter.15.cloned.1.call-done = bf16[640,896]{1,0:T(8,128)(2,1)} async-done(((bf16[2560,896]{1,0:T(8,128)(2,1)}), bf16[640,896]{1,0:T(8,128)(2,1)}) %reduce-scatter.15.cloned.1.call-update) | async-done | bytes 1146896 | tf_op jit(solution)/shard_map/reduce_scatter | solution.py:87
  1237.8 4.3 all-to-all-start.7
  1245.7 4.6 copy.243
  1255.4 68.4 %reduce-scatter.13.cloned.1.call-done = bf16[640,896]{1,0:T(8,128)(2,1)} async-done(((bf16[2560,896]{1,0:T(8,128)(2,1)}), bf16[640,896]{1,0:T(8,128)(2,1)}) %reduce-scatter.13.cloned.1.call-update) | async-done | bytes 1146896 | tf_op jit(solution)/shard_map/reduce_scatter | solution.py:87
  1323.8 4.3 all-to-all-start.6
  1349.9 28.7 %reduce-scatter.19.cloned.1.call-done = bf16[640,512]{1,0:T(8,128)(2,1)} async-done(((bf16[2560,512]{1,0:T(8,128)(2,1)}), bf16[640,512]{1,0:T(8,128)(2,1)}) %reduce-scatter.19.cloned.1.call-update) | async-done | bytes 655376 | tf_op jit(solution)/shard_map/reduce_scatter | solution.py:87
  1382.6 8.4 multiply_add_fusion
  1391.0 4.5 copy.241
  1395.6 5.3 reshape.546
  1404.3 6.1 reshape.547
  (671 shorter events, 488.0 us)
Async XLA Ops:
  16.0 92.9 %all-to-all-start = ((bf16[8,80,896]{2,1,0:T(8,128)(2,1)}), bf16[8,80,896]{2,1,0:T(8,128)(2,1)}, u32[]{:S(2)}, u32[]{:S(2)}) async-start(bf16[8,80,896]{2,1,0:T(8,128)(2,1)} %copy.176), calls=%async_computation | async-start | bytes 2293760 | tf_op jit(solution)/shard_map/all_to_all | solution.py:73
  21.1 154.7 %all-gather.9.cloned.1.call-start = ((), (), s32[]{:S(2)}) async-start(), calls=%async_computation.15 | async-start | bytes 3276800 | tf_op jit(solution)/shard_map/all_gather | solution.py:83
  105.4 32.0 %collective-permute-start.1 = (bf16[256,2560]{0,1:T(8,128)(2,1)}, bf16[256,2560]{0,1:T(8,128)(2,1)}, u32[]{:S(2)}, u32[]{:S(2)}) collective-permute-start(bf16[256,2560]{0,1:T(8,128)(2,1)} %get-tuple-element.362), channel_id=1, source_target_pairs={{0,1},{1,0},{16,17},{17,16},{2,3},{3,2},{18,19},{19,18},{4,5},{5,4... | collective-permute-start | bytes 3932168 | tf_op jit(solution)/shard_map/ppermute | solution.py:47
  105.4 53.9 %collective-permute-start.5 = (bf16[256,2560]{0,1:T(8,128)(2,1)}, bf16[256,2560]{0,1:T(8,128)(2,1)}, u32[]{:S(2)}, u32[]{:S(2)}) collective-permute-start(bf16[256,2560]{0,1:T(8,128)(2,1)} %get-tuple-element.362), channel_id=1, source_target_pairs={{0,17},{1,16},{16,1},{17,0},{2,19},{3,18},{18,3},{19,2},{4,21},{5,... | collective-permute-start | bytes 3932168 | tf_op jit(solution)/shard_map/ppermute | solution.py:47
  107.4 53.2 %collective-permute-start.3 = (bf16[256,2560]{0,1:T(8,128)(2,1)}, bf16[256,2560]{0,1:T(8,128)(2,1)}, u32[]{:S(2)}, u32[]{:S(2)}) collective-permute-start(bf16[256,2560]{0,1:T(8,128)(2,1)} %get-tuple-element.362), channel_id=1, source_target_pairs={{0,16},{1,17},{16,0},{17,1},{2,18},{3,19},{18,2},{19,3},{4,20},{5,... | collective-permute-start | bytes 3932168 | tf_op jit(solution)/shard_map/ppermute | solution.py:47
  108.8 51.8 %collective-permute-start = (bf16[256,2560]{0,1:T(8,128)(2,1)}, bf16[256,2560]{0,1:T(8,128)(2,1)}, u32[]{:S(2)}, u32[]{:S(2)}) collective-permute-start(bf16[256,2560]{0,1:T(8,128)(2,1)} %get-tuple-element.362), channel_id=1, source_target_pairs={{0,8},{8,0},{1,9},{9,1},{2,10},{10,2},{3,11},{11,3},{4,12},{12,4},... | collective-permute-start | bytes 3932168 | tf_op jit(solution)/shard_map/ppermute | solution.py:43
  110.8 142.9 %all-gather.11.cloned.1.call-start = ((), (), s32[]{:S(2)}) async-start(), calls=%async_computation.16 | async-start | bytes 3276800 | tf_op jit(solution)/shard_map/all_gather | solution.py:83
  137.4 28.4 %collective-permute-start.2 = (bf16[256,2560]{0,1:T(8,128)(2,1)}, bf16[256,2560]{0,1:T(8,128)(2,1)}, u32[]{:S(2)}, u32[]{:S(2)}) collective-permute-start(bf16[256,2560]{0,1:T(8,128)(2,1)} %collective-permute-done.1), channel_id=1, source_target_pairs={{0,8},{8,0},{1,9},{9,1},{2,10},{10,2},{3,11},{11,3},{4,12},{12,4},... | collective-permute-start | bytes 3932168 | tf_op jit(solution)/shard_map/ppermute | solution.py:43
  188.1 152.4 %all-gather.13.cloned.1.call-start = ((), (), s32[]{:S(2)}) async-start(), calls=%async_computation.17 | async-start | bytes 2457600 | tf_op jit(solution)/shard_map/all_gather | solution.py:83
  190.1 386.3 %all-gather.17.cloned.1.call-start = ((), (), s32[]{:S(2)}) async-start(), calls=%async_computation.19 | async-start | bytes 5734400 | tf_op jit(solution)/shard_map/all_gather | solution.py:83
  213.8 20.2 %all-to-all-start.1 = ((bf16[8,80,896]{2,1,0:T(8,128)(2,1)}), bf16[8,80,896]{2,1,0:T(8,128)(2,1)}, u32[]{:S(2)}, u32[]{:S(2)}) async-start(bf16[8,80,896]{2,1,0:T(8,128)(2,1)} %copy.192), calls=%async_computation.1 | async-start | bytes 2293760 | tf_op jit(solution)/shard_map/all_to_all | solution.py:73
  218.0 375.3 %all-gather.15.cloned.1.call-start = ((), (), s32[]{:S(2)}) async-start(), calls=%async_computation.18 | async-start | bytes 5734400 | tf_op jit(solution)/shard_map/all_gather | solution.py:83
  354.6 35.8 %collective-permute-start.7 = (bf16[256,2560]{0,1:T(8,128)(2,1)}, bf16[256,2560]{0,1:T(8,128)(2,1)}, u32[]{:S(2)}, u32[]{:S(2)}) collective-permute-start(bf16[256,2560]{0,1:T(8,128)(2,1)} %bitcast.489), channel_id=1, source_target_pairs={{0,8},{8,0},{1,9},{9,1},{2,10},{10,2},{3,11},{11,3},{4,12},{12,4},... | collective-permute-start | bytes 3932168 | tf_op jit(solution)/shard_map/ppermute | solution.py:43
  357.1 36.8 %collective-permute-start.9 = (bf16[256,2560]{0,1:T(8,128)(2,1)}, bf16[256,2560]{0,1:T(8,128)(2,1)}, u32[]{:S(2)}, u32[]{:S(2)}) collective-permute-start(bf16[256,2560]{0,1:T(8,128)(2,1)} %bitcast.487), channel_id=1, source_target_pairs={{0,8},{8,0},{1,9},{9,1},{2,10},{10,2},{3,11},{11,3},{4,12},{12,4},... | collective-permute-start | bytes 3932168 | tf_op jit(solution)/shard_map/ppermute | solution.py:43
  368.8 32.9 %collective-permute-start.33 = (bf16[256,2560]{0,1:T(8,128)(2,1)}, bf16[256,2560]{0,1:T(8,128)(2,1)}, u32[]{:S(2)}, u32[]{:S(2)}) collective-permute-start(bf16[256,2560]{0,1:T(8,128)(2,1)} %bitcast.44), channel_id=1, source_target_pairs={{0,17},{1,16},{16,1},{17,0},{2,19},{3,18},{18,3},{19,2},{4,21},{5,... | collective-permute-start | bytes 3932168 | tf_op jit(solution)/shard_map/ppermute | solution.py:47
  369.9 59.0 %collective-permute-start.31 = (bf16[256,2560]{0,1:T(8,128)(2,1)}, bf16[256,2560]{0,1:T(8,128)(2,1)}, u32[]{:S(2)}, u32[]{:S(2)}) collective-permute-start(bf16[256,2560]{0,1:T(8,128)(2,1)} %bitcast.44), channel_id=1, source_target_pairs={{0,16},{1,17},{16,0},{17,1},{2,18},{3,19},{18,2},{19,3},{4,20},{5,... | collective-permute-start | bytes 3932168 | tf_op jit(solution)/shard_map/ppermute | solution.py:47
  371.3 75.9 %collective-permute-start.29 = (bf16[256,2560]{0,1:T(8,128)(2,1)}, bf16[256,2560]{0,1:T(8,128)(2,1)}, u32[]{:S(2)}, u32[]{:S(2)}) collective-permute-start(bf16[256,2560]{0,1:T(8,128)(2,1)} %bitcast.44), channel_id=1, source_target_pairs={{0,1},{1,0},{16,17},{17,16},{2,3},{3,2},{18,19},{19,18},{4,5},{5,4... | collective-permute-start | bytes 3932168 | tf_op jit(solution)/shard_map/ppermute | solution.py:47
  373.7 68.4 %all-to-all-start.3 = ((bf16[8,80,896]{2,1,0:T(8,128)(2,1)}), bf16[8,80,896]{2,1,0:T(8,128)(2,1)}, u32[]{:S(2)}, u32[]{:S(2)}) async-start(bf16[8,80,896]{2,1,0:T(8,128)(2,1)} %copy.194), calls=%async_computation.3 | async-start | bytes 2293760 | tf_op jit(solution)/shard_map/all_to_all | solution.py:73
  378.0 232.8 %all-gather.19.cloned.1.call-start = ((), (), s32[]{:S(2)}) async-start(), calls=%async_computation.20 | async-start | bytes 5734400 | tf_op jit(solution)/shard_map/all_gather | solution.py:83
  393.9 36.2 %collective-permute-start.28 = (bf16[256,2560]{0,1:T(8,128)(2,1)}, bf16[256,2560]{0,1:T(8,128)(2,1)}, u32[]{:S(2)}, u32[]{:S(2)}) collective-permute-start(bf16[256,2560]{0,1:T(8,128)(2,1)} %bitcast.44), channel_id=1, source_target_pairs={{0,8},{8,0},{1,9},{9,1},{2,10},{10,2},{3,11},{11,3},{4,12},{12,4},... | collective-permute-start | bytes 3932168 | tf_op jit(solution)/shard_map/ppermute | solution.py:43
  397.1 50.1 %collective-permute-start.13 = (bf16[256,2560]{0,1:T(8,128)(2,1)}, bf16[256,2560]{0,1:T(8,128)(2,1)}, u32[]{:S(2)}, u32[]{:S(2)}) collective-permute-start(bf16[256,2560]{0,1:T(8,128)(2,1)} %bitcast.24), channel_id=1, source_target_pairs={{0,8},{8,0},{1,9},{9,1},{2,10},{10,2},{3,11},{11,3},{4,12},{12,4},... | collective-permute-start | bytes 3932168 | tf_op jit(solution)/shard_map/ppermute | solution.py:43
  401.7 68.5 %collective-permute-start.8 = (bf16[256,2560]{0,1:T(8,128)(2,1)}, bf16[256,2560]{0,1:T(8,128)(2,1)}, u32[]{:S(2)}, u32[]{:S(2)}) collective-permute-start(bf16[256,2560]{0,1:T(8,128)(2,1)} %fusion.90), channel_id=1, source_target_pairs={{0,17},{1,16},{16,1},{17,0},{2,19},{3,18},{18,3},{19,2},{4,21},{5,... | collective-permute-start | bytes 3932168 | tf_op jit(solution)/shard_map/ppermute | solution.py:47
  428.9 68.3 %collective-permute-start.10 = (bf16[256,2560]{0,1:T(8,128)(2,1)}, bf16[256,2560]{0,1:T(8,128)(2,1)}, u32[]{:S(2)}, u32[]{:S(2)}) collective-permute-start(bf16[256,2560]{0,1:T(8,128)(2,1)} %fusion.89), channel_id=1, source_target_pairs={{0,16},{1,17},{16,0},{17,1},{2,18},{3,19},{18,2},{19,3},{4,20},{5,... | collective-permute-start | bytes 3932168 | tf_op jit(solution)/shard_map/ppermute | solution.py:47
  430.1 67.0 %collective-permute-start.12 = (bf16[256,2560]{0,1:T(8,128)(2,1)}, bf16[256,2560]{0,1:T(8,128)(2,1)}, u32[]{:S(2)}, u32[]{:S(2)}) collective-permute-start(bf16[256,2560]{0,1:T(8,128)(2,1)} %fusion.88), channel_id=1, source_target_pairs={{0,1},{1,0},{16,17},{17,16},{2,3},{3,2},{18,19},{19,18},{4,5},{5,4... | collective-permute-start | bytes 3932168 | tf_op jit(solution)/shard_map/ppermute | solution.py:47
  442.2 621.4 %reduce-scatter.9.cloned.1.call-start = ((), (), s32[]{:S(2)}) async-start(), calls=%async_computation.21 | async-start | bytes 3276800 | tf_op jit(solution)/shard_map/reduce_scatter | solution.py:87
  447.2 90.1 %collective-permute-start.34 = (bf16[256,2560]{0,1:T(8,128)(2,1)}, bf16[256,2560]{0,1:T(8,128)(2,1)S(1)}, u32[]{:S(2)}, u32[]{:S(2)}) collective-permute-start(bf16[256,2560]{0,1:T(8,128)(2,1)} %collective-permute-done.33), channel_id=1, source_target_pairs={{0,8},{8,0},{1,9},{9,1},{2,10},{10,2},{3,11},{11,3},{4,12},{12,4},... | collective-permute-start | bytes 3932168 | tf_op jit(solution)/shard_map/ppermute | solution.py:43
  447.2 63.1 %collective-permute-start.32 = (bf16[256,2560]{0,1:T(8,128)(2,1)}, bf16[256,2560]{0,1:T(8,128)(2,1)S(1)}, u32[]{:S(2)}, u32[]{:S(2)}) collective-permute-start(bf16[256,2560]{0,1:T(8,128)(2,1)} %collective-permute-done.31), channel_id=1, source_target_pairs={{0,8},{8,0},{1,9},{9,1},{2,10},{10,2},{3,11},{11,3},{4,12},{12,4},... | collective-permute-start | bytes 3932168 | tf_op jit(solution)/shard_map/ppermute | solution.py:43
  470.2 36.5 %collective-permute-start.30 = (bf16[256,2560]{0,1:T(8,128)(2,1)}, bf16[256,2560]{0,1:T(8,128)(2,1)S(1)}, u32[]{:S(2)}, u32[]{:S(2)}) collective-permute-start(bf16[256,2560]{0,1:T(8,128)(2,1)} %collective-permute-done.29), channel_id=1, source_target_pairs={{0,8},{8,0},{1,9},{9,1},{2,10},{10,2},{3,11},{11,3},{4,12},{12,4},... | collective-permute-start | bytes 3932168 | tf_op jit(solution)/shard_map/ppermute | solution.py:43
  503.1 31.7 %collective-permute-start.15 = (bf16[256,2560]{0,1:T(8,128)(2,1)S(1)}, bf16[256,2560]{0,1:T(8,128)(2,1)S(1)}, u32[]{:S(2)}, u32[]{:S(2)}) collective-permute-start(bf16[256,2560]{0,1:T(8,128)(2,1)S(1)} %get-tuple-element.291), channel_id=1, source_target_pairs={{0,1},{1,0},{16,17},{17,16},{2,3},{3,2},{18,19},{19,18},{4,5},{5,4... | collective-permute-start | bytes 3932168 | tf_op jit(solution)/shard_map/ppermute | solution.py:47
  507.9 54.9 %collective-permute-start.19 = (bf16[256,2560]{0,1:T(8,128)(2,1)S(1)}, bf16[256,2560]{0,1:T(8,128)(2,1)S(1)}, u32[]{:S(2)}, u32[]{:S(2)}) collective-permute-start(bf16[256,2560]{0,1:T(8,128)(2,1)S(1)} %get-tuple-element.291), channel_id=1, source_target_pairs={{0,17},{1,16},{16,1},{17,0},{2,19},{3,18},{18,3},{19,2},{4,21},{5,... | collective-permute-start | bytes 3932168 | tf_op jit(solution)/shard_map/ppermute | solution.py:47
  509.5 58.2 %collective-permute-start.17 = (bf16[256,2560]{0,1:T(8,128)(2,1)S(1)}, bf16[256,2560]{0,1:T(8,128)(2,1)S(1)}, u32[]{:S(2)}, u32[]{:S(2)}) collective-permute-start(bf16[256,2560]{0,1:T(8,128)(2,1)S(1)} %get-tuple-element.291), channel_id=1, source_target_pairs={{0,16},{1,17},{16,0},{17,1},{2,18},{3,19},{18,2},{19,3},{4,20},{5,... | collective-permute-start | bytes 3932168 | tf_op jit(solution)/shard_map/ppermute | solution.py:47
  510.2 57.5 %collective-permute-start.14 = (bf16[256,2560]{0,1:T(8,128)(2,1)S(1)}, bf16[256,2560]{0,1:T(8,128)(2,1)S(1)}, u32[]{:S(2)}, u32[]{:S(2)}) collective-permute-start(bf16[256,2560]{0,1:T(8,128)(2,1)S(1)} %get-tuple-element.291), channel_id=1, source_target_pairs={{0,8},{8,0},{1,9},{9,1},{2,10},{10,2},{3,11},{11,3},{4,12},{12,4},... | collective-permute-start | bytes 3932168 | tf_op jit(solution)/shard_map/ppermute | solution.py:43
  534.7 35.6 %collective-permute-start.16 = (bf16[256,2560]{0,1:T(8,128)(2,1)S(1)}, bf16[256,2560]{0,1:T(8,128)(2,1)S(1)}, u32[]{:S(2)}, u32[]{:S(2)}) collective-permute-start(bf16[256,2560]{0,1:T(8,128)(2,1)S(1)} %collective-permute-done.15), channel_id=1, source_target_pairs={{0,8},{8,0},{1,9},{9,1},{2,10},{10,2},{3,11},{11,3},{4,12},{12,4},... | collective-permute-start | bytes 3932168 | tf_op jit(solution)/shard_map/ppermute | solution.py:43
  694.2 32.8 %collective-permute-start.36 = (bf16[256,2560]{0,1:T(8,128)(2,1)}, bf16[256,2560]{0,1:T(8,128)(2,1)}, u32[]{:S(2)}, u32[]{:S(2)}) collective-permute-start(bf16[256,2560]{0,1:T(8,128)(2,1)} %fusion.79), channel_id=1, source_target_pairs={{0,17},{1,16},{16,1},{17,0},{2,19},{3,18},{18,3},{19,2},{4,21},{5,... | collective-permute-start | bytes 3932168 | tf_op jit(solution)/shard_map/ppermute | solution.py:47
  698.2 56.4 %collective-permute-start.38 = (bf16[256,2560]{0,1:T(8,128)(2,1)}, bf16[256,2560]{0,1:T(8,128)(2,1)}, u32[]{:S(2)}, u32[]{:S(2)}) collective-permute-start(bf16[256,2560]{0,1:T(8,128)(2,1)} %fusion.78), channel_id=1, source_target_pairs={{0,16},{1,17},{16,0},{17,1},{2,18},{3,19},{18,2},{19,3},{4,20},{5,... | collective-permute-start | bytes 3932168 | tf_op jit(solution)/shard_map/ppermute | solution.py:47
  700.3 54.3 %collective-permute-start.40 = (bf16[256,2560]{0,1:T(8,128)(2,1)}, bf16[256,2560]{0,1:T(8,128)(2,1)}, u32[]{:S(2)}, u32[]{:S(2)}) collective-permute-start(bf16[256,2560]{0,1:T(8,128)(2,1)} %fusion.77), channel_id=1, source_target_pairs={{0,1},{1,0},{16,17},{17,16},{2,3},{3,2},{18,19},{19,18},{4,5},{5,4... | collective-permute-start | bytes 3932168 | tf_op jit(solution)/shard_map/ppermute | solution.py:47
  763.2 32.0 %collective-permute-start.43 = (bf16[256,2560]{0,1:T(8,128)(2,1)}, bf16[256,2560]{0,1:T(8,128)(2,1)}, u32[]{:S(2)}, u32[]{:S(2)}) collective-permute-start(bf16[256,2560]{0,1:T(8,128)(2,1)} %get-tuple-element.364), channel_id=1, source_target_pairs={{0,1},{1,0},{16,17},{17,16},{2,3},{3,2},{18,19},{19,18},{4,5},{5,4... | collective-permute-start | bytes 3932168 | tf_op jit(solution)/shard_map/ppermute | solution.py:47
  763.6 58.8 %collective-permute-start.47 = (bf16[256,2560]{0,1:T(8,128)(2,1)}, bf16[256,2560]{0,1:T(8,128)(2,1)S(1)}, u32[]{:S(2)}, u32[]{:S(2)}) collective-permute-start(bf16[256,2560]{0,1:T(8,128)(2,1)} %get-tuple-element.364), channel_id=1, source_target_pairs={{0,17},{1,16},{16,1},{17,0},{2,19},{3,18},{18,3},{19,2},{4,21},{5,... | collective-permute-start | bytes 3932168 | tf_op jit(solution)/shard_map/ppermute | solution.py:47
  765.3 58.4 %collective-permute-start.45 = (bf16[256,2560]{0,1:T(8,128)(2,1)}, bf16[256,2560]{0,1:T(8,128)(2,1)S(1)}, u32[]{:S(2)}, u32[]{:S(2)}) collective-permute-start(bf16[256,2560]{0,1:T(8,128)(2,1)} %get-tuple-element.364), channel_id=1, source_target_pairs={{0,16},{1,17},{16,0},{17,1},{2,18},{3,19},{18,2},{19,3},{4,20},{5,... | collective-permute-start | bytes 3932168 | tf_op jit(solution)/shard_map/ppermute | solution.py:47
  766.7 57.0 %collective-permute-start.42 = (bf16[256,2560]{0,1:T(8,128)(2,1)}, bf16[256,2560]{0,1:T(8,128)(2,1)}, u32[]{:S(2)}, u32[]{:S(2)}) collective-permute-start(bf16[256,2560]{0,1:T(8,128)(2,1)} %get-tuple-element.364), channel_id=1, source_target_pairs={{0,8},{8,0},{1,9},{9,1},{2,10},{10,2},{3,11},{11,3},{4,12},{12,4},... | collective-permute-start | bytes 3932168 | tf_op jit(solution)/shard_map/ppermute | solution.py:43
  795.2 33.7 %collective-permute-start.44 = (bf16[256,2560]{0,1:T(8,128)(2,1)}, bf16[256,2560]{0,1:T(8,128)(2,1)}, u32[]{:S(2)}, u32[]{:S(2)}) collective-permute-start(bf16[256,2560]{0,1:T(8,128)(2,1)} %collective-permute-done.43), channel_id=1, source_target_pairs={{0,8},{8,0},{1,9},{9,1},{2,10},{10,2},{3,11},{11,3},{4,12},{12,4},... | collective-permute-start | bytes 3932168 | tf_op jit(solution)/shard_map/ppermute | solution.py:43
  972.1 123.0 %reduce-scatter.11.cloned.1.call-start = ((), (), s32[]{:S(2)}) async-start(), calls=%async_computation.22 | async-start | bytes 2457600 | tf_op jit(solution)/shard_map/reduce_scatter | solution.py:87
  982.7 169.2 %reduce-scatter.17.cloned.1.call-start = ((), (), s32[]{:S(2)}) async-start(), calls=%async_computation.25 | async-start | bytes 5734400 | tf_op jit(solution)/shard_map/reduce_scatter | solution.py:87
  999.0 238.7 %reduce-scatter.15.cloned.1.call-start = ((), (), s32[]{:S(2)}) async-start(), calls=%async_computation.24 | async-start | bytes 5734400 | tf_op jit(solution)/shard_map/reduce_scatter | solution.py:87
  1015.4 308.4 %reduce-scatter.13.cloned.1.call-start = ((), (), s32[]{:S(2)}) async-start(), calls=%async_computation.23 | async-start | bytes 5734400 | tf_op jit(solution)/shard_map/reduce_scatter | solution.py:87
  1036.0 56.3 %collective-permute-start.21 = (bf16[256,2560]{0,1:T(8,128)(2,1)}, bf16[256,2560]{0,1:T(8,128)(2,1)}, u32[]{:S(2)}, u32[]{:S(2)}) collective-permute-start(bf16[256,2560]{0,1:T(8,128)(2,1)} %bitcast.34), channel_id=1, source_target_pairs={{0,8},{8,0},{1,9},{9,1},{2,10},{10,2},{3,11},{11,3},{4,12},{12,4},... | collective-permute-start | bytes 3932168 | tf_op jit(solution)/shard_map/ppermute | solution.py:43
  1077.8 29.8 %collective-permute-start.49 = (bf16[256,2560]{0,1:T(8,128)(2,1)}, bf16[256,2560]{0,1:T(8,128)(2,1)}, u32[]{:S(2)}, u32[]{:S(2)}) collective-permute-start(bf16[256,2560]{0,1:T(8,128)(2,1)} %bitcast.485), channel_id=1, source_target_pairs={{0,8},{8,0},{1,9},{9,1},{2,10},{10,2},{3,11},{11,3},{4,12},{12,4},... | collective-permute-start | bytes 3932168 | tf_op jit(solution)/shard_map/ppermute | solution.py:43
  1090.3 292.3 %collective-permute-start.27 = (bf16[256,2560]{0,1:T(8,128)(2,1)}, bf16[256,2560]{0,1:T(8,128)(2,1)}, u32[]{:S(2)}, u32[]{:S(2)}) collective-permute-start(bf16[256,2560]{0,1:T(8,128)(2,1)} %bitcast.480), channel_id=1, source_target_pairs={{0,8},{8,0},{1,9},{9,1},{2,10},{10,2},{3,11},{11,3},{4,12},{12,4},... | collective-permute-start | bytes 3932168 | tf_op jit(solution)/shard_map/ppermute | solution.py:43
  1092.2 21.0 %collective-permute-start.51 = (bf16[256,2560]{0,1:T(8,128)(2,1)}, bf16[256,2560]{0,1:T(8,128)(2,1)}, u32[]{:S(2)}, u32[]{:S(2)}) collective-permute-start(bf16[256,2560]{0,1:T(8,128)(2,1)} %bitcast.488), channel_id=1, source_target_pairs={{0,8},{8,0},{1,9},{9,1},{2,10},{10,2},{3,11},{11,3},{4,12},{12,4},... | collective-permute-start | bytes 3932168 | tf_op jit(solution)/shard_map/ppermute | solution.py:43
  1095.1 56.8 %all-to-all-start.5 = ((bf16[8,80,384]{2,1,0:T(8,128)(2,1)}), bf16[8,80,384]{2,1,0:T(8,128)(2,1)S(1)}, u32[]{:S(2)}, u32[]{:S(2)}) async-start(bf16[8,80,384]{2,1,0:T(8,128)(2,1)} %bitcast.500), calls=%async_computation.7 | async-start | bytes 983040 | tf_op jit(solution)/shard_map/all_to_all | solution.py:78
  1107.1 61.8 %collective-permute-start.55 = (bf16[256,2560]{0,1:T(8,128)(2,1)}, bf16[256,2560]{0,1:T(8,128)(2,1)}, u32[]{:S(2)}, u32[]{:S(2)}) collective-permute-start(bf16[256,2560]{0,1:T(8,128)(2,1)} %bitcast.486), channel_id=1, source_target_pairs={{0,8},{8,0},{1,9},{9,1},{2,10},{10,2},{3,11},{11,3},{4,12},{12,4},... | collective-permute-start | bytes 3932168 | tf_op jit(solution)/shard_map/ppermute | solution.py:43
  1110.4 59.0 %collective-permute-start.50 = (bf16[256,2560]{0,1:T(8,128)(2,1)}, bf16[256,2560]{0,1:T(8,128)(2,1)}, u32[]{:S(2)}, u32[]{:S(2)}) collective-permute-start(bf16[256,2560]{0,1:T(8,128)(2,1)} %fusion.75), channel_id=1, source_target_pairs={{0,17},{1,16},{16,1},{17,0},{2,19},{3,18},{18,3},{19,2},{4,21},{5,... | collective-permute-start | bytes 3932168 | tf_op jit(solution)/shard_map/ppermute | solution.py:47
  1116.0 54.8 %collective-permute-start.52 = (bf16[256,2560]{0,1:T(8,128)(2,1)}, bf16[256,2560]{0,1:T(8,128)(2,1)}, u32[]{:S(2)}, u32[]{:S(2)}) collective-permute-start(bf16[256,2560]{0,1:T(8,128)(2,1)} %fusion.74), channel_id=1, source_target_pairs={{0,16},{1,17},{16,0},{17,1},{2,18},{3,19},{18,2},{19,3},{4,20},{5,... | collective-permute-start | bytes 3932168 | tf_op jit(solution)/shard_map/ppermute | solution.py:47
  1118.1 55.3 %collective-permute-start.54 = (bf16[256,2560]{0,1:T(8,128)(2,1)}, bf16[256,2560]{0,1:T(8,128)(2,1)}, u32[]{:S(2)}, u32[]{:S(2)}) collective-permute-start(bf16[256,2560]{0,1:T(8,128)(2,1)} %fusion.73), channel_id=1, source_target_pairs={{0,1},{1,0},{16,17},{17,16},{2,3},{3,2},{18,19},{19,18},{4,5},{5,4... | collective-permute-start | bytes 3932168 | tf_op jit(solution)/shard_map/ppermute | solution.py:47
  1151.9 85.9 %all-to-all-start.8 = ((bf16[8,80,896]{2,1,0:T(8,128)(2,1)}), bf16[8,80,896]{2,1,0:T(8,128)(2,1)}, u32[]{:S(2)}, u32[]{:S(2)}) async-start(bf16[8,80,896]{2,1,0:T(8,128)(2,1)} %bitcast.498), calls=%async_computation.13 | async-start | bytes 2293760 | tf_op jit(solution)/shard_map/all_to_all | solution.py:78
  1168.9 81.5 %collective-permute-start.23 = (bf16[256,2560]{0,1:T(8,128)(2,1)}, bf16[256,2560]{0,1:T(8,128)(2,1)}, u32[]{:S(2)}, u32[]{:S(2)}) collective-permute-start(bf16[256,2560]{0,1:T(8,128)(2,1)} %bitcast.482), channel_id=1, source_target_pairs={{0,8},{8,0},{1,9},{9,1},{2,10},{10,2},{3,11},{11,3},{4,12},{12,4},... | collective-permute-start | bytes 3932168 | tf_op jit(solution)/shard_map/ppermute | solution.py:43
  1169.3 158.7 %collective-permute-start.25 = (bf16[256,2560]{0,1:T(8,128)(2,1)}, bf16[256,2560]{0,1:T(8,128)(2,1)}, u32[]{:S(2)}, u32[]{:S(2)}) collective-permute-start(bf16[256,2560]{0,1:T(8,128)(2,1)} %bitcast.481), channel_id=1, source_target_pairs={{0,8},{8,0},{1,9},{9,1},{2,10},{10,2},{3,11},{11,3},{4,12},{12,4},... | collective-permute-start | bytes 3932168 | tf_op jit(solution)/shard_map/ppermute | solution.py:43
  1170.8 211.7 %collective-permute-start.22 = (bf16[256,2560]{0,1:T(8,128)(2,1)}, bf16[256,2560]{0,1:T(8,128)(2,1)}, u32[]{:S(2)}, u32[]{:S(2)}) collective-permute-start(bf16[256,2560]{0,1:T(8,128)(2,1)} %fusion.85), channel_id=1, source_target_pairs={{0,17},{1,16},{16,1},{17,0},{2,19},{3,18},{18,3},{19,2},{4,21},{5,... | collective-permute-start | bytes 3932168 | tf_op jit(solution)/shard_map/ppermute | solution.py:47
  1237.8 86.0 %all-to-all-start.7 = ((bf16[8,80,896]{2,1,0:T(8,128)(2,1)}), bf16[8,80,896]{2,1,0:T(8,128)(2,1)}, u32[]{:S(2)}, u32[]{:S(2)}) async-start(bf16[8,80,896]{2,1,0:T(8,128)(2,1)} %bitcast.496), calls=%async_computation.11 | async-start | bytes 2293760 | tf_op jit(solution)/shard_map/all_to_all | solution.py:78
  1242.1 136.5 %reduce-scatter.19.cloned.1.call-start = ((), (), s32[]{:S(2)}) async-start(), calls=%async_computation.26 | async-start | bytes 3276800 | tf_op jit(solution)/shard_map/reduce_scatter | solution.py:87
  1253.5 129.0 %collective-permute-start.24 = (bf16[256,2560]{0,1:T(8,128)(2,1)}, bf16[256,2560]{0,1:T(8,128)(2,1)}, u32[]{:S(2)}, u32[]{:S(2)}) collective-permute-start(bf16[256,2560]{0,1:T(8,128)(2,1)} %fusion.84), channel_id=1, source_target_pairs={{0,16},{1,17},{16,0},{17,1},{2,18},{3,19},{18,2},{19,3},{4,20},{5,... | collective-permute-start | bytes 3932168 | tf_op jit(solution)/shard_map/ppermute | solution.py:47
  1323.8 20.2 %all-to-all-start.6 = ((bf16[8,80,896]{2,1,0:T(8,128)(2,1)}), bf16[8,80,896]{2,1,0:T(8,128)(2,1)}, u32[]{:S(2)}, u32[]{:S(2)}) async-start(bf16[8,80,896]{2,1,0:T(8,128)(2,1)} %bitcast.497), calls=%async_computation.9 | async-start | bytes 2293760 | tf_op jit(solution)/shard_map/all_to_all | solution.py:78
  1331.2 51.4 %collective-permute-start.26 = (bf16[256,2560]{0,1:T(8,128)(2,1)}, bf16[256,2560]{0,1:T(8,128)(2,1)}, u32[]{:S(2)}, u32[]{:S(2)}) collective-permute-start(bf16[256,2560]{0,1:T(8,128)(2,1)} %fusion.83), channel_id=1, source_target_pairs={{0,1},{1,0},{16,17},{17,16},{2,3},{3,2},{18,19},{19,18},{4,5},{5,4... | collective-permute-start | bytes 3932168 | tf_op jit(solution)/shard_map/ppermute | solution.py:47
  1378.6 31.9 %all-to-all-start.4 = ((bf16[8,80,512]{2,1,0:T(8,128)(2,1)}), bf16[8,80,512]{2,1,0:T(8,128)(2,1)S(1)}, u32[]{:S(2)}, u32[]{:S(2)}) async-start(bf16[8,80,512]{2,1,0:T(8,128)(2,1)} %bitcast.499), calls=%async_computation.5 | async-start | bytes 1310720 | tf_op jit(solution)/shard_map/all_to_all | solution.py:78
  (83 other events, 1783.4 us)
Sparse Core Ops, SparseCore 0:
  111.0 51.3 all-gather.8
  188.3 53.3 all-gather.10
  243.3 42.3 all-gather.12
  287.1 86.0 all-gather.16
  374.6 85.7 all-gather.14
  461.8 85.7 all-gather.18
  972.2 50.8 reduce-scatter.8
  1026.0 41.1 reduce-scatter.10
  1069.5 82.3 reduce-scatter.16
  1154.1 83.6 reduce-scatter.14
  1240.1 83.6 reduce-scatter.12
  1325.9 52.6 reduce-scatter.18

commit v2 on v1

v2 whole, which is shorter than its diff:
```python
import functools
import math

import jax
import jax.numpy as jnp
from jax import lax
from jax.experimental import pallas as pl
from jax.experimental.pallas import tpu as pltpu
from jax.sharding import Mesh
from jax.sharding import PartitionSpec as P

HEADS = 32
KV_HEADS = 8
HEAD_DIM = 80
HALF = HEAD_DIM // 2
REPEAT = HEADS // KV_HEADS

EPSILON = 1e-05
ROPE_BASE = 10000.0

CHIPS = 4
SPLIT = 2 * CHIPS
GROUP = ("y", "core", "lo")
EVERY = ("y", "core", "hi", "lo")


def dot(left, right):
    return lax.dot_general(
        left, right, (((1,), (0,)), ((), ())), preferred_element_type=jnp.float32
    )


def by_columns(left, right):
    return lax.dot_general(
        left, right, (((1,), (1,)), ((), ())), preferred_element_type=jnp.float32
    )


def by_rows(left, right):
    return lax.dot_general(
        left, right, (((0,), (0,)), ((), ())), preferred_element_type=jnp.float32
    )


def swap(value, axis, step, size):
    return lax.ppermute(value, axis, [(place, place ^ step) for place in range(size)])


def to_group(weight):
    rows, cols = weight.shape[0], weight.shape[1] // SPLIT
    split = jnp.swapaxes(weight.reshape(rows, SPLIT, cols), 0, 1)
    return lax.all_to_all(split, GROUP, 0, 0, tiled=True).reshape(SPLIT * rows, cols)


def from_group(grads):
    rows, cols = grads.shape[0] // SPLIT, grads.shape[1]
    return lax.all_to_all(grads.reshape(SPLIT, rows, cols), GROUP, 0, 0, tiled=True)


def along(value):
    return lax.all_gather(value, "hi", axis=0, tiled=True)


def sum_along(value):
    return lax.psum_scatter(value, "hi", scatter_dimension=0, tiled=True)


MESH = pl.DeviceIdType.MESH
HALVES = 2


def places():
    chip = lax.axis_index("y") * lax.axis_size("lo") + lax.axis_index("lo")
    near = chip + 1 - 2 * lax.rem(chip, 2)
    return lax.axis_index("core"), (chip, near, lax.rem(chip + 2, CHIPS), CHIPS - 1 - chip)


def device_at(chip, core):
    lo_n = lax.axis_size("lo")
    return (lax.div(chip, lo_n), core, lax.axis_index("hi"), lax.rem(chip, lo_n))


def place_at(chip, core):
    lo_n = lax.axis_size("lo")
    return (lax.div(chip, lo_n) * 2 + core) * lo_n + lax.rem(chip, lo_n)


def peers():
    core, chips = places()
    return device_at(chips[0], 1 - core), device_at(chips[1], core), device_at(chips[2], core)


def along_hi(step):
    hi_n = lax.axis_size("hi")
    hi = lax.rem(lax.axis_index("hi") + step, hi_n)
    return lax.axis_index("y"), lax.axis_index("core"), hi, lax.axis_index("lo")


def exchange(source_of, dest_ref, sign, zero_ref, send_sem, recv_sem, fill_sem):
    hi_n, hi = lax.axis_size("hi"), lax.axis_index("hi")
    parts = []
    for step in range(1, hi_n):
        copy = pltpu.make_async_remote_copy(
            src_ref=source_of(step),
            dst_ref=dest_ref.at[step - 1],
            send_sem=send_sem.at[step - 1],
            recv_sem=recv_sem.at[step - 1],
            device_id=along_hi(step if sign > 0 else hi_n - step),
            device_id_type=MESH,
        )
        fill = pltpu.make_async_copy(zero_ref, dest_ref.at[step - 1], fill_sem.at[step - 1])
        down, up = hi >= step, hi + step < hi_n
        sends, gets = (up, down) if sign > 0 else (down, up)
        parts.append((copy, fill, sends, gets))

    def start():
        zero_ref[...] = jnp.zeros_like(zero_ref)
        for copy, fill, sends, gets in parts:
            pl.when(sends)(copy.start)
            pl.when(jnp.logical_not(gets))(fill.start)

    def wait():
        for copy, fill, sends, gets in parts:
            pl.when(sends)(copy.wait_send)
            pl.when(gets)(copy.wait_recv)
            pl.when(jnp.logical_not(gets))(fill.wait)

    return start, wait


def turn_scratch(shape, dtype, others):
    return [pltpu.VMEM(shape, dtype)] + [pltpu.SemaphoreType.DMA((others,))] * 3


def meet(devices):
    barrier = pltpu.get_barrier_semaphore()
    for device in devices:
        pl.semaphore_signal(barrier, inc=1, device_id=device, device_id_type=MESH)
    pl.semaphore_wait(barrier, len(devices))


def gather_dot_kernel(weights_n, gated, *refs):
    refs = list(refs)

    def take(count):
        taken = refs[:count]
        del refs[:count]
        return taken

    outs_n = 3 if gated else weights_n
    (x_ref,) = take(1)
    weight_refs = take(weights_n)
    (all_ref,) = take(1)
    out_refs = take(outs_n)
    (x_buf,) = take(1)
    weight_bufs = take(weights_n)
    out_bufs = take(outs_n)
    load_sem, weight_sem, keep_sem, out_sem, send_sem, recv_sem = refs
    core_peer, near_peer, far_peer = peers()
    rows = x_ref.shape[0]
    half = rows // HALVES

    def piece(ref, at):
        return ref.at[pl.ds(at * half, half)]

    def route(index, source, step, core, device):
        return [
            pltpu.make_async_remote_copy(
                src_ref=piece(source, at),
                dst_ref=piece(x_buf.at[step, core], at),
                send_sem=send_sem.at[index, at],
                recv_sem=recv_sem.at[index, at],
                device_id=device,
                device_id_type=MESH,
            )
            for at in range(HALVES)
        ]

    to_near = route(0, x_ref, 1, 0, near_peer)
    to_far = route(1, x_ref, 2, 0, far_peer)
    to_core = route(2, x_ref, 0, 1, core_peer)
    onward = route(3, x_buf.at[2, 0], 3, 0, near_peer)
    near_core = route(4, x_buf.at[1, 0], 1, 1, core_peer)
    far_core = route(5, x_buf.at[2, 0], 2, 1, core_peer)
    onward_core = route(6, x_buf.at[3, 0], 3, 1, core_peer)

    load = pltpu.make_async_copy(x_ref, x_buf.at[0, 0], load_sem)
    load.start()
    fetches = []
    for at in range(weights_n):
        fetch = pltpu.make_async_copy(weight_refs[at], weight_bufs[at], weight_sem.at[at])
        fetch.start()
        fetches.append(fetch)
    meet((core_peer, near_peer, far_peer))
    for at in range(HALVES):
        to_near[at].start()
        to_far[at].start()
    for at in range(HALVES):
        to_core[at].start()
    kept, stored = [], []

    def keep(step, core):
        copy = pltpu.make_async_copy(
            x_buf.at[step, core], all_ref.at[step, core], keep_sem.at[step, core]
        )
        copy.start()
        kept.append(copy)

    def compute(step, core):
        turn = len(stored) % 2
        if len(stored) >= 2:
            for copy in stored[-2]:
                copy.wait()
        values = [dot(x_buf[step, core], buf[...]) for buf in weight_bufs]
        if gated:
            gate, up = values
            values = [gate, up, gate / (1.0 + jnp.exp(-gate)) * up]
        copies = []
        for at, value in enumerate(values):
            out_bufs[at][turn] = value.astype(out_bufs[at].dtype)
            copy = pltpu.make_async_copy(
                out_bufs[at].at[turn], out_refs[at].at[step, core], out_sem.at[at, turn]
            )
            copy.start()
            copies.append(copy)
        stored.append(copies)

    load.wait()
    keep(0, 0)
    for fetch in fetches:
        fetch.wait()
    compute(0, 0)
    for at in range(HALVES):
        to_core[at].wait_recv()
    keep(0, 1)
    compute(0, 1)
    for at in range(HALVES):
        to_far[at].wait_recv()
        onward[at].start()
        far_core[at].start()
        to_near[at].wait_recv()
        near_core[at].start()
    keep(2, 0)
    keep(1, 0)
    compute(2, 0)
    compute(1, 0)
    for step, copies in ((2, far_core), (1, near_core)):
        for at in range(HALVES):
            copies[at].wait_recv()
        keep(step, 1)
        compute(step, 1)
    for at in range(HALVES):
        onward[at].wait_recv()
        onward_core[at].start()
    keep(3, 0)
    compute(3, 0)
    for at in range(HALVES):
        onward_core[at].wait_recv()
    keep(3, 1)
    compute(3, 1)
    for copies in (to_near, to_far, to_core, onward, near_core, far_core, onward_core):
        for copy in copies:
            copy.wait_send()
    for copy in kept:
        copy.wait()
    for copies in stored[-2:]:
        for copy in copies:
            copy.wait()


def gather_dot(value, weights, dtypes, collective_id, gated=False):
    rows, width = value.shape
    cols = [weight.shape[1] for weight in weights]
    out_cols = cols[:1] * 3 if gated else cols
    flops = 2 * SPLIT * rows * width * sum(cols)
    anywhere = pl.BlockSpec(memory_space=pl.ANY)
    return pl.pallas_call(
        functools.partial(gather_dot_kernel, len(weights), gated),
        in_specs=[anywhere] * (1 + len(weights)),
        out_specs=[anywhere] * (1 + len(out_cols)),
        out_shape=[jax.ShapeDtypeStruct((CHIPS, 2, rows, width), value.dtype)]
        + [
            jax.ShapeDtypeStruct((CHIPS, 2, rows, count), dtype)
            for count, dtype in zip(out_cols, dtypes)
        ],
        scratch_shapes=[pltpu.VMEM((CHIPS, 2, rows, width), value.dtype)]
        + [pltpu.VMEM((width, count), jnp.bfloat16) for count in cols]
        + [pltpu.VMEM((2, rows, count), dtype) for count, dtype in zip(out_cols, dtypes)]
        + [
            pltpu.SemaphoreType.DMA,
            pltpu.SemaphoreType.DMA((len(weights),)),
            pltpu.SemaphoreType.DMA((CHIPS, 2)),
            pltpu.SemaphoreType.DMA((len(out_cols), 2)),
            pltpu.SemaphoreType.DMA((7, HALVES)),
            pltpu.SemaphoreType.DMA((7, HALVES)),
        ],
        compiler_params=pltpu.CompilerParams(
            vmem_limit_bytes=60 << 20, collective_id=collective_id, has_side_effects=True
        ),
        cost_estimate=pl.CostEstimate(
            flops=flops * 6, bytes_accessed=SPLIT * rows * width * 4, transcendentals=0
        ),
        name=f"gather_dot_{collective_id}",
    )(value, *weights)


def dot_scatter_kernel(lefts_n, parts_n, extra, *refs):
    refs = list(refs)

    def take(count):
        taken = refs[:count]
        del refs[:count]
        return taken

    left_refs = take(lefts_n)
    weight_refs = take(lefts_n)
    extra_ref = take(extra)
    (out_ref,) = take(1)
    extra_out = take(extra)
    left_bufs = take(lefts_n)
    weight_bufs = take(lefts_n)
    core_out, core_in, chip_out, chip_in = take(4)
    left_sem, weight_sem, core_send, core_recv, chip_send, chip_recv = take(6)
    core_peer, near_peer, far_peer = peers()
    rows = left_refs[0].shape[2]
    cols = weight_refs[0].shape[0] // parts_n
    tile = 256 if cols % 256 == 0 else 128
    order = (3, 1, 2, 0)

    fetches = {}
    for part in range(parts_n):
        for at in range(lefts_n):
            fetches["weight", part, at] = pltpu.make_async_copy(
                weight_refs[at].at[pl.ds(part * cols, cols)],
                weight_bufs[at].at[pl.ds(part * cols, cols)],
                weight_sem.at[at, part],
            )
    for step in order:
        for core in (1, 0):
            for at in range(lefts_n):
                fetches[step, core, at] = pltpu.make_async_copy(
                    left_refs[at].at[step, core],
                    left_bufs[at].at[step, core],
                    left_sem.at[at, step, core],
                )
    for at in range(lefts_n):
        fetches["weight", 0, at].start()
    for step in order[:1]:
        for core in (1, 0):
            for at in range(lefts_n):
                fetches[step, core, at].start()
    for part in range(1, parts_n):
        for at in range(lefts_n):
            fetches["weight", part, at].start()
    for step in order[1:]:
        for core in (1, 0):
            for at in range(lefts_n):
                fetches[step, core, at].start()
    hi_n = lax.axis_size("hi")
    meet([core_peer, near_peer, far_peer] + [along_hi(step) for step in range(1, hi_n) if extra])
    if extra:
        start_turns, wait_turns = exchange(
            lambda step: extra_ref[0].at[step], extra_out[0], -1, *take(4)
        )
        start_turns()
    waited = set()

    def ready(*key):
        for at in range(lefts_n):
            if key + (at,) not in waited:
                waited.add(key + (at,))
                fetches[key + (at,)].wait()

    def product(step, core, part, place):
        total = None
        for left, weight in zip(left_bufs, weight_bufs):
            at = pl.multiple_of(part * cols + place * tile, tile)
            term = by_columns(left[step, core], weight[pl.ds(at, tile)])
            total = term if total is None else total + term
        return total

    def wide(part, place):
        return pl.ds(pl.multiple_of(part * cols + place * tile, tile), tile)

    def each_tile(body):
        def run(place, carry):
            body(place, pl.ds(pl.multiple_of(place * tile, tile), tile))
            return carry

        lax.fori_loop(0, cols // tile, run, 0)

    def core_copy(step, part):
        return pltpu.make_async_remote_copy(
            src_ref=core_out.at[step, part],
            dst_ref=core_in.at[step, part],
            send_sem=core_send.at[step, part],
            recv_sem=core_recv.at[step, part],
            device_id=core_peer,
            device_id_type=MESH,
        )

    def chip_copy(step, part):
        return pltpu.make_async_remote_copy(
            src_ref=chip_out.at[step - 1, part],
            dst_ref=chip_in.at[step - 1, part],
            send_sem=chip_send.at[step - 1, part],
            recv_sem=chip_recv.at[step - 1, part],
            device_id=far_peer if step == 2 else near_peer,
            device_id_type=MESH,
        )

    def other_core(step, part):
        ready("weight", part)
        ready(step, 1)

        def body(place, columns):
            core_out[step, part, :, columns] = product(step, 1, part, place).astype(jnp.bfloat16)

        each_tile(body)
        core_copy(step, part).start()

    def this_core(step, part):
        ready(step, 0)
        core_copy(step, part).wait_recv()
        if step == 2:
            chip_copy(3, part).wait_recv()

        def body(place, columns):
            total = product(step, 0, part, place)
            total += core_in[step, part, :, columns].astype(jnp.float32)
            if step == 2:
                total += chip_in[2, part, :, columns].astype(jnp.float32)
            if step:
                chip_out[step - 1, part, :, columns] = total.astype(jnp.bfloat16)
            else:
                out_ref[:, wide(part, place)] = total

        each_tile(body)
        if step:
            chip_copy(step, part).start()

    parts = range(parts_n)
    for step in (3, 1):
        for part in parts:
            other_core(step, part)
        for part in parts:
            this_core(step, part)
    for step in (2, 0):
        for part in parts:
            other_core(step, part)
    for part in parts:
        this_core(0, part)
    for part in parts:
        this_core(2, part)
    for step in (1, 2):
        for part in parts:
            chip_copy(step, part).wait_recv()
            columns = pl.ds(part * cols, cols)
            out_ref[:, columns] += chip_in[step - 1, part].astype(jnp.float32)
    for part in parts:
        for step in range(CHIPS):
            core_copy(step, part).wait_send()
            if step:
                chip_copy(step, part).wait_send()
    if extra:
        wait_turns()


def dot_scatter(lefts, weights, collective_id, extra=()):
    others = lax.axis_size("hi") - 1
    lefts = [left.reshape(CHIPS, 2, left.size // (SPLIT * left.shape[-1]), left.shape[-1]) for left in lefts]
    rows = lefts[0].shape[2]
    parts_n = 2
    cols = weights[0].shape[0] // parts_n
    depths = [left.shape[3] for left in lefts]
    flops = 2 * SPLIT * rows * cols * parts_n * sum(depths)
    anywhere = pl.BlockSpec(memory_space=pl.ANY)
    out, *received = pl.pallas_call(
        functools.partial(dot_scatter_kernel, len(lefts), parts_n, len(extra)),
        in_specs=[anywhere] * (2 * len(lefts) + len(extra)),
        out_specs=[pl.BlockSpec(memory_space=pltpu.VMEM)] + [anywhere] * len(extra),
        out_shape=[jax.ShapeDtypeStruct((rows, parts_n * cols), jnp.float32)]
        + [jax.ShapeDtypeStruct((others,) + array.shape[1:], array.dtype) for array in extra],
        scratch_shapes=[pltpu.VMEM((CHIPS, 2, rows, depth), jnp.bfloat16) for depth in depths]
        + [pltpu.VMEM((parts_n * cols, depth), jnp.bfloat16) for depth in depths]
        + [
            pltpu.VMEM((CHIPS, parts_n, rows, cols), jnp.bfloat16),
            pltpu.VMEM((CHIPS, parts_n, rows, cols), jnp.bfloat16),
            pltpu.VMEM((CHIPS - 1, parts_n, rows, cols), jnp.bfloat16),
            pltpu.VMEM((CHIPS - 1, parts_n, rows, cols), jnp.bfloat16),
            pltpu.SemaphoreType.DMA((len(lefts), CHIPS, 2)),
            pltpu.SemaphoreType.DMA((len(lefts), parts_n)),
            pltpu.SemaphoreType.DMA((CHIPS, parts_n)),
            pltpu.SemaphoreType.DMA((CHIPS, parts_n)),
            pltpu.SemaphoreType.DMA((CHIPS - 1, parts_n)),
            pltpu.SemaphoreType.DMA((CHIPS - 1, parts_n)),
        ]
        + [
            scratch
            for array in extra
            for scratch in turn_scratch(array.shape[1:], array.dtype, others)
        ],
        compiler_params=pltpu.CompilerParams(
            vmem_limit_bytes=60 << 20, collective_id=collective_id, has_side_effects=True
        ),
        cost_estimate=pl.CostEstimate(
            flops=flops * 6, bytes_accessed=SPLIT * rows * cols * parts_n * 4, transcendentals=0
        ),
        name=f"dot_scatter_{collective_id}",
    )(*lefts, *weights, *extra)
    return (out, *received) if extra else out


def shuffle_kernel(order, piece, x_ref, out_ref):
    rows = x_ref[...]
    out_ref[...] = jnp.concatenate([rows[:, at * piece : (at + 1) * piece] for at in order], 1)


def shuffle(value, order):
    rows, width = value.shape
    return pl.pallas_call(
        functools.partial(shuffle_kernel, order, width // len(order)),
        out_shape=jax.ShapeDtypeStruct(value.shape, value.dtype),
        compiler_params=params(),
        name="shuffle",
    )(value)


def products_kernel(lefts, *refs):
    left_refs, right_refs, out_ref = refs[: max(lefts) + 1], refs[max(lefts) + 1 : -1], refs[-1]
    at = 0
    for left, right_ref in zip(lefts, right_refs):
        cols = right_ref.shape[1]
        out_ref[:, at : at + cols] = by_rows(left_refs[left][...], right_ref[...]).astype(
            jnp.bfloat16
        )
        at += cols


def products(lefts, rights, block=256):
    arrays, uses = lefts
    tokens, width = arrays[0].shape
    total = sum(right.shape[1] for right in rights)
    return pl.pallas_call(
        functools.partial(products_kernel, uses),
        grid=(width // block,),
        in_specs=[pl.BlockSpec((tokens, block), lambda at: (0, at)) for _ in arrays]
        + [
            pl.BlockSpec((tokens, right.shape[1]), lambda at: (0, 0), pipeline_mode=pl.Buffered(1))
            for right in rights
        ],
        out_specs=pl.BlockSpec((block, total), lambda at: (at, 0)),
        out_shape=jax.ShapeDtypeStruct((width, total), jnp.bfloat16),
        compiler_params=params(),
        cost_estimate=pl.CostEstimate(
            flops=4 * tokens * width * total, bytes_accessed=2 * tokens * width, transcendentals=0
        ),
        name="products",
    )(*arrays, *rights)


def project_kernel(
    x_ref, weight_ref, cosine_ref, sine_ref, query_ref, key_value_ref
):
    rows = dot(x_ref[...], weight_ref[...])
    count = rows.shape[0] // cosine_ref.shape[1]
    cosine = jnp.concatenate([cosine_ref[0]] * count, 0)
    sine_table = jnp.concatenate([sine_ref[0]] * count, 0)
    turned = []
    for values in heads_of(rows, REPEAT + 1):
        first_half, second_half = values[:, :HALF], values[:, HALF:]
        turned += [
            first_half * cosine - second_half * sine_table,
            second_half * cosine + first_half * sine_table,
        ]
    query_ref[...] = jnp.concatenate(turned[: 2 * REPEAT], 1).astype(jnp.bfloat16)
    value = rows[:, HEAD_DIM * (REPEAT + 1) : HEAD_DIM * (REPEAT + 2)]
    both = jnp.concatenate(turned[2 * REPEAT :] + [value], 1).astype(jnp.bfloat16)
    length = cosine_ref.shape[1]
    key_value_ref[...] = jnp.concatenate(
        [both[length * at : length * (at + 1)] for at in range(count)], 1
    )


def spread_kernel(weights_n, extra, *refs):
    refs = list(refs)

    def take(count):
        taken = refs[:count]
        del refs[:count]
        return taken

    (x_ref,), weight_refs, extra_ref = take(1), take(weights_n), take(extra)
    (all_ref,), group_refs, extra_out = take(1), take(weights_n), take(extra)
    local_sem, send_sem, recv_sem, spread_send, spread_recv = take(5)
    core_peer, near_peer, far_peer = peers()
    core, chips = places()
    cols = group_refs[0].shape[2]
    own_place = place_at(chips[0], core)

    def route(index, source, step, to_core, device):
        return pltpu.make_async_remote_copy(
            src_ref=source,
            dst_ref=all_ref.at[step, to_core],
            send_sem=send_sem.at[index],
            recv_sem=recv_sem.at[index],
            device_id=device,
            device_id_type=MESH,
        )

    to_near = route(0, x_ref, 1, 0, near_peer)
    to_far = route(1, x_ref, 2, 0, far_peer)
    to_core = route(2, x_ref, 0, 1, core_peer)
    onward = route(3, all_ref.at[2, 0], 3, 0, near_peer)
    near_core = route(4, all_ref.at[1, 0], 1, 1, core_peer)
    far_core = route(5, all_ref.at[2, 0], 2, 1, core_peer)
    onward_core = route(6, all_ref.at[3, 0], 3, 1, core_peer)
    own = pltpu.make_async_copy(x_ref, all_ref.at[0, 0], local_sem.at[weights_n])
    own.start()
    mine = []
    for at in range(weights_n):
        columns = pl.ds(pl.multiple_of(own_place * cols, 128), cols)
        copy = pltpu.make_async_copy(
            weight_refs[at].at[:, columns], group_refs[at].at[own_place], local_sem.at[at]
        )
        copy.start()
        mine.append(copy)
    others = [(step, flip) for step in range(CHIPS) for flip in range(2)][1:]
    devices = [device_at(chips[step], 1 - core if flip else core) for step, flip in others]
    hi_n = lax.axis_size("hi")
    meet(devices + [along_hi(step) for step in range(1, hi_n) if extra])
    if extra:
        start_turns, wait_turns = exchange(lambda step: extra_ref[0], extra_out[0], 1, *take(4))
        start_turns()
    to_near.start()
    to_far.start()
    to_core.start()
    copies = []
    for at in range(weights_n):
        for index, (step, flip) in enumerate(others):
            place = place_at(chips[step], 1 - core if flip else core)
            columns = pl.ds(pl.multiple_of(place * cols, 128), cols)
            copies.append(
                pltpu.make_async_remote_copy(
                    src_ref=weight_refs[at].at[:, columns],
                    dst_ref=group_refs[at].at[own_place],
                    send_sem=spread_send.at[at, index],
                    recv_sem=spread_recv.at[at, index],
                    device_id=devices[index],
                    device_id_type=MESH,
                )
            )
    to_far.wait_recv()
    onward.start()
    far_core.start()
    to_near.wait_recv()
    near_core.start()
    for copy in copies:
        copy.start()
    onward.wait_recv()
    onward_core.start()
    for copy in (near_core, far_core, to_core, onward_core):
        copy.wait_recv()
    for copy in (to_near, to_far, to_core, onward, near_core, far_core, onward_core):
        copy.wait_send()
    for copy in copies:
        copy.wait()
    if extra:
        wait_turns()
    for copy in mine:
        copy.wait()
    own.wait()


def spread_and_gather(value, weights, collective_id, extra=()):
    others = lax.axis_size("hi") - 1
    rows, width = value.shape
    own_rows, cols = weights[0].shape[0], weights[0].shape[1] // SPLIT
    anywhere = pl.BlockSpec(memory_space=pl.ANY)
    count = len(weights)
    gathered, *groups = pl.pallas_call(
        functools.partial(spread_kernel, count, len(extra)),
        in_specs=[anywhere] * (1 + count + len(extra)),
        out_specs=[anywhere] * (1 + count + len(extra)),
        out_shape=[jax.ShapeDtypeStruct((CHIPS, 2, rows, width), value.dtype)]
        + [jax.ShapeDtypeStruct((SPLIT, own_rows, cols), jnp.bfloat16)] * count
        + [jax.ShapeDtypeStruct((others,) + array.shape, array.dtype) for array in extra],
        scratch_shapes=[
            pltpu.SemaphoreType.DMA((count + 1,)),
            pltpu.SemaphoreType.DMA((7,)),
            pltpu.SemaphoreType.DMA((7,)),
            pltpu.SemaphoreType.DMA((count, SPLIT - 1)),
            pltpu.SemaphoreType.DMA((count, SPLIT - 1)),
        ]
        + [scratch for array in extra for scratch in turn_scratch(array.shape, array.dtype, others)],
        compiler_params=pltpu.CompilerParams(
            vmem_limit_bytes=60 << 20, collective_id=collective_id, has_side_effects=True
        ),
        cost_estimate=pl.CostEstimate(
            flops=10**11, bytes_accessed=SPLIT * rows * width * 4, transcendentals=0
        ),
        name=f"spread_{collective_id}",
    )(value, *weights, *extra)
    groups[:count] = [group.reshape(SPLIT * own_rows, cols) for group in groups[:count]]
    return gathered, *groups


def after(value, *others):
    return lax.optimization_barrier((value,) + others)[0]


def by_step(value, at, axis):
    steps = [
        lax.dynamic_index_in_dim(value, at ^ step, axis) for step in range(value.shape[axis])
    ]
    return jnp.concatenate(steps, axis)


def params(limit=60):
    return pltpu.CompilerParams(vmem_limit_bytes=limit << 20)


def heads_of(values, count):
    return [values[:, HEAD_DIM * at : HEAD_DIM * (at + 1)] for at in range(count)]


def allow(key_seg_ref, key_place_ref, query_seg_ref, query_place_ref):
    allowed = (key_seg_ref[0] == query_seg_ref[0]) & (key_place_ref[...] <= query_place_ref[...])
    return jnp.where(allowed, 0.0, -1e30)


def unpack(own_ref, others_ref, pair_ref):
    pair, length = 2 * HEAD_DIM, own_ref.shape[0]
    count = own_ref.shape[1] // pair
    for case in range(count):

        @pl.when(pl.program_id(0) % count == case)
        def _():
            columns = slice(pair * case, pair * (case + 1))
            pair_ref[:length] = own_ref[:, columns]
            for step in range(others_ref.shape[0]):
                pair_ref[length * (step + 1) : length * (step + 2)] = others_ref[step, :, columns]


def attend_kernel(
    query_ref, own_ref, others_ref, key_seg_ref, key_place_ref, query_seg_ref, query_place_ref,
    mixed_ref, log_ref, bias_ref, pair_ref,
):
    queries_len = query_seg_ref.shape[2]
    seq_len = key_seg_ref.shape[1]
    to_log2 = 1.0 / math.sqrt(HEAD_DIM) / math.log(2.0)
    bias_ref[...] = allow(key_seg_ref, key_place_ref, query_seg_ref, query_place_ref)
    rows = query_ref[0, :, 0, 0].reshape(queries_len, REPEAT * HEAD_DIM)
    unpack(own_ref, others_ref, pair_ref)
    key_rows, value_rows = heads_of(pair_ref[...], 2)
    mixed = []
    for at, query_rows in enumerate(heads_of(rows, REPEAT)):
        scores = by_columns(key_rows, query_rows) * to_log2 + bias_ref[...]
        highest = jnp.max(scores, 0, keepdims=True)
        weight = jnp.exp2(scores - highest)
        total = jnp.sum(weight, 0, keepdims=True)
        probabilities = (weight * (1.0 / total)).astype(jnp.bfloat16)
        mixed.append(by_rows(value_rows, probabilities).T)
        log_ref[0, at : at + 1] = highest + jnp.log2(total)
    mixed.append(jnp.zeros((queries_len, mixed_ref.shape[5] - REPEAT * HEAD_DIM), jnp.float32))
    mixed = jnp.concatenate(mixed, 1).astype(jnp.bfloat16)
    mixed_ref[0, :, 0, 0] = mixed.reshape(mixed_ref.shape[1], mixed_ref.shape[4], mixed.shape[1])


def attend_back_kernel(
    query_ref, own_ref, others_ref, grad_ref, log_ref, key_seg_ref, key_place_ref, query_seg_ref,
    query_place_ref, cosine_ref, sine_ref, grad_query_ref, grad_key_value_ref, bias_ref, pair_ref,
):
    queries_len = query_seg_ref.shape[2]
    seq_len = key_seg_ref.shape[1]
    scaling = 1.0 / math.sqrt(HEAD_DIM)
    to_log2 = scaling / math.log(2.0)
    bias_ref[...] = allow(key_seg_ref, key_place_ref, query_seg_ref, query_place_ref)
    query_rows = query_ref[0, :, 0, 0].reshape(queries_len, REPEAT * HEAD_DIM)
    grad_rows = grad_ref[0, :, 0, 0].reshape(queries_len, grad_ref.shape[5])
    unpack(own_ref, others_ref, pair_ref)
    key_rows, value_rows = heads_of(pair_ref[...], 2)
    cosine, sine_table = cosine_ref[...], sine_ref[...]
    grad_keys = jnp.zeros((seq_len, HEAD_DIM), jnp.float32)
    grad_values = jnp.zeros((seq_len, HEAD_DIM), jnp.float32)
    grad_queries = []
    for at in range(REPEAT):
        query, grad = heads_of(query_rows, REPEAT)[at], heads_of(grad_rows, REPEAT)[at]
        scores = by_columns(key_rows, query) * to_log2 + bias_ref[...]
        probabilities = jnp.exp2(scores - log_ref[0, at : at + 1])
        grad_probs = by_columns(value_rows, grad)
        centre = jnp.sum(probabilities * grad_probs, 0, keepdims=True)
        grad_scores = (probabilities * (grad_probs - centre)).astype(jnp.bfloat16)
        grad_values += dot(probabilities.astype(jnp.bfloat16), grad)
        grad_keys += dot(grad_scores, query)
        turned = by_rows(key_rows, grad_scores) * scaling
        first_half, second_half = turned[:HALF], turned[HALF:]
        turned = jnp.concatenate(
            [
                first_half * cosine + second_half * sine_table,
                second_half * cosine - first_half * sine_table,
            ],
            0,
        )
        grad_queries.append(turned.T)
    grad_queries = jnp.concatenate(grad_queries, 1).astype(jnp.bfloat16)
    grad_query_ref[0, :, 0, 0] = grad_queries.reshape(
        grad_query_ref.shape[1], grad_query_ref.shape[4], grad_queries.shape[1]
    )
    both = jnp.concatenate([grad_keys * scaling, grad_values], 1).astype(jnp.bfloat16)
    both = both.reshape(grad_key_value_ref.shape[0], queries_len, 2 * HEAD_DIM)
    count = grad_key_value_ref.shape[2] // (2 * HEAD_DIM)
    for case in range(count):

        @pl.when(pl.program_id(0) % count == case)
        def _():
            columns = slice(2 * HEAD_DIM * case, 2 * HEAD_DIM * (case + 1))
            grad_key_value_ref[:, :, columns] = both


def unrotate_kernel(grad_query_ref, own_ref, others_ref, cosine_ref, sine_ref, grad_ref):
    cosine, sine_table = cosine_ref[0], sine_ref[0]
    total = own_ref[0].astype(jnp.float32)
    for step in range(others_ref.shape[0]):
        total += others_ref[step].astype(jnp.float32)
    for at in range(grad_ref.shape[1] * grad_ref.shape[2]):
        place = (0, at // grad_ref.shape[2], at % grad_ref.shape[2])
        rows = total[:, 2 * HEAD_DIM * at : 2 * HEAD_DIM * (at + 1)]
        first_half, second_half = rows[:, :HALF], rows[:, HALF:HEAD_DIM]
        turned = jnp.concatenate(
            [
                first_half * cosine + second_half * sine_table,
                second_half * cosine - first_half * sine_table,
                rows[:, HEAD_DIM:],
                jnp.zeros((rows.shape[0], grad_ref.shape[4] - (REPEAT + 2) * HEAD_DIM), jnp.float32),
            ],
            1,
        ).astype(jnp.bfloat16)
        grad_ref[place] = jnp.concatenate([grad_query_ref[place], turned], 1)


def shards(
    sizes,
    hidden_in,
    attn_gain,
    query_weight,
    key_weight,
    value_weight,
    out_weight,
    mlp_gain,
    gate_weight,
    up_weight,
    down_weight,
    segment_ids,
    grad_output,
):
    y_n, hi_n, lo_n = sizes
    seq_b, local_len, width = hidden_in.shape
    seq_len = segment_ids.shape[1]
    rows = seq_b * local_len
    tokens = SPLIT * rows
    own_rows = query_weight.shape[0]
    ff_width = gate_weight.shape[1]
    ff_pad = -(-ff_width // (SPLIT * 128)) * SPLIT * 128
    query_cols = HEADS * HEAD_DIM // SPLIT
    qkv_cols = query_cols + 2 * HEAD_DIM
    y_at, core_at = lax.axis_index("y"), lax.axis_index("core")
    hi_at, lo_at = lax.axis_index("hi"), lax.axis_index("lo")

    pieces = [(outer, at) for at in range(hi_n) for outer in range(2 * y_n)]
    order = [outer * hi_n + at for outer, at in pieces]
    back = [order.index(at) for at in range(len(order))]

    offset = (hi_at * lo_n + lo_at) * local_len
    own_segments = lax.dynamic_slice_in_dim(segment_ids, offset, local_len, 1)
    small = jnp.concatenate(
        [attn_gain, mlp_gain, own_segments.astype(jnp.bfloat16).reshape(rows)]
    )
    small_pad = -(-small.shape[0] // 128) * 128
    small = jnp.pad(small, (0, small_pad - small.shape[0])).reshape(1, 1, 1, 1, small_pad)
    for axis, name, size in ((3, "lo", lo_n), (1, "core", 2), (0, "y", y_n), (2, "hi", hi_n)):
        steps = [small] + [swap(small, name, step, size) for step in range(1, size)]
        small = jnp.concatenate(steps, axis)
    small = small.astype(jnp.float32)

    def gain_of(values):
        for at, axis in ((y_at, 0), (core_at, 1), (hi_at, 2), (lo_at, 3)):
            values = by_step(values, at, axis)
        return values.transpose(2, 0, 1, 3, 4).reshape(width)

    gain_one = gain_of(small[..., :own_rows])
    gain_two = gain_of(small[..., own_rows : 2 * own_rows])
    segments = small[..., 2 * own_rows : 2 * own_rows + rows]
    segments = segments.reshape(y_n, 2, hi_n, lo_n, seq_b, local_len)
    segments = by_step(segments, hi_at, 2).transpose(0, 1, 4, 2, 3, 5)
    steps = [(hi_at - step) % hi_n for step in range(hi_n)]
    segments = jnp.concatenate(
        [lax.dynamic_index_in_dim(segments, step, 3) for step in steps], 3
    )
    seqs = y_n * 2 * seq_b
    queries_len = lo_n * local_len
    key_segments = segments.reshape(seqs, seq_len)
    query_segments = key_segments[:, :queries_len]
    lo_place = lo_at ^ jnp.arange(lo_n)
    inner = (lo_place[:, None] * local_len + jnp.arange(local_len)[None, :]).reshape(queries_len)
    query_place = hi_at * queries_len + inner
    key_place = (hi_at - jnp.arange(hi_n)) % hi_n
    key_place = (key_place[:, None] * queries_len + inner[None, :]).reshape(seq_len)
    place_shape = (lo_n, local_len)
    frequency = ROPE_BASE ** (-(jnp.arange(HALF, dtype=jnp.float32) * 2.0 / HEAD_DIM))
    angles = query_place.astype(jnp.float32)[:, None] * frequency[None, :]
    cosine, sine_table = jnp.cos(angles), jnp.sin(angles)

    def spread(*groups):
        pieces = []
        for group, total in zip(groups[::2], groups[1::2]):
            pieces += [piece.reshape(own_rows, SPLIT, -1) for piece in group]
            empty = total - sum(piece.size // (own_rows * SPLIT) for piece in group)
            if empty:
                pieces.append(jnp.zeros((own_rows, SPLIT, empty), jnp.bfloat16))
        return to_group(jnp.concatenate(pieces, -1).reshape(own_rows, -1))

    def widen(weight):
        return jnp.pad(weight, ((0, 0), (0, ff_pad - ff_width)))

    def everywhere(weight):
        return along(weight)

    first_group = spread(
        [query_weight, key_weight, value_weight], 512, [out_weight], 512, [widen(gate_weight)], ff_pad // SPLIT
    )
    qkv_full = everywhere(first_group[:, :512])
    out_full = everywhere(first_group[:, 512:1024])
    gate_full = everywhere(first_group[:, 1024:])

    source = shuffle(hidden_in.reshape(rows, width), order).astype(jnp.float32)
    inv_one = lax.rsqrt(jnp.mean(source * source, -1, keepdims=True) + EPSILON)
    normed_one = source * inv_one
    normed_low, up_group = spread_and_gather(
        (normed_one * gain_one).astype(jnp.bfloat16), [widen(up_weight)], 0
    )
    normed_low = normed_low.reshape(tokens, width)
    slots = (y_n, lo_n, 2, seq_b, local_len)
    packed = 2 * seq_b * 2 * HEAD_DIM

    def over_slots(cols):
        return pl.BlockSpec((1, 2, seq_b, local_len, cols), lambda lo: (lo, 0, 0, 0, 0))

    def slot_table():
        return pl.BlockSpec((1, local_len, HALF), lambda chip: (chip % lo_n, 0, 0))

    def slot_rows(cols):
        return pl.BlockSpec((2 * rows, cols), lambda lo: (lo, 0))

    queries, key_value = pl.pallas_call(
        project_kernel,
        grid=(CHIPS,),
        in_specs=[
            slot_rows(width),
            pl.BlockSpec((width, 512), lambda lo: (0, 0), pipeline_mode=pl.Buffered(1)),
            slot_table(),
            slot_table(),
        ],
        out_specs=[slot_rows(query_cols), pl.BlockSpec((local_len, packed), lambda lo: (lo, 0))],
        out_shape=[
            jax.ShapeDtypeStruct((tokens, query_cols), jnp.bfloat16),
            jax.ShapeDtypeStruct((CHIPS * local_len, packed), jnp.bfloat16),
        ],
        compiler_params=params(),
        name="project",
    )(
        normed_low,
        qkv_full,
        cosine.reshape(place_shape + (HALF,)),
        sine_table.reshape(place_shape + (HALF,)),
    )
    queries = queries.reshape(slots + (query_cols,))
    cotangent = shuffle(grad_output.reshape(rows, width), order)
    cotangent_all, down_group, others = spread_and_gather(
        cotangent, [widen(down_weight)], 7, (key_value,)
    )
    cotangent_all = cotangent_all.reshape(tokens, width)
    up_full = everywhere(up_group)
    down_full = everywhere(down_group)


    def of_seq(at):
        return at // (2 * seq_b), 0, at // seq_b % 2, at % seq_b, 0, 0

    def per_seq(cols):
        return pl.BlockSpec((1, lo_n, 1, 1, local_len, cols), of_seq)

    own_spec = pl.BlockSpec((queries_len, packed), lambda at: (at // (2 * seq_b), 0))
    others_spec = pl.BlockSpec(
        (hi_n - 1, queries_len, packed), lambda at: (0, at // (2 * seq_b), 0)
    )
    pair_scratch = pltpu.VMEM((seq_len, 2 * HEAD_DIM), jnp.bfloat16)
    log_spec = pl.BlockSpec((1, REPEAT, queries_len), lambda at: (at, 0, 0))
    mask_specs = [
        pl.BlockSpec((1, seq_len, 1), lambda at: (at, 0, 0)),
        pl.BlockSpec((seq_len, 1), lambda at: (0, 0)),
        pl.BlockSpec((1, 1, queries_len), lambda at: (at, 0, 0)),
        pl.BlockSpec((1, queries_len), lambda at: (0, 0)),
    ]
    masks = (
        key_segments.reshape(seqs, seq_len, 1),
        key_place.reshape(seq_len, 1),
        query_segments.reshape(seqs, 1, queries_len),
        query_place.reshape(1, queries_len),
    )
    mixed_rows, log_total = pl.pallas_call(
        attend_kernel,
        grid=(seqs,),
        in_specs=[per_seq(query_cols), own_spec, others_spec] + mask_specs,
        out_specs=[per_seq(512), log_spec],
        out_shape=[
            jax.ShapeDtypeStruct(slots + (512,), jnp.bfloat16),
            jax.ShapeDtypeStruct((seqs, REPEAT, queries_len), jnp.float32),
        ],
        scratch_shapes=[pltpu.VMEM((seq_len, queries_len), jnp.float32), pair_scratch],
        compiler_params=params(),
        name="attend",
    )(queries, key_value, others, *masks)
    mixed_rows = mixed_rows.reshape(tokens, 512)
    middle = source + dot_scatter([mixed_rows], [out_full], 1)

    inv_two = lax.rsqrt(jnp.mean(middle * middle, -1, keepdims=True) + EPSILON)
    normed_two = middle * inv_two
    normed_mid, gate_value, up_value, active = gather_dot(
        (normed_two * gain_two).astype(jnp.bfloat16),
        [gate_full, up_full],
        (jnp.float32, jnp.float32, jnp.bfloat16),
        2,
        gated=True,
    )
    normed_mid = normed_mid.reshape(tokens, width)
    gate_value = gate_value.reshape(tokens, -1)
    up_value = up_value.reshape(tokens, -1)
    active = active.reshape(tokens, -1)
    grad_active = dot(cotangent_all, down_full)
    sigmoid_gate = jax.nn.sigmoid(gate_value)
    grad_gate = (
        grad_active * up_value * sigmoid_gate * (1.0 + gate_value * (1.0 - sigmoid_gate))
    ).astype(jnp.bfloat16)
    grad_up = (grad_active * jax.nn.silu(gate_value)).astype(jnp.bfloat16)
    grad_norm_mid = dot_scatter([grad_gate, grad_up], [gate_full, up_full], 4)
    scaled_two = grad_norm_mid * gain_two
    grad_middle = cotangent.astype(jnp.float32) + inv_two * (
        scaled_two - normed_two * jnp.mean(scaled_two * normed_two, -1, keepdims=True)
    )

    def finish(back):
        return jnp.swapaxes(back, 0, 1).astype(jnp.float32)

    gate_up_product = products(([normed_mid], (0, 0)), [grad_gate, grad_up])
    gate_up_summed = sum_along(gate_up_product)
    gate_up_back = from_group(gate_up_summed)
    gate_up_grads = finish(gate_up_back)
    gate_grads = gate_up_grads[..., : ff_pad // SPLIT].reshape(own_rows, ff_pad)[:, :ff_width]
    up_grads = gate_up_grads[..., ff_pad // SPLIT :].reshape(own_rows, ff_pad)[:, :ff_width]
    grad_middle = after(grad_middle, gate_up_product)

    grad_branch, grad_mixed = gather_dot(
        grad_middle.astype(jnp.bfloat16), [out_full], (jnp.bfloat16,), 5
    )
    grad_branch = grad_branch.reshape(tokens, width)
    down_product = products(([after(cotangent_all, grad_mixed)], (0,)), [active])
    grad_mixed = after(grad_mixed, down_product)
    down_summed = sum_along(after(down_product, gate_up_summed))
    down_back = from_group(down_summed)
    down_grads = finish(down_back).reshape(own_rows, ff_pad)[:, :ff_width]

    grad_queries, grad_key_value = pl.pallas_call(
        attend_back_kernel,
        grid=(seqs,),
        in_specs=[per_seq(query_cols), own_spec, others_spec, per_seq(512), log_spec]
        + mask_specs
        + [pl.BlockSpec((HALF, queries_len), lambda at: (0, 0))] * 2,
        out_specs=[
            per_seq(query_cols),
            pl.BlockSpec((hi_n, queries_len, packed), lambda at: (0, at // (2 * seq_b), 0)),
        ],
        out_shape=[
            jax.ShapeDtypeStruct(slots + (query_cols,), jnp.bfloat16),
            jax.ShapeDtypeStruct((hi_n, CHIPS * local_len, packed), jnp.bfloat16),
        ],
        scratch_shapes=[pltpu.VMEM((seq_len, queries_len), jnp.float32), pair_scratch],
        compiler_params=params(),
        name="attend_back",
    )(
        queries, key_value, others, grad_mixed.reshape(slots + (512,)), log_total, *masks,
        cosine.T, sine_table.T,
    )
    final, others = dot_scatter(
        [after(active, gate_up_back)], [down_full], 3, (grad_key_value,)
    )
    result = shuffle((middle + final).astype(jnp.bfloat16), back)
    flat = (CHIPS, 2, seq_b, local_len)
    grad_qkv = pl.pallas_call(
        unrotate_kernel,
        grid=(CHIPS,),
        in_specs=[
            over_slots(query_cols),
            pl.BlockSpec((1, local_len, packed), lambda chip: (0, chip, 0)),
            pl.BlockSpec((hi_n - 1, local_len, packed), lambda chip: (0, chip, 0)),
            slot_table(),
            slot_table(),
        ],
        out_specs=over_slots(512),
        out_shape=jax.ShapeDtypeStruct(flat + (512,), jnp.bfloat16),
        compiler_params=params(),
        name="unrotate",
    )(
        after(grad_queries, final).reshape(flat + (query_cols,)),
        grad_key_value,
        others,
        cosine.reshape(place_shape + (HALF,)),
        sine_table.reshape(place_shape + (HALF,)),
    ).reshape(tokens, 512)
    heads_product = products(([normed_low, grad_branch], (0, 1)), [grad_qkv, mixed_rows])
    grad_norm_one = dot_scatter([after(grad_qkv, heads_product, down_back)], [qkv_full], 6)
    scaled_one = grad_norm_one * gain_one
    grad_input = grad_middle + inv_one * (
        scaled_one - normed_one * jnp.mean(scaled_one * normed_one, -1, keepdims=True)
    )
    head_grads = finish(from_group(sum_along(heads_product)))
    grad_query = head_grads[..., :query_cols].reshape(own_rows, -1)
    grad_key = head_grads[..., query_cols : query_cols + HEAD_DIM].reshape(own_rows, -1)
    grad_value = head_grads[..., query_cols + HEAD_DIM : qkv_cols].reshape(own_rows, -1)

    def gain_grad(gain, pairs):
        total = sum(jnp.sum(weight.astype(jnp.float32) * grad, 1) for weight, grad in pairs)
        return total / gain.astype(jnp.float32)

    attn_gain_grad = gain_grad(
        attn_gain,
        [(query_weight, grad_query), (key_weight, grad_key), (value_weight, grad_value)],
    )
    mlp_gain_grad = gain_grad(mlp_gain, [(gate_weight, gate_grads), (up_weight, up_grads)])
    return (
        result.reshape(seq_b, local_len, width),
        shuffle(grad_input, back).reshape(seq_b, local_len, width),
        attn_gain_grad,
        grad_query,
        grad_key,
        grad_value,
        head_grads[..., 512 : 512 + query_cols].reshape(own_rows, -1),
        mlp_gain_grad,
        gate_grads,
        up_grads,
        down_grads,
    )


def solution(mesh):
    y_n = mesh.shape["batch"] // 2
    lo_n = CHIPS // y_n
    hi_n = mesh.shape["seq"] // lo_n
    fine = Mesh(mesh.devices.reshape(y_n, 2, hi_n, lo_n), EVERY)
    token = P(("y", "core"), ("hi", "lo"), None)
    vector = P(EVERY)
    matrix = P(EVERY, None)
    in_specs = (
        token, vector, matrix, matrix, matrix, matrix, vector, matrix, matrix, matrix,
        P(("y", "core"), None), token,
    )
    out_specs = (
        token, token, vector, matrix, matrix, matrix, matrix, vector, matrix, matrix, matrix,
    )

    def run(*arrays):
        return shards((y_n, hi_n, lo_n), *arrays)

    return jax.shard_map(run, mesh=fine, in_specs=in_specs, out_specs=out_specs, check_vma=False)
```

time: 1440 us -> 1040 us (0.72)
  Pallas kernels: 0 us -> 770 us
  waiting for transfers between devices: 500 us -> 100 us
  matrix products: 313 us -> 22 us
  local copies, waits for them, and re-layouts: 316 us -> 38.4 us
  other arithmetic: 115 us -> 34.7 us
  blocking collectives: 90.9 us -> 35.2 us
  starting transfers between devices: 70.1 us -> 18 us
    pallas_call x0 -> x19, Pallas kernels: none -> 770 us  [the longest x4 306 us: dot_scatter(): pl.pallas_call(functools.partial(dot_scatter_kernel, len(lefts), parts_n,...]
    ppermute x56 -> x6, waiting for transfers between devices: 284 us -> 8.3 us  [swap(): lax.ppermute(value, axis, [(place, place ^ step) for place in range(size)])]
    dot_general x66 -> x0, matrix products: 238 us -> none  [the longest x5 66.4 us: by_rows(): lax.dot_general(left, right, (((0,), (0,)), ((), ())), preferred_element_...]
    reduce_scatter x6 -> x3, waiting for transfers between devices: 190 us -> 16.2 us  [sum_along(): return lax.psum_scatter(value, 'hi', scatter_dimension=0, tiled=True)]
    unnamed x208 -> x90, local copies, waits for them, and re-layouts: 147 us -> 10.1 us
    all_gather x1 -> x0, blocking collectives: 71.6 us -> none  [shards(): small = lax.all_gather(small, EVERY, axis=0, tiled=True).astype(jnp.float32)]
    reshape x22 -> x17, local copies, waits for them, and re-layouts: 59.3 us -> 6.23 us  [the longest x9 3.7 us: spread(): pieces += [piece.reshape(own_rows, SPLIT, -1) for piece in group]]
    dot_general x5 -> x1, matrix products: 75 us -> 22 us  [dot(): lax.dot_general(left, right, (((1,), (0,)), ((), ())), preferred_element_...]
  transfers between devices with their start and end apart: 76 -> 17, of which waited for: 23 -> 9; matrix products, arithmetic and copies ran while one was open for 35% -> 5% of each run, Pallas kernels for 0% -> 72%
where the time goes in v2:
time: 1040 us; the launch traced here: 1030 us
  Pallas kernels  770 us (74%)
  waiting for transfers between devices  100 us (10%)
  local copies, waits for them, and re-layouts  38.4 us (4%)
  blocking collectives  35.2 us (3%)
  other arithmetic  34.7 us (3%)
  matrix products  22 us (2%)
  starting transfers between devices  18 us (2%)
  between operations  15.3 us (1%)
    pallas_call x4, Pallas kernels, dot_scatter(): pl.pallas_call(functools.partial(dot_scatter_kernel, len(lefts), parts_n,...  306 us
    pallas_call x2, Pallas kernels, spread_and_gather(): pl.pallas_call(functools.partial(spread_kernel, count, len(extra)), in_sp...  162 us
    pallas_call x2, Pallas kernels, gather_dot(): pl.pallas_call(functools.partial(gather_dot_kernel, len(weights), gated),...  128 us
    pallas_call x3, Pallas kernels, products(): pl.pallas_call(functools.partial(products_kernel, uses), grid=(width // b...  63.9 us
    all_gather x5, waiting for transfers between devices, along(): return lax.all_gather(value, 'hi', axis=0, tiled=True)  51.9 us
    pallas_call x1, Pallas kernels, shards(): pl.pallas_call(attend_back_kernel, grid=(seqs,), in_specs=[per_seq(query_...  39.9 us
    pallas_call x1, Pallas kernels, shards(): pl.pallas_call(attend_kernel, grid=(seqs,), in_specs=[per_seq(query_cols)...  36.5 us
    all_to_all x1, blocking collectives, to_group(): lax.all_to_all(split, GROUP, 0, 0, tiled=True).reshape(SPLIT * rows, cols)  35.2 us
  transfers between devices with their start and end apart: 17, of which 9 were waited for; matrix products, arithmetic and copies ran while one was open for 5% of the time, Pallas kernels for 72%

profile of v2, /device:TPU:0, one launch (start us, length us, event | category | flops | bytes accessed | tf_op | source)
XLA Modules:
  0.0 1034.4 jit_solution(17161124864883117532)
XLA Ops:
  7.2 1.4 pad.16
  8.6 1.1 copy.66
  13.8 4.4 concatenate.57
  18.2 35.2 %all_to_all.20 = bf16[8,80,1920]{2,1,0:T(8,128)(2,1)S(1)} all-to-all(bf16[8,80,1920]{2,1,0:T(8,128)(2,1)S(1)} %bitcast.113), channel_id=1, replica_groups=mesh['y'=2,'core'=2,'hi'=4,'lo'=2] {'y','core','lo'}, dimensions={0} | all-to-all | bytes 4915200 | tf_op jit(solution)/shard_map/all_to_all | solution.py:52
  53.4 1.4 copy-done.10
  54.8 1.2 fusion.52
  57.8 2.8 collective-permute-done
  60.6 2.9 shuffle.4
  64.1 1.8 fusion.17
  65.9 1.3 collective-permute-done.2
  67.2 1.6 collective-permute-start.3
  68.8 2.6 collective-permute-start.4
  71.7 1.1 pad.15.refs_1_
  72.8 1.5 collective-permute-done.4
  74.3 2.8 collective-permute-done.5
  77.4 1.4 fusion.12.refs_0_
  78.9 73.5 %spread_0.1 = (bf16[4,2,256,2560]{3,2,1,0:T(8,128)(2,1)}, bf16[8,80,896]{2,1,0:T(8,128)(2,1)}) custom-call(bf16[256,2560]{1,0:T(8,128)(2,1)} %fusion.12.refs_0_, bf16[80,7168]{1,0:T(8,128)(2,1)} %pad.15.refs_1_), custom_call_target="tpu_custom_call" | custom-call | flops 99999997952 | bytes 20971520 | tf_op jit(solution)/shard_map/spread_0/pallas_call | solution.py:681
  152.6 2.9 shuffle.5.refs_0_
  155.5 1.1 pad.17.refs_1_
  157.3 1.0 copy.64
  158.4 1.2 multiply_sine_fusion
  159.9 5.3 reshape_reshape.9.key_seg_ref
  166.1 2.3 slice.74
  168.7 13.6 %project.1 = (bf16[2048,320]{1,0:T(8,128)(2,1)}, bf16[512,640]{1,0:T(8,128)(2,1)}) custom-call(bf16[2048,2560]{1,0:T(8,128)(2,1)} %bitcast.109, bf16[2560,512]{1,0:T(8,128)(2,1)} %all-gather.6.cloned.1.call-done.weight_ref.refs_1_, f32[2,128,40]{2,1,0:T(8,128)} %get-tuple-element.112.cosine_ref, f32[2,128,40]{2,1,0:T(8,128)} %get-tuple-element.111.sine_ref), custom_call_target="tpu_custom_call" | custom-call | tf_op jit(solution)/shard_map/project/pallas_call | solution.py:955
  182.4 88.4 %spread_7.1 = (bf16[4,2,256,2560]{3,2,1,0:T(8,128)(2,1)}, bf16[8,80,896]{2,1,0:T(8,128)(2,1)}, bf16[3,512,640]{2,1,0:T(8,128)(2,1)}) custom-call(bf16[256,2560]{1,0:T(8,128)(2,1)} %shuffle.5.refs_0_, bf16[80,7168]{1,0:T(8,128)(2,1)} %pad.17.refs_1_, bf16[512,640]{1,0:T(8,128)(2,1)} %get-tuple-element.39.refs_2_.own_ref), custom_call_target="tpu_custom_call" | custom-call | flops 99999997952 | bytes 20971520 | tf_op jit(solution)/shard_map/spread_7/pallas_call | solution.py:681
  270.8 36.5 %attend.1 = (bf16[2,2,2,2,128,512]{5,4,3,2,1,0:T(8,128)(2,1)}, f32[8,4,256]{2,1,0:T(4,128)}) custom-call(bf16[2,2,2,2,128,320]{5,4,3,2,1,0:T(8,128)(2,1)} %bitcast.116, bf16[512,640]{1,0:T(8,128)(2,1)} %get-tuple-element.39.refs_2_.own_ref, bf16[3,512,640]{2,1,0:T(8,128)(2,1)} %get-tuple-element.40.others_ref, f32[8,1024,1]{2,1,0:T(8,128)} %reshape_reshape.9.key_seg_ref, ...), custom_call_target="tpu_custom_call" | custom-call | tf_op jit(solution)/shard_map/attend/pallas_call | solution.py:1011
  307.4 66.9 %dot_scatter_1.1 = f32[256,2560]{1,0:T(8,128)} custom-call(bf16[4,2,256,512]{3,2,1,0:T(8,128)(2,1)} %bitcast.140, bf16[2560,512]{1,0:T(8,128)(2,1)} %all-gather.8.cloned.1.call-done.refs_1_), custom_call_target="tpu_custom_call" | custom-call | flops 32212254720 | bytes 20971520 | tf_op jit(solution)/shard_map/dot_scatter_1/pallas_call | solution.py:478
  374.3 2.3 multiply_reduce_fusion.1
  376.8 1.6 multiply_convert_fusion.refs_0_
  378.9 18.4 %all-gather.10.cloned.1.call-done.refs_1_.refs_2_ = bf16[2560,896]{1,0:T(8,128)(2,1)} async-done(((bf16[640,896]{1,0:T(8,128)(2,1)}), bf16[2560,896]{1,0:T(8,128)(2,1)}) %all-gather.10.cloned.1.call-update) | async-done | bytes 4587536 | tf_op jit(solution)/shard_map/all_gather | solution.py:61
  397.3 67.1 %gather_dot_2.1 = (bf16[4,2,256,2560]{3,2,1,0:T(8,128)(2,1)}, f32[4,2,256,896]{3,2,1,0:T(8,128)}, f32[4,2,256,896]{3,2,1,0:T(8,128)}, bf16[4,2,256,896]{3,2,1,0:T(8,128)(2,1)}) custom-call(bf16[256,2560]{1,0:T(8,128)(2,1)} %multiply_convert_fusion.refs_0_, bf16[2560,896]{1,0:T(8,128)(2,1)} %all-gather.10.cloned.1.call-done.refs_1_.refs_2_, ...), custom_call_target="tpu_custom_call" | custom-call | flops 112742891520 | bytes 20971520 | tf_op jit(solution)/shard_map/gather_dot_2/pallas_call | solution.py:277
  464.4 33.4 %all-gather.14.cloned.1.call-done.refs_1_ = bf16[2560,896]{1,0:T(8,128)(2,1)} async-done(((bf16[640,896]{1,0:T(8,128)(2,1)}), bf16[2560,896]{1,0:T(8,128)(2,1)}) %all-gather.14.cloned.1.call-update) | async-done | bytes 4587536 | tf_op jit(solution)/shard_map/all_gather | solution.py:61
  497.8 22.0 %fusion.7 = (bf16[2048,896]{1,0:T(8,128)(2,1)}, bf16[2048,896]{1,0:T(8,128)(2,1)}) fusion(f32[4,2,256,896]{3,2,1,0:T(8,128)} %get-tuple-element.48, f32[4,2,256,896]{3,2,1,0:T(8,128)} %get-tuple-element.47, bf16[2048,2560]{1,0:T(8,128)(2,1)} %bitcast.142, bf16[2560,896]{1,0:T(8,128)(2,1)} %all-gather.14.cloned.1.call-done.refs_1_), kind=kOutput, calls=%fused_computation.10 | convolution fusion | flops 9419096064 | bytes 37093376 | tf_op jit(solution)/shard_map/dot_general | solution.py:28
  519.9 28.5 %products.3 = bf16[2560,1792]{1,0:T(8,128)(2,1)} custom-call(bf16[2048,2560]{1,0:T(8,128)(2,1)} %bitcast.145, bf16[2048,896]{1,0:T(8,128)(2,1)} %get-tuple-element.68.refs_1_, bf16[2048,896]{1,0:T(8,128)(2,1)} %get-tuple-element.67.refs_2_), custom_call_target="tpu_custom_call" | custom-call | flops 37580963840 | bytes 10485760 | tf_op jit(solution)/shard_map/products/pallas_call | solution.py:544
  548.4 71.6 %dot_scatter_4.1 = f32[256,2560]{1,0:T(8,128)} custom-call(bf16[4,2,256,896]{3,2,1,0:T(8,128)(2,1)} %bitcast.148, bf16[4,2,256,896]{3,2,1,0:T(8,128)(2,1)} %bitcast.147, bf16[2560,896]{1,0:T(8,128)(2,1)} %all-gather.10.cloned.1.call-done.refs_1_.refs_2_, bf16[2560,896]{1,0:T(8,128)(2,1)} %all-gather.12.cloned.1.call-done.refs_2_.refs_3_), custom_call_target="tpu_custom_call" | custom-call | flops 112742891520 | bytes 20971520 | tf_op jit(solution)/shard_map/dot_scatter_4/pallas_call | solution.py:478
  620.1 2.5 multiply_reduce_fusion
  623.0 1.1 multiply_add_fusion
  624.1 1.5 copy-done.7
  625.6 1.2 convert_element_type.92.refs_0_
  626.8 61.2 %gather_dot_5.1 = (bf16[4,2,256,2560]{3,2,1,0:T(8,128)(2,1)}, bf16[4,2,256,512]{3,2,1,0:T(8,128)(2,1)}) custom-call(bf16[256,2560]{1,0:T(8,128)(2,1)} %convert_element_type.92.refs_0_, bf16[2560,512]{1,0:T(8,128)(2,1)} %all-gather.8.cloned.1.call-done.refs_1_), custom_call_target="tpu_custom_call" | custom-call | flops 32212254720 | bytes 20971520 | tf_op jit(solution)/shard_map/gather_dot_5/pallas_call | solution.py:277
  687.9 16.1 %reduce-scatter.4.cloned.1.call-done = bf16[640,1792]{1,0:T(8,128)(2,1)} async-done(((bf16[2560,1792]{1,0:T(8,128)(2,1)}), bf16[640,1792]{1,0:T(8,128)(2,1)}) %reduce-scatter.4.cloned.1.call-update) | async-done | bytes 2293776 | tf_op jit(solution)/shard_map/reduce_scatter | solution.py:65
  704.1 3.6 all-to-all-start.1
  707.7 16.6 %products.4 = bf16[2560,896]{1,0:T(8,128)(2,1)} custom-call(bf16[2048,2560]{1,0:T(8,128)(2,1)} %bitcast.143, bf16[2048,896]{1,0:T(8,128)(2,1)} %bitcast.146), custom_call_target="tpu_custom_call" | custom-call | flops 18790481920 | bytes 10485760 | tf_op jit(solution)/shard_map/products/pallas_call | solution.py:544
  725.9 39.9 %attend_back.1 = (bf16[2,2,2,2,128,320]{5,4,3,2,1,0:T(8,128)(2,1)}, bf16[4,512,640]{2,1,0:T(8,128)(2,1)}) custom-call(bf16[2,2,2,2,128,320]{5,4,3,2,1,0:T(8,128)(2,1)} %bitcast.117, bf16[512,640]{1,0:T(8,128)(2,1)} %get-tuple-element.39.refs_2_.own_ref, bf16[3,512,640]{2,1,0:T(8,128)(2,1)} %get-tuple-element.40.others_ref, ...), custom_call_target="tpu_custom_call" | custom-call | tf_op jit(solution)/shard_map/attend_back/pallas_call | solution.py:1073
  765.8 100.9 %dot_scatter_3.1 = (f32[256,2560]{1,0:T(8,128)}, bf16[3,512,640]{2,1,0:T(8,128)(2,1)}) custom-call(bf16[4,2,256,896]{3,2,1,0:T(8,128)(2,1)} %get-tuple-element.43, bf16[2560,896]{1,0:T(8,128)(2,1)} %all-gather.14.cloned.1.call-done.refs_1_, bf16[4,512,640]{2,1,0:T(8,128)(2,1)} %get-tuple-element.55.refs_2_.own_ref), custom_call_target="tpu_custom_call" | custom-call | flops 56371445760 | bytes 20971520 | tf_op jit(solution)/shard_map/dot_scatter_3/pallas_call | solution.py:478
  866.7 7.4 unrotate.1
  874.1 18.8 %products.5 = bf16[2560,1024]{1,0:T(8,128)(2,1)} custom-call(bf16[2048,2560]{1,0:T(8,128)(2,1)} %bitcast.110, bf16[2048,2560]{1,0:T(8,128)(2,1)} %bitcast.144, bf16[2048,512]{1,0:T(8,128)(2,1)} %bitcast.127, bf16[2048,512]{1,0:T(8,128)(2,1)} %bitcast.141), custom_call_target="tpu_custom_call" | custom-call | flops 21474836480 | bytes 10485760 | tf_op jit(solution)/shard_map/products/pallas_call | solution.py:544
  892.9 2.6 convert_bitcast_fusion
  895.5 3.9 all-to-all-start.2
  899.3 2.6 slice_bitcast_fusion
  903.4 1.7 multiply_reduce_fusion.2
  905.2 1.7 multiply_reduce_fusion.3
  907.4 7.8 all-to-all-done.2
  916.3 66.7 %dot_scatter_6.1 = f32[256,2560]{1,0:T(8,128)} custom-call(bf16[4,2,256,512]{3,2,1,0:T(8,128)(2,1)} %bitcast.128, bf16[2560,512]{1,0:T(8,128)(2,1)} %all-gather.6.cloned.1.call-done.weight_ref.refs_1_), custom_call_target="tpu_custom_call" | custom-call | flops 32212254720 | bytes 20971520 | tf_op jit(solution)/shard_map/dot_scatter_6/pallas_call | solution.py:478
  983.0 2.5 fusion.13
  985.7 6.0 fusion.16
  991.7 4.1 shuffle.7
  995.8 2.9 shuffle.6
  998.9 3.6 all-to-all-start.3
  1002.5 1.5 slice_convert_fusion
  1004.0 16.2 %all-to-all-done.3 = bf16[8,80,1024]{2,1,0:T(8,128)(2,1)S(1)} async-done(((bf16[8,80,1024]{2,1,0:T(8,128)(2,1)}), bf16[8,80,1024]{2,1,0:T(8,128)(2,1)S(1)}, u32[]{:S(2)}, u32[]{:S(2)}) %all-to-all-start.3) | async-done | bytes 1310752 | tf_op jit(solution)/shard_map/all_to_all | solution.py:57
  1022.4 1.2 copy.49
  1023.8 1.1 multiply_reduce_fusion.5
  1025.7 1.1 reshape.341
  (181 shorter events, 18.9 us)
Async XLA Ops:
  7.2 2.6 copy-start.18
  7.2 161.5 %all-gather.6.cloned.1.call-start = ((), (), s32[]{:S(2)}) async-start(), calls=%async_computation.7 | async-start | bytes 3276800 | tf_op jit(solution)/shard_map/all_gather | solution.py:61
  8.6 1.6 copy-start.23
  8.6 2.0 copy-start.25
  9.7 1.8 copy-start.24
  53.4 1.4 copy-start.10
  53.4 3.4 copy-start.37
  53.4 3.4 copy-start.39
  56.0 15.7 %copy-start.14 = (bf16[80,6912]{1,0:T(8,128)(2,1)S(1)}, bf16[80,6912]{1,0:T(8,128)(2,1)}, u32[]{:S(2)}) copy-start(bf16[80,6912]{1,0:T(8,128)(2,1)} %param.20) | copy-start | bytes 3317764
  56.0 251.3 %all-gather.8.cloned.1.call-start = ((), (), s32[]{:S(2)}) async-start(), calls=%async_computation.8 | async-start | bytes 3276800 | tf_op jit(solution)/shard_map/all_gather | solution.py:61
  56.9 3.6 collective-permute-start
  60.6 2.9 collective-permute-start.1
  63.5 13.9 %copy-start = (bf16[256,2560]{1,0:T(8,128)(2,1)S(1)}, bf16[256,2560]{1,0:T(8,128)(2,1)}, u32[]{:S(2)}) copy-start(bf16[256,2560]{1,0:T(8,128)(2,1)} %shuffle.4) | copy-start | bytes 3932164
  63.5 3.7 collective-permute-start.2
  67.2 5.6 collective-permute-start.3
  68.8 5.4 collective-permute-start.4
  71.4 5.6 collective-permute-start.5
  71.7 7.2 copy-start.31
  77.4 75.0 %copy-start.27 = (f32[2560]{0:T(1024)}, f32[2560]{0:T(1024)S(1)}, u32[]{:S(2)}) copy-start(f32[2560]{0:T(1024)S(1)} %mul.178) | copy-start | bytes 30724
  78.9 300.0 %all-gather.12.cloned.1.call-start = ((), (), s32[]{:S(2)}) async-start(), calls=%async_computation.10 | async-start | bytes 5734400 | tf_op jit(solution)/shard_map/all_gather | solution.py:61
  152.4 3.1 copy-start.20
  152.4 244.9 %all-gather.10.cloned.1.call-start = ((), (), s32[]{:S(2)}) async-start(), calls=%async_computation.9 | async-start | bytes 5734400 | tf_op jit(solution)/shard_map/all_gather | solution.py:61
  156.6 0.7 copy-start.41
  158.4 7.7 copy-start.35
  166.1 210.5 %copy-start.29 = (f32[2560]{0:T(1024)}, f32[2560]{0:T(1024)S(1)}, u32[]{:S(2)}) copy-start(f32[2560]{0:T(1024)S(1)} %mul.190) | copy-start | bytes 30724
  168.4 329.4 %all-gather.14.cloned.1.call-start = ((), (), s32[]{:S(2)}) async-start(), calls=%async_computation.11 | async-start | bytes 5734400 | tf_op jit(solution)/shard_map/all_gather | solution.py:61
  307.4 66.9 %copy-start.1 = (bf16[256,2560]{1,0:T(8,128)(2,1)S(1)}, bf16[256,2560]{1,0:T(8,128)(2,1)}, u32[]{:S(2)}) copy-start(bf16[256,2560]{1,0:T(8,128)(2,1)} %shuffle.4) | copy-start | bytes 3932164
  374.3 2.5 copy-start.4
  376.8 1.6 copy-start.33
  378.4 325.6 %reduce-scatter.4.cloned.1.call-start = ((), (), s32[]{:S(2)}) async-start(), calls=%async_computation.12 | async-start | bytes 11468800 | tf_op jit(solution)/shard_map/reduce_scatter | solution.py:65
  548.4 71.7 %copy-start.2 = (bf16[256,2560]{1,0:T(8,128)(2,1)S(1)}, bf16[256,2560]{1,0:T(8,128)(2,1)}, u32[]{:S(2)}) copy-start(bf16[256,2560]{1,0:T(8,128)(2,1)} %shuffle.4) | copy-start | bytes 3932164
  548.4 71.7 %copy-start.5 = (f32[256,2560]{1,0:T(8,128)S(1)}, f32[256,2560]{1,0:T(8,128)}, u32[]{:S(2)}) copy-start(f32[256,2560]{1,0:T(8,128)} %dot_scatter_1.1) | copy-start | bytes 7864324
  548.4 71.7 %copy-start.30 = (f32[2560]{0:T(1024)S(1)}, f32[2560]{0:T(1024)}, u32[]{:S(2)}) copy-start(f32[2560]{0:T(1024)} %copy-done.29) | copy-start | bytes 30724
  548.4 71.7 %copy-start.34 = (f32[256]{0:T(256)S(1)}, f32[256]{0:T(256)}, u32[]{:S(2)}) copy-start(f32[256]{0:T(256)} %copy-done.33) | copy-start | bytes 3076
  620.1 2.6 copy-start.9
  620.1 2.9 copy-start.11
  624.1 1.5 copy-start.7
  704.1 61.7 %all-to-all-start.1 = ((bf16[8,80,1792]{2,1,0:T(8,128)(2,1)}), bf16[8,80,1792]{2,1,0:T(8,128)(2,1)S(1)}, u32[]{:S(2)}, u32[]{:S(2)}) async-start(bf16[8,80,1792]{2,1,0:T(8,128)(2,1)} %bitcast.125), calls=%async_computation.2 | async-start | bytes 4587520 | tf_op jit(solution)/shard_map/all_to_all | solution.py:57
  707.7 187.8 %reduce-scatter.6.cloned.1.call-start = ((), (), s32[]{:S(2)}) async-start(), calls=%async_computation.13 | async-start | bytes 5734400 | tf_op jit(solution)/shard_map/reduce_scatter | solution.py:65
  724.3 0.7 copy-start.42
  724.3 0.7 copy-start.36
  724.4 274.6 %reduce-scatter.8.cloned.1.call-start = ((), (), s32[]{:S(2)}) async-start(), calls=%async_computation.14 | async-start | bytes 6553600 | tf_op jit(solution)/shard_map/reduce_scatter | solution.py:65
  895.5 19.8 %all-to-all-start.2 = ((bf16[8,80,896]{2,1,0:T(8,128)(2,1)}), bf16[8,80,896]{2,1,0:T(8,128)(2,1)S(1)}, u32[]{:S(2)}, u32[]{:S(2)}) async-start(bf16[8,80,896]{2,1,0:T(8,128)(2,1)} %bitcast.135), calls=%async_computation.4 | async-start | bytes 2293760 | tf_op jit(solution)/shard_map/all_to_all | solution.py:57
  902.2 1.2 copy-start.15
  903.4 1.7 copy-start.16
  905.2 1.7 copy-start.40
  915.3 1.0 copy-start.12
  916.3 66.7 %copy-start.3 = (bf16[256,2560]{1,0:T(8,128)(2,1)S(1)}, bf16[256,2560]{1,0:T(8,128)(2,1)}, u32[]{:S(2)}) copy-start(bf16[256,2560]{1,0:T(8,128)(2,1)} %shuffle.4) | copy-start | bytes 3932164
  916.3 66.7 %copy-start.28 = (f32[2560]{0:T(1024)S(1)}, f32[2560]{0:T(1024)}, u32[]{:S(2)}) copy-start(f32[2560]{0:T(1024)} %copy-done.27) | copy-start | bytes 30724
  916.3 66.7 %copy-start.32 = (f32[256]{0:T(256)S(1)}, f32[256]{0:T(256)}, u32[]{:S(2)}) copy-start(f32[256]{0:T(256)} %copy-done.31) | copy-start | bytes 3076
  916.3 69.2 %copy-start.8 = (f32[256,2560]{1,0:T(8,128)S(1)}, f32[256,2560]{1,0:T(8,128)}, u32[]{:S(2)}) copy-start(f32[256,2560]{1,0:T(8,128)} %copy-done.7) | copy-start | bytes 7864324
  983.0 2.6 copy-start.6
  995.8 2.9 copy-start.13
  998.9 21.2 %all-to-all-start.3 = ((bf16[8,80,1024]{2,1,0:T(8,128)(2,1)}), bf16[8,80,1024]{2,1,0:T(8,128)(2,1)S(1)}, u32[]{:S(2)}, u32[]{:S(2)}) async-start(bf16[8,80,1024]{2,1,0:T(8,128)(2,1)} %bitcast.132), calls=%async_computation.6 | async-start | bytes 2621440 | tf_op jit(solution)/shard_map/all_to_all | solution.py:57
  1020.7 1.5 copy-start.19
  1022.2 3.5 copy-start.17
  1022.2 3.0 copy-start.26
  1023.8 1.5 copy-start.21
  1024.9 1.9 copy-start.38
  1025.2 2.1 copy-start.22
Sparse Core Ops, SparseCore 0:
  56.1 55.0 all-gather.5
  113.4 53.4 all-gather.7
  168.5 123.8 all-gather.11
  293.9 103.4 all-gather.9
  398.7 99.0 all-gather.13
  548.5 155.5 reduce-scatter.3
  724.5 118.1 reduce-scatter.5
  893.0 91.8 reduce-scatter.7

commit v3 on v2

--- a/solution.py
+++ b/solution.py
@@ -20,6 +20,7 @@
 
 CHIPS = 4
 SPLIT = 2 * CHIPS
+OUT_COLS, QKV_COLS = 384, 512
 GROUP = ("y", "core", "lo")
 EVERY = ("y", "core", "hi", "lo")
 
@@ -96,7 +97,7 @@
     return lax.axis_index("y"), lax.axis_index("core"), hi, lax.axis_index("lo")
 
 
-def exchange(source_of, dest_ref, sign, zero_ref, send_sem, recv_sem, fill_sem):
+def exchange(source_of, dest_ref, zero_ref, send_sem, recv_sem, fill_sem):
     hi_n, hi = lax.axis_size("hi"), lax.axis_index("hi")
     parts = []
     for step in range(1, hi_n):
@@ -105,13 +106,11 @@
             dst_ref=dest_ref.at[step - 1],
             send_sem=send_sem.at[step - 1],
             recv_sem=recv_sem.at[step - 1],
-            device_id=along_hi(step if sign > 0 else hi_n - step),
+            device_id=along_hi(hi_n - step),
             device_id_type=MESH,
         )
         fill = pltpu.make_async_copy(zero_ref, dest_ref.at[step - 1], fill_sem.at[step - 1])
-        down, up = hi >= step, hi + step < hi_n
-        sends, gets = (up, down) if sign > 0 else (down, up)
-        parts.append((copy, fill, sends, gets))
+        parts.append((copy, fill, hi >= step, hi + step < hi_n))
 
     def start():
         zero_ref[...] = jnp.zeros_like(zero_ref)
@@ -128,6 +127,43 @@
     return start, wait
 
 
+def relay(source_ref, dest_ref, zero_ref, send_sem, recv_sem, fill_sem):
+    hi_n, hi = lax.axis_size("hi"), lax.axis_index("hi")
+    copies, fills = [], []
+    for step in range(1, hi_n):
+        copies.append(
+            pltpu.make_async_remote_copy(
+                src_ref=source_ref if step == 1 else dest_ref.at[step - 2],
+                dst_ref=dest_ref.at[step - 1],
+                send_sem=send_sem.at[step - 1],
+                recv_sem=recv_sem.at[step - 1],
+                device_id=along_hi(1),
+                device_id_type=MESH,
+            )
+        )
+        fills.append(pltpu.make_async_copy(zero_ref, dest_ref.at[step - 1], fill_sem.at[step - 1]))
+
+    def sends(step):
+        return jnp.logical_and(hi + 1 < hi_n, hi >= step - 1)
+
+    def start():
+        zero_ref[...] = jnp.zeros_like(zero_ref)
+        for step in range(1, hi_n):
+            pl.when(hi < step)(fills[step - 1].start)
+        pl.when(sends(1))(copies[0].start)
+
+    def run():
+        for step in range(1, hi_n):
+            pl.when(hi >= step)(copies[step - 1].wait_recv)
+            if step + 1 < hi_n:
+                pl.when(sends(step + 1))(copies[step].start)
+        for step in range(1, hi_n):
+            pl.when(sends(step))(copies[step - 1].wait_send)
+            pl.when(hi < step)(fills[step - 1].wait)
+
+    return start, run
+
+
 def turn_scratch(shape, dtype, others):
     return [pltpu.VMEM(shape, dtype)] + [pltpu.SemaphoreType.DMA((others,))] * 3
 
@@ -139,7 +175,7 @@
     pl.semaphore_wait(barrier, len(devices))
 
 
-def gather_dot_kernel(weights_n, gated, *refs):
+def gather_dot_kernel(weights_n, gated, starts, *refs):
     refs = list(refs)
 
     def take(count):
@@ -163,7 +199,7 @@
     def piece(ref, at):
         return ref.at[pl.ds(at * half, half)]
 
-    def route(index, source, step, core, device):
+    def route(index, source, step, core, device, halves=range(HALVES)):
         return [
             pltpu.make_async_remote_copy(
                 src_ref=piece(source, at),
@@ -173,13 +209,16 @@
                 device_id=device,
                 device_id_type=MESH,
             )
-            for at in range(HALVES)
+            for at in halves
         ]
 
     to_near = route(0, x_ref, 1, 0, near_peer)
     to_far = route(1, x_ref, 2, 0, far_peer)
     to_core = route(2, x_ref, 0, 1, core_peer)
-    onward = route(3, x_buf.at[2, 0], 3, 0, near_peer)
+    onward = [
+        *route(3, x_buf.at[2, 0], 3, 0, near_peer, (0,)),
+        *route(3, x_buf.at[1, 0], 3, 0, far_peer, (1,)),
+    ]
     near_core = route(4, x_buf.at[1, 0], 1, 1, core_peer)
     far_core = route(5, x_buf.at[2, 0], 2, 1, core_peer)
     onward_core = route(6, x_buf.at[3, 0], 3, 1, core_peer)
@@ -188,15 +227,15 @@
     load.start()
     fetches = []
     for at in range(weights_n):
-        fetch = pltpu.make_async_copy(weight_refs[at], weight_bufs[at], weight_sem.at[at])
+        columns = pl.ds(starts[at], weight_bufs[at].shape[1])
+        fetch = pltpu.make_async_copy(
+            weight_refs[at].at[:, columns], weight_bufs[at], weight_sem.at[at]
+        )
         fetch.start()
         fetches.append(fetch)
     meet((core_peer, near_peer, far_peer))
-    for at in range(HALVES):
-        to_near[at].start()
-        to_far[at].start()
-    for at in range(HALVES):
-        to_core[at].start()
+    for copy in (to_near[1], to_far[0], to_near[0], to_far[1], to_core[0], to_core[1]):
+        copy.start()
     kept, stored = [], []
 
     def keep(step, core):
@@ -234,12 +273,16 @@
         to_core[at].wait_recv()
     keep(0, 1)
     compute(0, 1)
-    for at in range(HALVES):
-        to_far[at].wait_recv()
-        onward[at].start()
-        far_core[at].start()
-        to_near[at].wait_recv()
-        near_core[at].start()
+    to_far[0].wait_recv()
+    onward[0].start()
+    far_core[0].start()
+    to_near[1].wait_recv()
+    onward[1].start()
+    near_core[1].start()
+    to_far[1].wait_recv()
+    far_core[1].start()
+    to_near[0].wait_recv()
+    near_core[0].start()
     keep(2, 0)
     keep(1, 0)
     compute(2, 0)
@@ -268,14 +311,15 @@
             copy.wait()
 
 
-def gather_dot(value, weights, dtypes, collective_id, gated=False):
+def gather_dot(value, weights, dtypes, collective_id, gated=False, windows=None):
     rows, width = value.shape
-    cols = [weight.shape[1] for weight in weights]
+    windows = windows or [(0, weight.shape[1]) for weight in weights]
+    cols = [count for start, count in windows]
     out_cols = cols[:1] * 3 if gated else cols
     flops = 2 * SPLIT * rows * width * sum(cols)
     anywhere = pl.BlockSpec(memory_space=pl.ANY)
     return pl.pallas_call(
-        functools.partial(gather_dot_kernel, len(weights), gated),
+        functools.partial(gather_dot_kernel, len(weights), gated, [at for at, count in windows]),
         in_specs=[anywhere] * (1 + len(weights)),
         out_specs=[anywhere] * (1 + len(out_cols)),
         out_shape=[jax.ShapeDtypeStruct((CHIPS, 2, rows, width), value.dtype)]
@@ -298,13 +342,72 @@
             vmem_limit_bytes=60 << 20, collective_id=collective_id, has_side_effects=True
         ),
         cost_estimate=pl.CostEstimate(
-            flops=flops * 6, bytes_accessed=SPLIT * rows * width * 4, transcendentals=0
+            flops=flops // 4, bytes_accessed=SPLIT * rows * width * 4, transcendentals=0
         ),
         name=f"gather_dot_{collective_id}",
     )(value, *weights)
 
 
-def dot_scatter_kernel(lefts_n, parts_n, extra, *refs):
+def hosted(uses, left_refs, right_refs, out_ref, *scratch):
+    right_bufs, (left_buf, out_buf, right_sem, left_sem, out_sem) = (
+        scratch[: len(uses)],
+        scratch[len(uses) :],
+    )
+    block = left_buf.shape[3]
+    count = out_ref.shape[0] // block
+    loads = [
+        pltpu.make_async_copy(ref, buf, right_sem.at[at])
+        for at, (ref, buf) in enumerate(zip(right_refs, right_bufs))
+    ]
+
+    def fetch(at, slot):
+        columns = pl.ds(pl.multiple_of(at * block, block), block)
+        return [
+            pltpu.make_async_copy(
+                ref.at[:, columns], left_buf.at[slot, index], left_sem.at[slot, index]
+            )
+            for index, ref in enumerate(left_refs)
+        ]
+
+    def store(at, slot):
+        rows = pl.ds(pl.multiple_of(at * block, block), block)
+        return pltpu.make_async_copy(out_buf.at[slot], out_ref.at[rows], out_sem.at[slot])
+
+    def start():
+        for copy in loads + fetch(0, 0):
+            copy.start()
+
+    def run():
+        for copy in loads:
+            copy.wait()
+
+        def body(at, carry):
+            slot = lax.rem(at, 2)
+
+            @pl.when(at + 1 < count)
+            def _():
+                for copy in fetch(at + 1, 1 - slot):
+                    copy.start()
+
+            for copy in fetch(at, slot):
+                copy.wait()
+            pl.when(at >= 2)(lambda: store(at - 2, slot).wait())
+            column = 0
+            for index, buf in zip(uses, right_bufs):
+                value = by_rows(left_buf[slot, index], buf[...])
+                out_buf[slot, :, column : column + buf.shape[1]] = value.astype(jnp.bfloat16)
+                column += buf.shape[1]
+            store(at, slot).start()
+            return carry
+
+        lax.fori_loop(0, count, body, 0)
+        for at in (count - 2, count - 1):
+            store(at, at % 2).wait()
+
+    return start, run
+
+
+def dot_scatter_kernel(lefts_n, parts_n, extra, starts, uses, *refs):
     refs = list(refs)
 
     def take(count):
@@ -315,8 +418,11 @@
     left_refs = take(lefts_n)
     weight_refs = take(lefts_n)
     extra_ref = take(extra)
+    host_lefts = take(max(uses) + 1 if uses else 0)
+    host_rights = take(len(uses))
     (out_ref,) = take(1)
     extra_out = take(extra)
+    host_out = take(1 if uses else 0)
     left_bufs = take(lefts_n)
     weight_bufs = take(lefts_n)
     core_out, core_in, chip_out, chip_in = take(4)
@@ -331,7 +437,9 @@
     for part in range(parts_n):
         for at in range(lefts_n):
             fetches["weight", part, at] = pltpu.make_async_copy(
-                weight_refs[at].at[pl.ds(part * cols, cols)],
+                weight_refs[at].at[
+                    pl.ds(part * cols, cols), pl.ds(starts[at], weight_bufs[at].shape[1])
+                ],
                 weight_bufs[at].at[pl.ds(part * cols, cols)],
                 weight_sem.at[at, part],
             )
@@ -360,9 +468,12 @@
     meet([core_peer, near_peer, far_peer] + [along_hi(step) for step in range(1, hi_n) if extra])
     if extra:
         start_turns, wait_turns = exchange(
-            lambda step: extra_ref[0].at[step], extra_out[0], -1, *take(4)
+            lambda step: extra_ref[0].at[step], extra_out[0], *take(4)
         )
         start_turns()
+    if uses:
+        start_host, run_host = hosted(uses, host_lefts, host_rights, host_out[0], *take(len(uses) + 5))
+        start_host()
     waited = set()
 
     def ready(*key):
@@ -405,9 +516,12 @@
             dst_ref=chip_in.at[step - 1, part],
             send_sem=chip_send.at[step - 1, part],
             recv_sem=chip_recv.at[step - 1, part],
-            device_id=far_peer if step == 2 else near_peer,
+            device_id=far_peer if step == 2 or (step == 3 and part % 2) else near_peer,
             device_id_type=MESH,
         )
+
+    def joint(part):
+        return 1 if part % 2 else 2
 
     def other_core(step, part):
         ready("weight", part)
@@ -422,13 +536,14 @@
     def this_core(step, part):
         ready(step, 0)
         core_copy(step, part).wait_recv()
-        if step == 2:
+        joins = step == joint(part)
+        if joins:
             chip_copy(3, part).wait_recv()
 
         def body(place, columns):
             total = product(step, 0, part, place)
             total += core_in[step, part, :, columns].astype(jnp.float32)
-            if step == 2:
+            if joins:
                 total += chip_in[2, part, :, columns].astype(jnp.float32)
             if step:
                 chip_out[step - 1, part, :, columns] = total.astype(jnp.bfloat16)
@@ -440,18 +555,23 @@
             chip_copy(step, part).start()
 
     parts = range(parts_n)
-    for step in (3, 1):
-        for part in parts:
-            other_core(step, part)
-        for part in parts:
-            this_core(step, part)
-    for step in (2, 0):
-        for part in parts:
-            other_core(step, part)
+    for part in parts:
+        other_core(3, part)
+    for part in parts:
+        this_core(3, part)
+    for part in parts:
+        other_core(3 - joint(part), part)
+    for part in parts:
+        this_core(3 - joint(part), part)
+    for part in parts:
+        other_core(joint(part), part)
+        other_core(0, part)
     for part in parts:
         this_core(0, part)
     for part in parts:
-        this_core(2, part)
+        this_core(joint(part), part)
+    if uses:
+        run_host()
     for step in (1, 2):
         for part in parts:
             chip_copy(step, part).wait_recv()
@@ -466,7 +586,11 @@
         wait_turns()
 
 
-def dot_scatter(lefts, weights, collective_id, extra=()):
+def dot_scatter(lefts, weights, collective_id, extra=(), windows=None, host=((), (), ())):
+    windows = windows or [(0, weight.shape[1]) for weight in weights]
+    host_lefts, uses, host_rights = host
+    total = sum(right.shape[1] for right in host_rights)
+    block = 256
     others = lax.axis_size("hi") - 1
     lefts = [left.reshape(CHIPS, 2, left.size // (SPLIT * left.shape[-1]), left.shape[-1]) for left in lefts]
     rows = lefts[0].shape[2]
@@ -476,11 +600,16 @@
     flops = 2 * SPLIT * rows * cols * parts_n * sum(depths)
     anywhere = pl.BlockSpec(memory_space=pl.ANY)
     out, *received = pl.pallas_call(
-        functools.partial(dot_scatter_kernel, len(lefts), parts_n, len(extra)),
-        in_specs=[anywhere] * (2 * len(lefts) + len(extra)),
-        out_specs=[pl.BlockSpec(memory_space=pltpu.VMEM)] + [anywhere] * len(extra),
+        functools.partial(
+            dot_scatter_kernel, len(lefts), parts_n, len(extra), [at for at, count in windows], uses
+        ),
+        in_specs=[anywhere]
+        * (2 * len(lefts) + len(extra) + len(host_lefts) + len(host_rights)),
+        out_specs=[pl.BlockSpec(memory_space=pltpu.VMEM)]
+        + [anywhere] * (len(extra) + bool(uses)),
         out_shape=[jax.ShapeDtypeStruct((rows, parts_n * cols), jnp.float32)]
-        + [jax.ShapeDtypeStruct((others,) + array.shape[1:], array.dtype) for array in extra],
+        + [jax.ShapeDtypeStruct((others,) + array.shape[1:], array.dtype) for array in extra]
+        + [jax.ShapeDtypeStruct((parts_n * cols, total), jnp.bfloat16)] * bool(uses),
         scratch_shapes=[pltpu.VMEM((CHIPS, 2, rows, depth), jnp.bfloat16) for depth in depths]
         + [pltpu.VMEM((parts_n * cols, depth), jnp.bfloat16) for depth in depths]
         + [
@@ -499,16 +628,25 @@
             scratch
             for array in extra
             for scratch in turn_scratch(array.shape[1:], array.dtype, others)
-        ],
+        ]
+        + [pltpu.VMEM(right.shape, right.dtype) for right in host_rights]
+        + [
+            pltpu.VMEM((2, len(host_lefts)) + (SPLIT * rows, block), jnp.bfloat16),
+            pltpu.VMEM((2, block, total), jnp.bfloat16),
+            pltpu.SemaphoreType.DMA((len(uses),)),
+            pltpu.SemaphoreType.DMA((2, len(host_lefts))),
+            pltpu.SemaphoreType.DMA((2,)),
+        ]
+        * bool(uses),
         compiler_params=pltpu.CompilerParams(
             vmem_limit_bytes=60 << 20, collective_id=collective_id, has_side_effects=True
         ),
         cost_estimate=pl.CostEstimate(
-            flops=flops * 6, bytes_accessed=SPLIT * rows * cols * parts_n * 4, transcendentals=0
+            flops=flops // 4, bytes_accessed=SPLIT * rows * cols * parts_n * 4, transcendentals=0
         ),
         name=f"dot_scatter_{collective_id}",
-    )(*lefts, *weights, *extra)
-    return (out, *received) if extra else out
+    )(*lefts, *weights, *extra, *host_lefts, *host_rights)
+    return (out, *received) if received else out
 
 
 def shuffle_kernel(order, piece, x_ref, out_ref):
@@ -526,43 +664,40 @@
     )(value)
 
 
-def products_kernel(lefts, *refs):
-    left_refs, right_refs, out_ref = refs[: max(lefts) + 1], refs[max(lefts) + 1 : -1], refs[-1]
-    at = 0
-    for left, right_ref in zip(lefts, right_refs):
-        cols = right_ref.shape[1]
-        out_ref[:, at : at + cols] = by_rows(left_refs[left][...], right_ref[...]).astype(
-            jnp.bfloat16
-        )
-        at += cols
-
-
-def products(lefts, rights, block=256):
-    arrays, uses = lefts
-    tokens, width = arrays[0].shape
-    total = sum(right.shape[1] for right in rights)
+def products_kernel(left_ref, *refs):
+    left = left_ref[...]
+    for right_ref, out_ref in zip(refs[: len(refs) // 2], refs[len(refs) // 2 :]):
+        out_ref[...] = by_rows(left, right_ref[...]).astype(jnp.bfloat16)
+
+
+def products(left, rights, block=256):
+    tokens, width = left.shape
+    cols = [right.shape[1] for right in rights]
     return pl.pallas_call(
-        functools.partial(products_kernel, uses),
+        products_kernel,
         grid=(width // block,),
-        in_specs=[pl.BlockSpec((tokens, block), lambda at: (0, at)) for _ in arrays]
+        in_specs=[pl.BlockSpec((tokens, block), lambda at: (0, at))]
         + [
-            pl.BlockSpec((tokens, right.shape[1]), lambda at: (0, 0), pipeline_mode=pl.Buffered(1))
-            for right in rights
+            pl.BlockSpec((tokens, count), lambda at: (0, 0), pipeline_mode=pl.Buffered(1))
+            for count in cols
         ],
-        out_specs=pl.BlockSpec((block, total), lambda at: (at, 0)),
-        out_shape=jax.ShapeDtypeStruct((width, total), jnp.bfloat16),
+        out_specs=[pl.BlockSpec((block, count), lambda at: (at, 0)) for count in cols],
+        out_shape=[jax.ShapeDtypeStruct((width, count), jnp.bfloat16) for count in cols],
         compiler_params=params(),
         cost_estimate=pl.CostEstimate(
-            flops=4 * tokens * width * total, bytes_accessed=2 * tokens * width, transcendentals=0
+            flops=4 * tokens * width * sum(cols), bytes_accessed=2 * tokens * width, transcendentals=0
         ),
         name="products",
-    )(*arrays, *rights)
+    )(left, *rights)
 
 
 def project_kernel(
-    x_ref, weight_ref, cosine_ref, sine_ref, query_ref, key_value_ref
+    x_ref, gain_ref, weight_ref, cosine_ref, sine_ref, low_ref, query_ref, key_value_ref
 ):
-    rows = dot(x_ref[...], weight_ref[...])
+    source = x_ref[...].astype(jnp.float32)
+    inverse = lax.rsqrt(jnp.mean(source * source, -1, keepdims=True) + EPSILON)
+    low_ref[...] = (source * inverse * gain_ref[...]).astype(jnp.bfloat16)
+    rows = dot(low_ref[...], weight_ref[:, OUT_COLS:])
     count = rows.shape[0] // cosine_ref.shape[1]
     cosine = jnp.concatenate([cosine_ref[0]] * count, 0)
     sine_table = jnp.concatenate([sine_ref[0]] * count, 0)
@@ -598,20 +733,28 @@
     cols = group_refs[0].shape[2]
     own_place = place_at(chips[0], core)
 
-    def route(index, source, step, to_core, device):
-        return pltpu.make_async_remote_copy(
-            src_ref=source,
-            dst_ref=all_ref.at[step, to_core],
-            send_sem=send_sem.at[index],
-            recv_sem=recv_sem.at[index],
-            device_id=device,
-            device_id_type=MESH,
-        )
+    half = x_ref.shape[0] // HALVES
+
+    def route(index, source, step, to_core, device, halves=range(HALVES)):
+        return [
+            pltpu.make_async_remote_copy(
+                src_ref=source.at[pl.ds(at * half, half)],
+                dst_ref=all_ref.at[step, to_core, pl.ds(at * half, half)],
+                send_sem=send_sem.at[index, at],
+                recv_sem=recv_sem.at[index, at],
+                device_id=device,
+                device_id_type=MESH,
+            )
+            for at in halves
+        ]
 
     to_near = route(0, x_ref, 1, 0, near_peer)
     to_far = route(1, x_ref, 2, 0, far_peer)
     to_core = route(2, x_ref, 0, 1, core_peer)
-    onward = route(3, all_ref.at[2, 0], 3, 0, near_peer)
+    onward = [
+        *route(3, all_ref.at[2, 0], 3, 0, near_peer, (0,)),
+        *route(3, all_ref.at[1, 0], 3, 0, far_peer, (1,)),
+    ]
     near_core = route(4, all_ref.at[1, 0], 1, 1, core_peer)
     far_core = route(5, all_ref.at[2, 0], 2, 1, core_peer)
     onward_core = route(6, all_ref.at[3, 0], 3, 1, core_peer)
@@ -630,11 +773,10 @@
     hi_n = lax.axis_size("hi")
     meet(devices + [along_hi(step) for step in range(1, hi_n) if extra])
     if extra:
-        start_turns, wait_turns = exchange(lambda step: extra_ref[0], extra_out[0], 1, *take(4))
+        start_turns, wait_turns = relay(extra_ref[0], extra_out[0], *take(4))
         start_turns()
-    to_near.start()
-    to_far.start()
-    to_core.start()
+    for copy in (to_near[1], to_far[0], to_near[0], to_far[1], to_core[0], to_core[1]):
+        copy.start()
     copies = []
     for at in range(weights_n):
         for index, (step, flip) in enumerate(others):
@@ -650,23 +792,31 @@
                     device_id_type=MESH,
                 )
             )
-    to_far.wait_recv()
-    onward.start()
-    far_core.start()
-    to_near.wait_recv()
-    near_core.start()
+    to_far[0].wait_recv()
+    onward[0].start()
+    far_core[0].start()
+    to_near[1].wait_recv()
+    onward[1].start()
+    near_core[1].start()
+    to_far[1].wait_recv()
+    far_core[1].start()
+    to_near[0].wait_recv()
+    near_core[0].start()
     for copy in copies:
         copy.start()
-    onward.wait_recv()
-    onward_core.start()
-    for copy in (near_core, far_core, to_core, onward_core):
-        copy.wait_recv()
-    for copy in (to_near, to_far, to_core, onward, near_core, far_core, onward_core):
-        copy.wait_send()
+    for at in range(HALVES):
+        onward[at].wait_recv()
+        onward_core[at].start()
+    for group in (near_core, far_core, to_core, onward_core):
+        for copy in group:
+            copy.wait_recv()
+    for group in (to_near, to_far, to_core, onward, near_core, far_core, onward_core):
+        for copy in group:
+            copy.wait_send()
+    if extra:
+        wait_turns()
     for copy in copies:
         copy.wait()
-    if extra:
-        wait_turns()
     for copy in mine:
         copy.wait()
     own.wait()
@@ -687,8 +837,8 @@
         + [jax.ShapeDtypeStruct((others,) + array.shape, array.dtype) for array in extra],
         scratch_shapes=[
             pltpu.SemaphoreType.DMA((count + 1,)),
-            pltpu.SemaphoreType.DMA((7,)),
-            pltpu.SemaphoreType.DMA((7,)),
+            pltpu.SemaphoreType.DMA((7, HALVES)),
+            pltpu.SemaphoreType.DMA((7, HALVES)),
             pltpu.SemaphoreType.DMA((count, SPLIT - 1)),
             pltpu.SemaphoreType.DMA((count, SPLIT - 1)),
         ]
@@ -697,7 +847,7 @@
             vmem_limit_bytes=60 << 20, collective_id=collective_id, has_side_effects=True
         ),
         cost_estimate=pl.CostEstimate(
-            flops=10**11, bytes_accessed=SPLIT * rows * width * 4, transcendentals=0
+            flops=10**9, bytes_accessed=SPLIT * rows * width * 4, transcendentals=0
         ),
         name=f"spread_{collective_id}",
     )(value, *weights, *extra)
@@ -726,7 +876,7 @@
 
 def allow(key_seg_ref, key_place_ref, query_seg_ref, query_place_ref):
     allowed = (key_seg_ref[0] == query_seg_ref[0]) & (key_place_ref[...] <= query_place_ref[...])
-    return jnp.where(allowed, 0.0, -1e30)
+    return jnp.where(allowed, 0.0, -1e30).T
 
 
 def unpack(own_ref, others_ref, pair_ref):
@@ -746,8 +896,8 @@
     query_ref, own_ref, others_ref, key_seg_ref, key_place_ref, query_seg_ref, query_place_ref,
     mixed_ref, log_ref, bias_ref, pair_ref,
 ):
-    queries_len = query_seg_ref.shape[2]
-    seq_len = key_seg_ref.shape[1]
+    queries_len = query_seg_ref.shape[1]
+    seq_len = key_seg_ref.shape[2]
     to_log2 = 1.0 / math.sqrt(HEAD_DIM) / math.log(2.0)
     bias_ref[...] = allow(key_seg_ref, key_place_ref, query_seg_ref, query_place_ref)
     rows = query_ref[0, :, 0, 0].reshape(queries_len, REPEAT * HEAD_DIM)
@@ -771,8 +921,8 @@
     query_ref, own_ref, others_ref, grad_ref, log_ref, key_seg_ref, key_place_ref, query_seg_ref,
     query_place_ref, cosine_ref, sine_ref, grad_query_ref, grad_key_value_ref, bias_ref, pair_ref,
 ):
-    queries_len = query_seg_ref.shape[2]
-    seq_len = key_seg_ref.shape[1]
+    queries_len = query_seg_ref.shape[1]
+    seq_len = key_seg_ref.shape[2]
     scaling = 1.0 / math.sqrt(HEAD_DIM)
     to_log2 = scaling / math.log(2.0)
     bias_ref[...] = allow(key_seg_ref, key_place_ref, query_seg_ref, query_place_ref)
@@ -871,11 +1021,28 @@
     order = [outer * hi_n + at for outer, at in pieces]
     back = [order.index(at) for at in range(len(order))]
 
+    def spread(*groups):
+        pieces = []
+        for group, total in zip(groups[::2], groups[1::2]):
+            pieces += [piece.reshape(own_rows, SPLIT, -1) for piece in group]
+            empty = total - sum(piece.size // (own_rows * SPLIT) for piece in group)
+            if empty:
+                pieces.append(jnp.zeros((own_rows, SPLIT, empty), jnp.bfloat16))
+        return to_group(jnp.concatenate(pieces, -1).reshape(own_rows, -1))
+
+    def widen(weight):
+        return jnp.pad(weight, ((0, 0), (0, ff_pad - ff_width)))
+
+    def everywhere(weight):
+        return along(weight)
+
+    first_group = spread([out_weight], OUT_COLS, [query_weight, key_weight, value_weight], QKV_COLS)
     offset = (hi_at * lo_n + lo_at) * local_len
     own_segments = lax.dynamic_slice_in_dim(segment_ids, offset, local_len, 1)
     small = jnp.concatenate(
         [attn_gain, mlp_gain, own_segments.astype(jnp.bfloat16).reshape(rows)]
     )
+    small = after(small, first_group)
     small_pad = -(-small.shape[0] // 128) * 128
     small = jnp.pad(small, (0, small_pad - small.shape[0])).reshape(1, 1, 1, 1, small_pad)
     for axis, name, size in ((3, "lo", lo_n), (1, "core", 2), (0, "y", y_n), (2, "hi", hi_n)):
@@ -906,40 +1073,31 @@
     query_place = hi_at * queries_len + inner
     key_place = (hi_at - jnp.arange(hi_n)) % hi_n
     key_place = (key_place[:, None] * queries_len + inner[None, :]).reshape(seq_len)
+    masks = (
+        key_segments.reshape(seqs, 1, seq_len),
+        key_place.reshape(1, seq_len),
+        query_segments.reshape(seqs, queries_len, 1),
+        query_place.reshape(queries_len, 1),
+    )
     place_shape = (lo_n, local_len)
     frequency = ROPE_BASE ** (-(jnp.arange(HALF, dtype=jnp.float32) * 2.0 / HEAD_DIM))
     angles = query_place.astype(jnp.float32)[:, None] * frequency[None, :]
     cosine, sine_table = jnp.cos(angles), jnp.sin(angles)
 
-    def spread(*groups):
-        pieces = []
-        for group, total in zip(groups[::2], groups[1::2]):
-            pieces += [piece.reshape(own_rows, SPLIT, -1) for piece in group]
-            empty = total - sum(piece.size // (own_rows * SPLIT) for piece in group)
-            if empty:
-                pieces.append(jnp.zeros((own_rows, SPLIT, empty), jnp.bfloat16))
-        return to_group(jnp.concatenate(pieces, -1).reshape(own_rows, -1))
-
-    def widen(weight):
-        return jnp.pad(weight, ((0, 0), (0, ff_pad - ff_width)))
-
-    def everywhere(weight):
-        return along(weight)
-
-    first_group = spread(
-        [query_weight, key_weight, value_weight], 512, [out_weight], 512, [widen(gate_weight)], ff_pad // SPLIT
-    )
-    qkv_full = everywhere(first_group[:, :512])
-    out_full = everywhere(first_group[:, 512:1024])
-    gate_full = everywhere(first_group[:, 1024:])
-
-    source = shuffle(hidden_in.reshape(rows, width), order).astype(jnp.float32)
+    heads_full = everywhere(first_group)
+    out_window, qkv_window = [(0, OUT_COLS)], [(OUT_COLS, QKV_COLS)]
+    hidden = shuffle(hidden_in.reshape(rows, width), order)
+    cotangent = shuffle(grad_output.reshape(rows, width), order)
+    hidden_all, gate_group, up_group = spread_and_gather(
+        after(hidden, first_group, gain_one, cotangent, *masks, cosine, sine_table),
+        [widen(gate_weight), widen(up_weight)],
+        0,
+    )
+    gate_full = everywhere(gate_group)
+    source = hidden.astype(jnp.float32)
     inv_one = lax.rsqrt(jnp.mean(source * source, -1, keepdims=True) + EPSILON)
     normed_one = source * inv_one
-    normed_low, up_group = spread_and_gather(
-        (normed_one * gain_one).astype(jnp.bfloat16), [widen(up_weight)], 0
-    )
-    normed_low = normed_low.reshape(tokens, width)
+
     slots = (y_n, lo_n, 2, seq_b, local_len)
     packed = 2 * seq_b * 2 * HEAD_DIM
 
@@ -952,30 +1110,36 @@
     def slot_rows(cols):
         return pl.BlockSpec((2 * rows, cols), lambda lo: (lo, 0))
 
-    queries, key_value = pl.pallas_call(
+    normed_low, queries, key_value = pl.pallas_call(
         project_kernel,
         grid=(CHIPS,),
         in_specs=[
             slot_rows(width),
-            pl.BlockSpec((width, 512), lambda lo: (0, 0), pipeline_mode=pl.Buffered(1)),
+            pl.BlockSpec((1, width), lambda lo: (0, 0)),
+            pl.BlockSpec(heads_full.shape, lambda lo: (0, 0), pipeline_mode=pl.Buffered(1)),
             slot_table(),
             slot_table(),
         ],
-        out_specs=[slot_rows(query_cols), pl.BlockSpec((local_len, packed), lambda lo: (lo, 0))],
+        out_specs=[
+            slot_rows(width),
+            slot_rows(query_cols),
+            pl.BlockSpec((local_len, packed), lambda lo: (lo, 0)),
+        ],
         out_shape=[
+            jax.ShapeDtypeStruct((tokens, width), jnp.bfloat16),
             jax.ShapeDtypeStruct((tokens, query_cols), jnp.bfloat16),
             jax.ShapeDtypeStruct((CHIPS * local_len, packed), jnp.bfloat16),
         ],
         compiler_params=params(),
         name="project",
     )(
-        normed_low,
-        qkv_full,
+        hidden_all.reshape(tokens, width),
+        gain_one.reshape(1, width),
+        heads_full,
         cosine.reshape(place_shape + (HALF,)),
         sine_table.reshape(place_shape + (HALF,)),
     )
     queries = queries.reshape(slots + (query_cols,))
-    cotangent = shuffle(grad_output.reshape(rows, width), order)
     cotangent_all, down_group, others = spread_and_gather(
         cotangent, [widen(down_weight)], 7, (key_value,)
     )
@@ -997,32 +1161,26 @@
     pair_scratch = pltpu.VMEM((seq_len, 2 * HEAD_DIM), jnp.bfloat16)
     log_spec = pl.BlockSpec((1, REPEAT, queries_len), lambda at: (at, 0, 0))
     mask_specs = [
-        pl.BlockSpec((1, seq_len, 1), lambda at: (at, 0, 0)),
-        pl.BlockSpec((seq_len, 1), lambda at: (0, 0)),
-        pl.BlockSpec((1, 1, queries_len), lambda at: (at, 0, 0)),
-        pl.BlockSpec((1, queries_len), lambda at: (0, 0)),
+        pl.BlockSpec((1, 1, seq_len), lambda at: (at, 0, 0)),
+        pl.BlockSpec((1, seq_len), lambda at: (0, 0)),
+        pl.BlockSpec((1, queries_len, 1), lambda at: (at, 0, 0)),
+        pl.BlockSpec((queries_len, 1), lambda at: (0, 0)),
     ]
-    masks = (
-        key_segments.reshape(seqs, seq_len, 1),
-        key_place.reshape(seq_len, 1),
-        query_segments.reshape(seqs, 1, queries_len),
-        query_place.reshape(1, queries_len),
-    )
     mixed_rows, log_total = pl.pallas_call(
         attend_kernel,
         grid=(seqs,),
         in_specs=[per_seq(query_cols), own_spec, others_spec] + mask_specs,
-        out_specs=[per_seq(512), log_spec],
+        out_specs=[per_seq(OUT_COLS), log_spec],
         out_shape=[
-            jax.ShapeDtypeStruct(slots + (512,), jnp.bfloat16),
+            jax.ShapeDtypeStruct(slots + (OUT_COLS,), jnp.bfloat16),
             jax.ShapeDtypeStruct((seqs, REPEAT, queries_len), jnp.float32),
         ],
         scratch_shapes=[pltpu.VMEM((seq_len, queries_len), jnp.float32), pair_scratch],
         compiler_params=params(),
         name="attend",
     )(queries, key_value, others, *masks)
-    mixed_rows = mixed_rows.reshape(tokens, 512)
-    middle = source + dot_scatter([mixed_rows], [out_full], 1)
+    mixed_rows = mixed_rows.reshape(tokens, OUT_COLS)
+    middle = source + dot_scatter([mixed_rows], [heads_full], 1, windows=out_window)
 
     inv_two = lax.rsqrt(jnp.mean(middle * middle, -1, keepdims=True) + EPSILON)
     normed_two = middle * inv_two
@@ -1037,13 +1195,19 @@
     gate_value = gate_value.reshape(tokens, -1)
     up_value = up_value.reshape(tokens, -1)
     active = active.reshape(tokens, -1)
-    grad_active = dot(cotangent_all, down_full)
+    (down_product,) = products(cotangent_all, [active])
+    down_summed = sum_along(down_product)
+    grad_active = dot(after(cotangent_all, down_product), down_full)
     sigmoid_gate = jax.nn.sigmoid(gate_value)
     grad_gate = (
         grad_active * up_value * sigmoid_gate * (1.0 + gate_value * (1.0 - sigmoid_gate))
     ).astype(jnp.bfloat16)
     grad_up = (grad_active * jax.nn.silu(gate_value)).astype(jnp.bfloat16)
-    grad_norm_mid = dot_scatter([grad_gate, grad_up], [gate_full, up_full], 4)
+    gate_product, up_product = products(normed_mid, [grad_gate, grad_up])
+    gate_summed = sum_along(gate_product)
+    grad_norm_mid = dot_scatter(
+        [after(grad_gate, gate_product), grad_up], [gate_full, up_full], 4
+    )
     scaled_two = grad_norm_mid * gain_two
     grad_middle = cotangent.astype(jnp.float32) + inv_two * (
         scaled_two - normed_two * jnp.mean(scaled_two * normed_two, -1, keepdims=True)
@@ -1052,28 +1216,25 @@
     def finish(back):
         return jnp.swapaxes(back, 0, 1).astype(jnp.float32)
 
-    gate_up_product = products(([normed_mid], (0, 0)), [grad_gate, grad_up])
-    gate_up_summed = sum_along(gate_up_product)
-    gate_up_back = from_group(gate_up_summed)
-    gate_up_grads = finish(gate_up_back)
-    gate_grads = gate_up_grads[..., : ff_pad // SPLIT].reshape(own_rows, ff_pad)[:, :ff_width]
-    up_grads = gate_up_grads[..., ff_pad // SPLIT :].reshape(own_rows, ff_pad)[:, :ff_width]
-    grad_middle = after(grad_middle, gate_up_product)
-
     grad_branch, grad_mixed = gather_dot(
-        grad_middle.astype(jnp.bfloat16), [out_full], (jnp.bfloat16,), 5
+        grad_middle.astype(jnp.bfloat16), [heads_full], (jnp.bfloat16,), 5, windows=out_window
     )
     grad_branch = grad_branch.reshape(tokens, width)
-    down_product = products(([after(cotangent_all, grad_mixed)], (0,)), [active])
-    grad_mixed = after(grad_mixed, down_product)
-    down_summed = sum_along(after(down_product, gate_up_summed))
-    down_back = from_group(down_summed)
-    down_grads = finish(down_back).reshape(own_rows, ff_pad)[:, :ff_width]
+    up_summed = sum_along(up_product)
+    both_back = from_group(
+        jnp.concatenate([after(down_summed, grad_mixed), after(gate_summed, grad_mixed)], 1)
+    )
+    down_back, gate_back = both_back[..., : ff_pad // SPLIT], both_back[..., ff_pad // SPLIT :]
+
+    def finish_mlp(back):
+        return finish(back).reshape(own_rows, ff_pad)[:, :ff_width]
+
+    down_grads, gate_grads = finish_mlp(down_back), finish_mlp(gate_back)
 
     grad_queries, grad_key_value = pl.pallas_call(
         attend_back_kernel,
         grid=(seqs,),
-        in_specs=[per_seq(query_cols), own_spec, others_spec, per_seq(512), log_spec]
+        in_specs=[per_seq(query_cols), own_spec, others_spec, per_seq(OUT_COLS), log_spec]
         + mask_specs
         + [pl.BlockSpec((HALF, queries_len), lambda at: (0, 0))] * 2,
         out_specs=[
@@ -1088,12 +1249,19 @@
         compiler_params=params(),
         name="attend_back",
     )(
-        queries, key_value, others, grad_mixed.reshape(slots + (512,)), log_total, *masks,
+        queries, key_value, others, grad_mixed.reshape(slots + (OUT_COLS,)), log_total, *masks,
         cosine.T, sine_table.T,
     )
-    final, others = dot_scatter(
-        [after(active, gate_up_back)], [down_full], 3, (grad_key_value,)
-    )
+    final, others, out_product = dot_scatter(
+        [after(active, both_back)],
+        [down_full],
+        3,
+        (grad_key_value,),
+        host=([grad_branch], (0,), [mixed_rows]),
+    )
+    out_summed = sum_along(after(out_product, up_summed))
+    up_back = from_group(after(up_summed, final))
+    up_grads = finish_mlp(up_back)
     result = shuffle((middle + final).astype(jnp.bfloat16), back)
     flat = (CHIPS, 2, seq_b, local_len)
     grad_qkv = pl.pallas_call(
@@ -1117,16 +1285,25 @@
         cosine.reshape(place_shape + (HALF,)),
         sine_table.reshape(place_shape + (HALF,)),
     ).reshape(tokens, 512)
-    heads_product = products(([normed_low, grad_branch], (0, 1)), [grad_qkv, mixed_rows])
-    grad_norm_one = dot_scatter([after(grad_qkv, heads_product, down_back)], [qkv_full], 6)
+    (qkv_product,) = products(normed_low, [grad_qkv])
+    qkv_summed = sum_along(qkv_product)
+    grad_norm_one = dot_scatter(
+        [after(grad_qkv, qkv_product, out_summed)], [heads_full], 6, windows=qkv_window
+    )
+    grad_norm_one = after(grad_norm_one, up_back)
     scaled_one = grad_norm_one * gain_one
     grad_input = grad_middle + inv_one * (
         scaled_one - normed_one * jnp.mean(scaled_one * normed_one, -1, keepdims=True)
     )
-    head_grads = finish(from_group(sum_along(heads_product)))
-    grad_query = head_grads[..., :query_cols].reshape(own_rows, -1)
-    grad_key = head_grads[..., query_cols : query_cols + HEAD_DIM].reshape(own_rows, -1)
-    grad_value = head_grads[..., query_cols + HEAD_DIM : qkv_cols].reshape(own_rows, -1)
+    head_grads = finish(from_group(jnp.concatenate([out_summed, qkv_summed], 1)))
+    key_at = OUT_COLS + query_cols
+
+    def columns(start, count):
+        return head_grads[..., start : start + count].reshape(own_rows, -1)
+
+    grad_query = columns(OUT_COLS, query_cols)
+    grad_key = columns(key_at, HEAD_DIM)
+    grad_value = columns(key_at + HEAD_DIM, HEAD_DIM)
 
     def gain_grad(gain, pairs):
         total = sum(jnp.sum(weight.astype(jnp.float32) * grad, 1) for weight, grad in pairs)
@@ -1144,7 +1321,7 @@
         grad_query,
         grad_key,
         grad_value,
-        head_grads[..., 512 : 512 + query_cols].reshape(own_rows, -1),
+        columns(0, query_cols),
         mlp_gain_grad,
         gate_grads,
         up_grads,

time: 1040 us -> 896 us (0.86)
  Pallas kernels: 770 us -> 669 us
  waiting for transfers between devices: 100 us -> 79.9 us
  local copies, waits for them, and re-layouts: 38.4 us -> 23.8 us
  blocking collectives: 35.2 us -> 21.2 us
    pallas_call x4, Pallas kernels: 306 us -> 263 us  [dot_scatter(): pl.pallas_call(functools.partial(dot_scatter_kernel, len(lefts), parts_n,...]
    pallas_call x5, Pallas kernels: 192 us -> 160 us  [the longest x2 102 us: gather_dot(): pl.pallas_call(functools.partial(gather_dot_kernel, len(weights), gated,...]
    pallas_call x2, Pallas kernels: 162 us -> 131 us  [spread_and_gather(): pl.pallas_call(functools.partial(spread_kernel, count, len(extra)), in_sp...]
    all_to_all x1, blocking collectives: 35.2 us -> 21.2 us  [to_group(): lax.all_to_all(split, GROUP, 0, 0, tiled=True).reshape(SPLIT * rows, cols)]
    all_to_all x3, waiting for transfers between devices: 24 us -> 12.3 us  [from_group(): lax.all_to_all(grads.reshape(SPLIT, rows, cols), GROUP, 0, 0, tiled=True)]
    all_gather x5 -> x4, waiting for transfers between devices: 51.9 us -> 40.8 us  [along(): return lax.all_gather(value, 'hi', axis=0, tiled=True)]
  transfers between devices with their start and end apart: 17 -> 18, of which waited for: 9 -> 8; matrix products, arithmetic and copies ran while one was open for 5% -> 7% of each run, Pallas kernels for 72% -> 75%
where the time goes in v3:
time: 896 us; the launch traced here: 888 us
  Pallas kernels  669 us (75%)
  waiting for transfers between devices  79.9 us (9%)
  other arithmetic  36.4 us (4%)
  local copies, waits for them, and re-layouts  23.8 us (3%)
  matrix products  22.3 us (2%)
  blocking collectives  21.2 us (2%)
  starting transfers between devices  20 us (2%)
  between operations  15.1 us (2%)
    pallas_call x4, Pallas kernels, dot_scatter(): pl.pallas_call(functools.partial(dot_scatter_kernel, len(lefts), parts_n,...  263 us
    pallas_call x2, Pallas kernels, spread_and_gather(): pl.pallas_call(functools.partial(spread_kernel, count, len(extra)), in_sp...  131 us
    pallas_call x2, Pallas kernels, gather_dot(): pl.pallas_call(functools.partial(gather_dot_kernel, len(weights), gated,...  102 us
    pallas_call x3, Pallas kernels, products(): pl.pallas_call(products_kernel, grid=(width // block,), in_specs=[pl.Bloc...  57.9 us
    all_gather x4, waiting for transfers between devices, along(): return lax.all_gather(value, 'hi', axis=0, tiled=True)  40.8 us
    pallas_call x1, Pallas kernels, shards(): pl.pallas_call(attend_back_kernel, grid=(seqs,), in_specs=[per_seq(query_...  40.3 us
    pallas_call x1, Pallas kernels, shards(): pl.pallas_call(attend_kernel, grid=(seqs,), in_specs=[per_seq(query_cols)...  36.9 us
    dot_general x1, matrix products, dot(): lax.dot_general(left, right, (((1,), (0,)), ((), ())), preferred_element_...  22.3 us
  transfers between devices with their start and end apart: 18, of which 8 were waited for; matrix products, arithmetic and copies ran while one was open for 7% of the time, Pallas kernels for 75%

profile of v3, /device:TPU:0, one launch (start us, length us, event | category | flops | bytes accessed | tf_op | source)
XLA Modules:
  0.0 887.9 jit_solution(2899345447683466234)
XLA Ops:
  7.2 1.4 reshape.305
  8.7 1.4 reshape.306
  10.8 2.6 concatenate.54
  13.4 21.2 %all_to_all.20 = bf16[8,80,896]{2,1,0:T(8,128)(2,1)} all-to-all(bf16[8,80,896]{2,1,0:T(8,128)(2,1)S(1)} %bitcast.119), channel_id=1, replica_groups=mesh['y'=2,'core'=2,'hi'=4,'lo'=2] {'y','core','lo'}, dimensions={0} | all-to-all | bytes 2293760 | tf_op jit(solution)/shard_map/all_to_all | solution.py:53
  35.5 0.9 collective-permute-start
  36.4 2.8 collective-permute-done
  39.3 1.1 collective-permute-done.1
  41.0 3.0 collective-permute-done.2
  44.1 1.6 collective-permute-start.3
  45.7 2.6 collective-permute-start.4
  49.2 2.9 shuffle.4.refs_0_
  52.1 3.0 shuffle.5.refs_0_
  55.1 1.1 pad.15.refs_1_
  56.2 1.1 pad.16.refs_2_
  57.7 71.2 %spread_0.1 = (bf16[4,2,256,2560]{3,2,1,0:T(8,128)(2,1)}, bf16[8,80,896]{2,1,0:T(8,128)(2,1)}, bf16[8,80,896]{2,1,0:T(8,128)(2,1)}) custom-call(bf16[256,2560]{1,0:T(8,128)(2,1)} %shuffle.4.refs_0_, bf16[80,7168]{1,0:T(8,128)(2,1)} %pad.15.refs_1_, bf16[80,7168]{1,0:T(8,128)(2,1)} %pad.16.refs_2_), custom_call_target="tpu_custom_call" | custom-call | flops 1000000000 | bytes 20971520 | tf_op jit(solution)/shard_map/spread_0/pallas_call | solution.py:831
  129.7 1.1 pad.17.refs_1_
  130.8 1.2 multiply_sine_fusion
  133.0 17.8 %project.1 = (bf16[2048,2560]{1,0:T(8,128)(2,1)}, bf16[2048,320]{1,0:T(8,128)(2,1)}, bf16[512,640]{1,0:T(8,128)(2,1)}) custom-call(bf16[2048,2560]{1,0:T(8,128)(2,1)} %bitcast.108, f32[1,2560]{1,0:T(1,128)} %reshape_reshape.11.gain_ref, bf16[2560,896]{1,0:T(8,128)(2,1)} %all-gather.5.cloned.1.call-done.weight_ref.refs_1_, ...), custom_call_target="tpu_custom_call" | custom-call | tf_op jit(solution)/shard_map/project/pallas_call | solution.py:1113
  150.8 59.7 %spread_7.1 = (bf16[4,2,256,2560]{3,2,1,0:T(8,128)(2,1)}, bf16[8,80,896]{2,1,0:T(8,128)(2,1)}, bf16[3,512,640]{2,1,0:T(8,128)(2,1)}) custom-call(bf16[256,2560]{1,0:T(8,128)(2,1)} %shuffle.5.refs_0_, bf16[80,7168]{1,0:T(8,128)(2,1)} %pad.17.refs_1_, bf16[512,640]{1,0:T(8,128)(2,1)} %get-tuple-element.51.refs_2_.own_ref), custom_call_target="tpu_custom_call" | custom-call | flops 1000000000 | bytes 20971520 | tf_op jit(solution)/shard_map/spread_7/pallas_call | solution.py:831
  211.0 0.8 copy.59.query_place_ref
  211.8 1.4 copy.58.query_seg_ref
  213.3 36.9 %attend.1 = (bf16[2,2,2,2,128,384]{5,4,3,2,1,0:T(8,128)(2,1)}, f32[8,4,256]{2,1,0:T(4,128)}) custom-call(bf16[2,2,2,2,128,320]{5,4,3,2,1,0:T(8,128)(2,1)} %bitcast.113, bf16[512,640]{1,0:T(8,128)(2,1)} %get-tuple-element.51.refs_2_.own_ref, bf16[3,512,640]{2,1,0:T(8,128)(2,1)} %get-tuple-element.52.others_ref, f32[8,1,1024]{2,1,0:T(1,128)} %bitcast.136, ...), custom_call_target="tpu_custom_call" | custom-call | tf_op jit(solution)/shard_map/attend/pallas_call | solution.py:1169
  250.2 54.6 %dot_scatter_1.1 = f32[256,2560]{1,0:T(8,128)} custom-call(bf16[4,2,256,384]{3,2,1,0:T(8,128)(2,1)} %bitcast.115, bf16[2560,896]{1,0:T(8,128)(2,1)} %all-gather.5.cloned.1.call-done.weight_ref.refs_1_), custom_call_target="tpu_custom_call" | custom-call | flops 1006632960 | bytes 20971520 | tf_op jit(solution)/shard_map/dot_scatter_1/pallas_call | solution.py:602
  304.8 2.7 multiply_reduce_fusion.1
  308.1 1.6 multiply_convert_fusion.refs_0_
  309.6 19.7 %all-gather.9.cloned.1.call-done.refs_2_.refs_3_ = bf16[2560,896]{1,0:T(8,128)(2,1)} async-done(((bf16[640,896]{1,0:T(8,128)(2,1)}), bf16[2560,896]{1,0:T(8,128)(2,1)}) %all-gather.9.cloned.1.call-update) | async-done | bytes 4587536 | tf_op jit(solution)/shard_map/all_gather | solution.py:62
  329.3 53.1 %gather_dot_2.1 = (bf16[4,2,256,2560]{3,2,1,0:T(8,128)(2,1)}, f32[4,2,256,896]{3,2,1,0:T(8,128)}, f32[4,2,256,896]{3,2,1,0:T(8,128)}, bf16[4,2,256,896]{3,2,1,0:T(8,128)(2,1)}) custom-call(bf16[256,2560]{1,0:T(8,128)(2,1)} %multiply_convert_fusion.refs_0_, bf16[2560,896]{1,0:T(8,128)(2,1)} %all-gather.7.cloned.1.call-done.refs_1_.refs_2_, ...), custom_call_target="tpu_custom_call" | custom-call | flops 4697620480 | bytes 20971520 | tf_op jit(solution)/shard_map/gather_dot_2/pallas_call | solution.py:321
  382.4 16.7 %products.3 = bf16[2560,896]{1,0:T(8,128)(2,1)} custom-call(bf16[2048,2560]{1,0:T(8,128)(2,1)} %bitcast.141, bf16[2048,896]{1,0:T(8,128)(2,1)} %bitcast.125), custom_call_target="tpu_custom_call" | custom-call | flops 18790481920 | bytes 10485760 | tf_op jit(solution)/shard_map/products/pallas_call | solution.py:676
  399.1 21.2 %all-gather.11.cloned.1.call-done.refs_1_ = bf16[2560,896]{1,0:T(8,128)(2,1)} async-done(((bf16[640,896]{1,0:T(8,128)(2,1)}), bf16[2560,896]{1,0:T(8,128)(2,1)}) %all-gather.11.cloned.1.call-update) | async-done | bytes 4587536 | tf_op jit(solution)/shard_map/all_gather | solution.py:62
  420.3 22.3 %fusion.7 = (bf16[2048,896]{1,0:T(8,128)(2,1)}, bf16[2048,896]{1,0:T(8,128)(2,1)}) fusion(f32[4,2,256,896]{3,2,1,0:T(8,128)} %get-tuple-element.61, f32[4,2,256,896]{3,2,1,0:T(8,128)} %get-tuple-element.60, bf16[2048,2560]{1,0:T(8,128)(2,1)} %bitcast.142, bf16[2560,896]{1,0:T(8,128)(2,1)} %all-gather.11.cloned.1.call-done.refs_1_), kind=kOutput, calls=%fused_computation.10 | convolution fusion | flops 9419096064 | bytes 37093376 | tf_op jit(solution)/shard_map/dot_general | solution.py:29
  442.6 28.5 %products.4 = (bf16[2560,896]{1,0:T(8,128)(2,1)}, bf16[2560,896]{1,0:T(8,128)(2,1)}) custom-call(bf16[2048,2560]{1,0:T(8,128)(2,1)} %bitcast.143, bf16[2048,896]{1,0:T(8,128)(2,1)} %get-tuple-element.64.refs_0_, bf16[2048,896]{1,0:T(8,128)(2,1)} %get-tuple-element.89.refs_1_), custom_call_target="tpu_custom_call" | custom-call | flops 37580963840 | bytes 10485760 | tf_op jit(solution)/shard_map/products/pallas_call | solution.py:676
  471.9 60.0 %dot_scatter_4.1 = f32[256,2560]{1,0:T(8,128)} custom-call(bf16[4,2,256,896]{3,2,1,0:T(8,128)(2,1)} %bitcast.124, bf16[4,2,256,896]{3,2,1,0:T(8,128)(2,1)} %bitcast.123, bf16[2560,896]{1,0:T(8,128)(2,1)} %all-gather.7.cloned.1.call-done.refs_1_.refs_2_, bf16[2560,896]{1,0:T(8,128)(2,1)} %all-gather.9.cloned.1.call-done.refs_2_.refs_3_), custom_call_target="tpu_custom_call" | custom-call | flops 4697620480 | bytes 20971520 | tf_op jit(solution)/shard_map/dot_scatter_4/pallas_call | solution.py:602
  532.0 3.1 fusion.15
  535.6 2.3 fusion.43.refs_0_
  537.9 49.1 %gather_dot_5.1 = (bf16[4,2,256,2560]{3,2,1,0:T(8,128)(2,1)}, bf16[4,2,256,384]{3,2,1,0:T(8,128)(2,1)}) custom-call(bf16[256,2560]{1,0:T(8,128)(2,1)} %fusion.43.refs_0_, bf16[2560,896]{1,0:T(8,128)(2,1)} %all-gather.5.cloned.1.call-done.weight_ref.refs_1_), custom_call_target="tpu_custom_call" | custom-call | flops 1006632960 | bytes 20971520 | tf_op jit(solution)/shard_map/gather_dot_5/pallas_call | solution.py:321
  587.0 18.4 %reduce-scatter.8.cloned.1.call-done = bf16[640,896]{1,0:T(8,128)(2,1)} async-done(((bf16[2560,896]{1,0:T(8,128)(2,1)}), bf16[640,896]{1,0:T(8,128)(2,1)}) %reduce-scatter.8.cloned.1.call-update) | async-done | bytes 1146896 | tf_op jit(solution)/shard_map/reduce_scatter | solution.py:66
  605.4 3.1 pad_maximum_fusion
  608.5 4.4 all-to-all-start.1
  613.0 0.9 multiply_sine_fusion.1
  613.9 40.3 %attend_back.1 = (bf16[2,2,2,2,128,320]{5,4,3,2,1,0:T(8,128)(2,1)}, bf16[4,512,640]{2,1,0:T(8,128)(2,1)}) custom-call(bf16[2,2,2,2,128,320]{5,4,3,2,1,0:T(8,128)(2,1)} %bitcast.114, bf16[512,640]{1,0:T(8,128)(2,1)} %get-tuple-element.51.refs_2_.own_ref, bf16[3,512,640]{2,1,0:T(8,128)(2,1)} %get-tuple-element.52.others_ref, ...), custom_call_target="tpu_custom_call" | custom-call | tf_op jit(solution)/shard_map/attend_back/pallas_call | solution.py:1234
  654.2 95.0 %dot_scatter_3.1 = (f32[256,2560]{1,0:T(8,128)}, bf16[3,512,640]{2,1,0:T(8,128)(2,1)}, bf16[2560,384]{1,0:T(8,128)(2,1)}) custom-call(bf16[4,2,256,896]{3,2,1,0:T(8,128)(2,1)} %get-tuple-element.56, bf16[2560,896]{1,0:T(8,128)(2,1)} %all-gather.11.cloned.1.call-done.refs_1_, bf16[4,512,640]{2,1,0:T(8,128)(2,1)} %get-tuple-element.70.refs_2_.own_ref, ...), custom_call_target="tpu_custom_call" | custom-call | flops 2348810240 | bytes 20971520 | tf_op jit(solution)/shard_map/dot_scatter_3/pallas_call | solution.py:602
  749.3 7.4 unrotate.1
  756.7 12.7 %products.5 = bf16[2560,512]{1,0:T(8,128)(2,1)} custom-call(bf16[2048,2560]{1,0:T(8,128)(2,1)} %get-tuple-element.76.left_ref, bf16[2048,512]{1,0:T(8,128)(2,1)} %bitcast.111), custom_call_target="tpu_custom_call" | custom-call | flops 10737418240 | bytes 10485760 | tf_op jit(solution)/shard_map/products/pallas_call | solution.py:676
  769.6 4.5 all-to-all-start.2
  774.1 1.8 slice_bitcast_fusion
  776.2 0.9 copy-done.6
  777.1 1.8 multiply_reduce_fusion.3
  778.9 1.5 slice_convert_fusion
  780.4 9.6 %all-to-all-done.2 = bf16[8,80,896]{2,1,0:T(8,128)(2,1)} async-done(((bf16[8,80,896]{2,1,0:T(8,128)(2,1)}), bf16[8,80,896]{2,1,0:T(8,128)(2,1)}, u32[]{:S(2)}, u32[]{:S(2)}) %all-to-all-start.2) | async-done | bytes 1146912 | tf_op jit(solution)/shard_map/all_to_all | solution.py:58
  790.0 1.5 copy.75
  791.6 1.7 multiply_reduce_fusion.2
  793.9 53.5 %dot_scatter_6.1 = f32[256,2560]{1,0:T(8,128)} custom-call(bf16[4,2,256,512]{3,2,1,0:T(8,128)(2,1)} %bitcast.112, bf16[2560,896]{1,0:T(8,128)(2,1)} %all-gather.5.cloned.1.call-done.weight_ref.refs_1_), custom_call_target="tpu_custom_call" | custom-call | flops 1342177280 | bytes 20971520 | tf_op jit(solution)/shard_map/dot_scatter_6/pallas_call | solution.py:602
  847.4 2.8 fusion.11
  850.3 2.2 pad_maximum_fusion.1
  852.5 4.3 all-to-all-start.3
  856.8 6.4 fusion.14
  863.2 4.1 shuffle.7
  867.3 2.8 shuffle.6
  870.1 2.6 all-to-all-done.3
  872.8 1.4 convert_bitcast_fusion
  874.3 0.9 fusion.45
  876.0 1.2 copy.64
  877.4 1.1 multiply_reduce_fusion.5
  879.3 1.1 reshape.343
  (140 shorter events, 11.4 us)
Async XLA Ops:
  7.2 3.0 copy-start.17
  7.2 3.3 copy-start.16
  7.2 125.8 %all-gather.5.cloned.1.call-start = ((), (), s32[]{:S(2)}) async-start(), calls=%async_computation.9 | async-start | bytes 5734400 | tf_op jit(solution)/shard_map/all_gather | solution.py:62
  10.7 24.6 %copy-start.19 = (bf16[80]{0:T(256)(128)(2,1)S(1)}, bf16[80]{0:T(256)(128)(2,1)}, u32[]{:S(2)}) copy-start(bf16[80]{0:T(256)(128)(2,1)} %param.13) | copy-start | bytes 484
  10.8 24.6 %copy-start.21 = (bf16[80]{0:T(256)(128)(2,1)S(1)}, bf16[80]{0:T(256)(128)(2,1)}, u32[]{:S(2)}) copy-start(bf16[80]{0:T(256)(128)(2,1)} %param.18) | copy-start | bytes 484
  34.6 275.0 %all-gather.7.cloned.1.call-start = ((), (), s32[]{:S(2)}) async-start(), calls=%async_computation.10 | async-start | bytes 5734400 | tf_op jit(solution)/shard_map/all_gather | solution.py:62
  35.5 3.6 collective-permute-start
  39.1 1.2 collective-permute-start.1
  40.4 3.7 collective-permute-start.2
  44.1 13.2 %collective-permute-start.3 = (bf16[2,2,1,2,512]{4,3,1,0,2:T(2,128)(2,1)S(1)}, bf16[2,2,1,2,512]{4,3,1,0,2:T(2,128)(2,1)S(1)}, u32[]{:S(2)}, u32[]{:S(2)}) collective-permute-start(bf16[2,2,1,2,512]{4,3,1,0,2:T(2,128)(2,1)S(1)} %pad_maximum_fusion.6), channel_id=1, source_target_pairs={{0,2},{2,0},{4,6},{6,4},{1,3},{3,1},{5,7},{7,5},{8,10},{10,8},{12,... | collective-permute-start | bytes 24584 | tf_op jit(solution)/shard_map/ppermute | solution.py:47
  45.7 11.6 %collective-permute-start.4 = (bf16[2,2,1,2,512]{4,3,1,0,2:T(2,128)(2,1)S(1)}, bf16[2,2,1,2,512]{4,3,1,0,2:T(2,128)(2,1)S(1)}, u32[]{:S(2)}, u32[]{:S(2)}) collective-permute-start(bf16[2,2,1,2,512]{4,3,1,0,2:T(2,128)(2,1)S(1)} %pad_maximum_fusion.6), channel_id=1, source_target_pairs={{0,4},{2,6},{4,0},{6,2},{1,5},{3,7},{5,1},{7,3},{8,12},{10,14},{12... | collective-permute-start | bytes 24584 | tf_op jit(solution)/shard_map/ppermute | solution.py:47
  48.3 9.0 %collective-permute-start.5 = (bf16[2,2,1,2,512]{4,3,1,0,2:T(2,128)(2,1)S(1)}, bf16[2,2,1,2,512]{4,3,1,0,2:T(2,128)(2,1)S(1)}, u32[]{:S(2)}, u32[]{:S(2)}) collective-permute-start(bf16[2,2,1,2,512]{4,3,1,0,2:T(2,128)(2,1)S(1)} %pad_maximum_fusion.6), channel_id=1, source_target_pairs={{0,6},{2,4},{4,2},{6,0},{1,7},{3,5},{5,3},{7,1},{8,14},{10,12},{12... | collective-permute-start | bytes 24584 | tf_op jit(solution)/shard_map/ppermute | solution.py:47
  49.2 5.9 copy-start.5
  52.1 4.1 copy-start.7
  57.6 72.0 %copy-start.14 = (f32[2,2,2,4,2,128]{5,4,3,2,1,0:T(2,128)}, f32[2,2,2,4,2,128]{5,4,3,2,1,0:T(2,128)S(1)}, u32[]{:S(2)}) copy-start(f32[2,2,2,4,2,128]{5,4,3,2,1,0:T(2,128)S(1)} %copy.56) | copy-start | bytes 98308
  57.7 72.0 %copy-start.11 = (bf16[80,6912]{1,0:T(8,128)(2,1)S(1)}, bf16[80,6912]{1,0:T(8,128)(2,1)}, u32[]{:S(2)}) copy-start(bf16[80,6912]{1,0:T(8,128)(2,1)} %param.21) | copy-start | bytes 3317764
  128.9 200.4 %all-gather.9.cloned.1.call-start = ((), (), s32[]{:S(2)}) async-start(), calls=%async_computation.11 | async-start | bytes 5734400 | tf_op jit(solution)/shard_map/all_gather | solution.py:62
  129.6 290.6 %all-gather.11.cloned.1.call-start = ((), (), s32[]{:S(2)}) async-start(), calls=%async_computation.13 | async-start | bytes 5734400 | tf_op jit(solution)/shard_map/all_gather | solution.py:62
  210.5 376.5 %reduce-scatter.6.cloned.1.call-start = ((), (), s32[]{:S(2)}) async-start(), calls=%async_computation.12 | async-start | bytes 5734400 | tf_op jit(solution)/shard_map/reduce_scatter | solution.py:66
  304.7 3.0 copy-start
  304.7 3.3 copy-start.1
  399.0 206.4 %reduce-scatter.8.cloned.1.call-start = ((), (), s32[]{:S(2)}) async-start(), calls=%async_computation.14 | async-start | bytes 5734400 | tf_op jit(solution)/shard_map/reduce_scatter | solution.py:66
  471.1 278.1 %reduce-scatter.10.cloned.1.call-start = ((), (), s32[]{:S(2)}) async-start(), calls=%async_computation.15 | async-start | bytes 5734400 | tf_op jit(solution)/shard_map/reduce_scatter | solution.py:66
  532.0 3.1 copy-start.2
  532.0 3.3 copy-start.3
  532.0 3.7 copy-start.4
  608.5 45.7 %all-to-all-start.1 = ((bf16[8,80,1792]{2,1,0:T(8,128)(2,1)}), bf16[8,80,1792]{2,1,0:T(8,128)(2,1)}, u32[]{:S(2)}, u32[]{:S(2)}) async-start(bf16[8,80,1792]{2,1,0:T(8,128)(2,1)} %bitcast.110), calls=%async_computation.3 | async-start | bytes 4587520 | tf_op jit(solution)/shard_map/all_to_all | solution.py:58
  612.9 181.0 %reduce-scatter.12.cloned.1.call-start = ((), (), s32[]{:S(2)}) async-start(), calls=%async_computation.16 | async-start | bytes 2457600 | tf_op jit(solution)/shard_map/reduce_scatter | solution.py:66
  749.3 101.0 %reduce-scatter.14.cloned.1.call-start = ((), (), s32[]{:S(2)}) async-start(), calls=%async_computation.17 | async-start | bytes 3276800 | tf_op jit(solution)/shard_map/reduce_scatter | solution.py:66
  769.6 20.5 %all-to-all-start.2 = ((bf16[8,80,896]{2,1,0:T(8,128)(2,1)}), bf16[8,80,896]{2,1,0:T(8,128)(2,1)}, u32[]{:S(2)}, u32[]{:S(2)}) async-start(bf16[8,80,896]{2,1,0:T(8,128)(2,1)} %bitcast.134), calls=%async_computation.6 | async-start | bytes 2293760 | tf_op jit(solution)/shard_map/all_to_all | solution.py:58
  775.9 1.3 copy-start.6
  790.0 1.6 copy-start.8
  791.6 1.8 copy-start.22
  847.4 2.8 copy-start.15
  852.5 20.2 %all-to-all-start.3 = ((bf16[8,80,896]{2,1,0:T(8,128)(2,1)}), bf16[8,80,896]{2,1,0:T(8,128)(2,1)}, u32[]{:S(2)}, u32[]{:S(2)}) async-start(bf16[8,80,896]{2,1,0:T(8,128)(2,1)} %bitcast.118), calls=%async_computation.8 | async-start | bytes 2293760 | tf_op jit(solution)/shard_map/all_to_all | solution.py:58
  874.3 1.5 copy-start.10
  875.8 3.5 copy-start.9
  875.8 3.0 copy-start.18
  877.4 1.5 copy-start.12
  878.5 1.9 copy-start.20
  878.8 2.1 copy-start.13
Sparse Core Ops, SparseCore 0:
  34.8 87.5 all-gather.4
  129.0 96.8 all-gather.6
  227.5 101.7 all-gather.8
  330.7 89.5 all-gather.10
  422.4 97.0 reduce-scatter.5
  521.7 83.6 reduce-scatter.7
  607.7 112.0 reduce-scatter.9
  749.4 39.5 reduce-scatter.11
  791.9 51.3 reduce-scatter.13
